TPU v7x, 128 devices: a whole 4x4x4 slice. The times are simulated.
128 devices in a mesh: dp: 16 (over x, z_hi, core), ctx: 8 (over z_lo, y).
Axes of the slice: x: 4, y: 4, z: 4 (z_hi: 2, z_lo: 2; z = z_hi * 2 + z_lo), core: 2. Of those that a mesh axis runs over, the one named last changes fastest.
Arguments:
- light_flux: float32 [16, 6, 4096], P('dp', None, 'ctx'), may hold values from -6 to 6
- lengths: int32 [16], P('dp'), may hold values from 1024 to 4096, as said below
- offsets: int32 [16, 4096], P('dp', 'ctx'), may hold values from 0 to 3
- start_weight: float32 [512, 3], replicated, may hold values from -3.5 to 3.5
- conv_weight: bfloat16 [2, 1024, 1536], P(None, 'dp'), may hold values from -0.15625 to 0.15625
- gate_bias: float32 [2, 1024], replicated, may hold values from -4 to 4
- mix_first: bfloat16 [1024, 512], P('dp'), may hold values from -0.25 to 0.25
- mix_last: bfloat16 [512, 512], P('dp'), may hold values from -0.25 to 0.25
- end_weight: float32 [6, 512], replicated, may hold values from -0.25 to 0.25
- cotangent: float32 [16, 3, 4096], P('dp', None, 'ctx'), may hold values from -0.0234375 to 0.0234375
Outputs:
- coupled: float32 [16, 3, 4096], P('dp', None, 'ctx')
- grad_start: float32 [512, 3], replicated
- grad_conv: float32 [2, 1024, 1536], P(None, 'dp')
- grad_bias: float32 [2, 1024], replicated
- grad_mix_first: float32 [1024, 512], P('dp')
- grad_mix_last: float32 [512, 512], P('dp')
- grad_end: float32 [6, 512], replicated
Inputs may be any that keep to these rules, and one draw needn't show every extreme that they name: `lengths`: epochs at or past a curve's length are padding; at least one curve has no padding.
All inputs are finite; a program needn't handle non-finite values.
Results may differ from a plain program's by a relative error of at most 0.0091.
Values may be sent and summed in bfloat16 or wider, within the bound.
No kernel may reach another device: no remote copies, remote signals or barrier semaphores. Data moves between devices by JAX's collectives and lax.ppermute only.
A program may use at most 128 MiB of HBM per device.

v0:
```python
import jax
import jax.numpy as jnp
from jax import lax
from jax.sharding import PartitionSpec as P

BUCKETS = 4


highest = lax.Precision.HIGHEST


def from_behind(array, axis, by):
    size = lax.axis_size(axis)
    pairs = [(i, i + by) for i in range(size) if 0 <= i + by < size]
    return lax.ppermute(array, axis, pairs)


def tap_stack(padded, bucket, dilation, reach_len, col_count):
    centre = lax.slice_in_dim(padded, reach_len, reach_len + col_count, axis=1)
    left_tap = lax.slice_in_dim(
        padded, reach_len - dilation, reach_len - dilation + col_count, axis=1
    )
    right_tap = lax.slice_in_dim(
        padded, reach_len + dilation, reach_len + dilation + col_count, axis=1
    )
    for shift_k in range(1, BUCKETS):
        chosen = (bucket == shift_k)[None, :]
        left_start = reach_len - dilation - shift_k
        right_start = reach_len + dilation + shift_k
        left_tap = jnp.where(
            chosen, lax.slice_in_dim(padded, left_start, left_start + col_count, axis=1), left_tap
        )
        right_tap = jnp.where(
            chosen,
            lax.slice_in_dim(padded, right_start, right_start + col_count, axis=1),
            right_tap,
        )
    return jnp.concatenate([left_tap, centre, right_tap], axis=0)


def place_piece(piece, start_col, total_len):
    return jnp.pad(piece, ((0, 0), (start_col, total_len - start_col - piece.shape[1])))


def tap_transpose(d_stacked, bucket, dilation, reach_len, col_count, channels):
    total_len = col_count + 2 * reach_len
    d_left = d_stacked[:channels]
    d_centre = d_stacked[channels : 2 * channels]
    d_right = d_stacked[2 * channels :]
    window = place_piece(d_centre, reach_len, total_len)
    for shift_k in range(BUCKETS):
        chosen = (bucket == shift_k)[None, :]
        left_part = jnp.where(chosen, d_left, 0.0)
        right_part = jnp.where(chosen, d_right, 0.0)
        window = window + place_piece(left_part, reach_len - dilation - shift_k, total_len)
        window = window + place_piece(right_part, reach_len + dilation + shift_k, total_len)
    return window


def gate_forward(preact):
    channels = preact.shape[0] // 2
    return jnp.tanh(preact[:channels]) * jax.nn.sigmoid(preact[channels:])


def gate_backward(preact, d_gated):
    channels = preact.shape[0] // 2
    tangent = jnp.tanh(preact[:channels])
    sigmoid_part = jax.nn.sigmoid(preact[channels:])
    d_upper = d_gated * sigmoid_part * (1.0 - tangent * tangent)
    d_lower = d_gated * tangent * sigmoid_part * (1.0 - sigmoid_part)
    return jnp.concatenate([d_upper, d_lower], axis=0).astype(jnp.bfloat16)


def contract_rows(left_op, right_op, precision=None):
    return lax.dot_general(
        left_op,
        right_op,
        (((1,), (1,)), ((), ())),
        precision=precision,
        preferred_element_type=jnp.float32,
    )


def contract_cols(left_op, right_op, precision=None):
    return lax.dot_general(
        left_op,
        right_op,
        (((0,), (0,)), ((), ())),
        precision=precision,
        preferred_element_type=jnp.float32,
    )


def extend(hidden, reach_len, shard_len):
    pieces_low = []
    pieces_high = []
    remain = reach_len
    distance = 1
    while remain > 0:
        amount = min(shard_len, remain)
        from_low = from_behind(hidden[:, shard_len - amount :], "ctx", distance)
        from_high = from_behind(hidden[:, :amount], "ctx", -distance)
        pieces_low.insert(0, from_low)
        pieces_high.append(from_high)
        remain = remain - amount
        distance = distance + 1
    return jnp.concatenate(pieces_low + [hidden] + pieces_high, axis=1)


def return_rims(grad_window, reach_len, shard_len):
    middle = grad_window[:, reach_len : reach_len + shard_len]
    remain = reach_len
    distance = 1
    end_col = reach_len
    while remain > 0:
        amount = min(shard_len, remain)
        piece_low = grad_window[:, end_col - amount : end_col]
        high_start = reach_len + shard_len + (reach_len - remain)
        piece_high = grad_window[:, high_start : high_start + amount]
        back_low = from_behind(piece_low, "ctx", -distance)
        back_high = from_behind(piece_high, "ctx", distance)
        middle = middle + place_piece(back_low, shard_len - amount, shard_len)
        middle = middle + place_piece(back_high, 0, shard_len)
        end_col = end_col - amount
        remain = remain - amount
        distance = distance + 1
    return middle


def layer_forward(conv_shard, mix_shard, bias_row, stacked):
    full_conv, full_mix = (
        lax.all_gather(conv_shard, "dp", axis=0, tiled=True),
        lax.all_gather(mix_shard, "dp", axis=0, tiled=True),
    )
    preact = jnp.dot(full_conv, stacked, preferred_element_type=jnp.float32) + bias_row[:, None]
    gated = gate_forward(preact).astype(jnp.bfloat16)
    mixed_rows = jnp.dot(full_mix, gated, preferred_element_type=jnp.float32)
    return (preact, gated, mixed_rows, (full_conv, full_mix))


def mix_back(mix_weight, d_mixed):
    return contract_cols(mix_weight, d_mixed)


def conv_back(conv_weight_rows, dz_rows):
    return contract_cols(conv_weight_rows, dz_rows)


def reduce_grad(left_op, right_op):
    full_grad = contract_rows(left_op, right_op)
    summed = lax.psum(full_grad, "ctx")
    return lax.psum_scatter(summed, "dp", scatter_dimension=0, tiled=True)


def local(
    light_flux,
    lengths,
    offsets,
    start_weight,
    conv_weight,
    gate_bias,
    mix_first,
    mix_last,
    end_weight,
    cotangent,
):
    shard_len = light_flux.shape[2]
    half_bands = light_flux.shape[1] // 2
    channels = start_weight.shape[0]
    position = lax.axis_index("ctx") * shard_len + jnp.arange(shard_len, dtype=jnp.int32)
    valid_mask = (position < lengths[0]).astype(jnp.float32)
    bucket = offsets[0]
    first_half = light_flux[0, :half_bands]
    second_half = light_flux[0, half_bands:]
    dilations = (shard_len // 4, shard_len + shard_len // 2)
    reaches = (dilations[0] + BUCKETS - 1, dilations[1] + BUCKETS - 1)
    hidden_first = (jnp.dot(start_weight, first_half, precision=highest) * valid_mask).astype(
        jnp.bfloat16
    )
    stacked_first = tap_stack(
        extend(hidden_first, reaches[0], shard_len), bucket, dilations[0], reaches[0], shard_len
    )
    pre_first, gated_first, mixed_first, kept_first = layer_forward(
        conv_weight[0], mix_first, gate_bias[0], stacked_first
    )
    hidden_second = (
        (hidden_first.astype(jnp.float32) + mixed_first[:channels]) * valid_mask
    ).astype(jnp.bfloat16)
    stacked_second = tap_stack(
        extend(hidden_second, reaches[1], shard_len), bucket, dilations[1], reaches[1], shard_len
    )
    pre_second, gated_second, mixed_second, kept_second = layer_forward(
        conv_weight[1], mix_last, gate_bias[1], stacked_second
    )
    skip_total = mixed_first[channels:] + mixed_second
    end_out = jnp.dot(end_weight, skip_total, precision=highest)
    growth = jnp.exp(end_out[:half_bands])
    coupled = ((growth * second_half + end_out[half_bands:]) * valid_mask)[None]
    d_coupled = cotangent[0] * valid_mask
    d_end = jnp.concatenate([d_coupled * growth * second_half, d_coupled], axis=0)
    grad_end_local = contract_rows(d_end, skip_total, highest)
    d_skip = contract_cols(end_weight, d_end, highest)
    d_skip_b = d_skip.astype(jnp.bfloat16)
    d_gated_second = mix_back(kept_second[1], d_skip_b)
    grad_mix_last = reduce_grad(d_skip_b, gated_second)
    dz_second = gate_backward(pre_second, d_gated_second)
    grad_conv_second = reduce_grad(dz_second, stacked_second)
    bias_second = jnp.sum(dz_second.astype(jnp.float32), axis=1)
    d_stacked_second = conv_back(kept_second[0], dz_second)
    d_window_second = tap_transpose(
        d_stacked_second, bucket, dilations[1], reaches[1], shard_len, channels
    )
    d_field_second = return_rims(d_window_second, reaches[1], shard_len)
    d_mixed_first = jnp.concatenate([d_field_second * valid_mask, d_skip], axis=0).astype(
        jnp.bfloat16
    )
    d_gated_first = mix_back(kept_first[1], d_mixed_first)
    grad_mix_first = reduce_grad(d_mixed_first, gated_first)
    dz_first = gate_backward(pre_first, d_gated_first)
    grad_conv_first = reduce_grad(dz_first, stacked_first)
    bias_first = jnp.sum(dz_first.astype(jnp.float32), axis=1)
    d_stacked_first = conv_back(kept_first[0], dz_first)
    d_window_first = tap_transpose(
        d_stacked_first, bucket, dilations[0], reaches[0], shard_len, channels
    )
    d_hidden_first = d_field_second * valid_mask + return_rims(
        d_window_first, reaches[0], shard_len
    )
    grad_start_local = contract_rows(d_hidden_first * valid_mask, first_half, highest)
    grad_start, grad_bias, grad_end = lax.psum(
        (grad_start_local, jnp.stack([bias_first, bias_second]), grad_end_local), ("dp", "ctx")
    )
    grad_conv = jnp.stack([grad_conv_first, grad_conv_second])
    return (coupled, grad_start, grad_conv, grad_bias, grad_mix_first, grad_mix_last, grad_end)


def solution(mesh):
    in_specs = (
        P("dp", None, "ctx"),
        P("dp"),
        P("dp", "ctx"),
        P(),
        P(None, "dp", None),
        P(),
        P("dp", None),
        P("dp", None),
        P(),
        P("dp", None, "ctx"),
    )
    out_specs = (
        P("dp", None, "ctx"),
        P(),
        P(None, "dp", None),
        P(),
        P("dp", None),
        P("dp", None),
        P(),
    )
    return jax.shard_map(local, mesh=mesh, in_specs=in_specs, out_specs=out_specs, check_vma=False)
```

profile of v0, /device:TPU:1, one launch (start us, length us, event | category | flops | bytes accessed | tf_op | source)
XLA Modules:
  0.0 635.6 jit_solution(13438480193903545730)
XLA Ops:
  7.3 1.8 fusion.83
  9.1 0.7 all-gather.6.cloned.1.call-update
  9.9 0.7 all-gather.10.cloned.1.call-update
  11.3 0.7 fusion.84
  12.0 1.7 fusion.11
  13.8 4.0 collective-permute-start
  17.8 1.3 collective-permute-start.1
  19.2 0.9 collective-permute-done
  20.1 3.8 collective-permute-done.1
  23.9 4.0 fusion.43
  28.0 39.5 %all-gather.8.cloned.1.call-done = bf16[1,1024,1536]{2,1,0:T(8,128)(2,1)} async-done(((bf16[1,64,1536]{2,1,0:T(8,128)(2,1)}), bf16[1,1024,1536]{2,1,0:T(8,128)(2,1)}) %all-gather.8.cloned.1.call-update) | async-done | bytes 3145744 | tf_op jit(solution)/shard_map/all_gather | solution.py:132
  67.5 3.7 add_bitcast_fusion.1
  71.2 1.4 copy-done.10
  73.0 40.6 %all-gather.6.cloned.1.call-done = bf16[1024,512]{1,0:T(8,128)(2,1)} async-done(((bf16[64,512]{1,0:T(8,128)(2,1)}), bf16[1024,512]{1,0:T(8,128)(2,1)}) %all-gather.6.cloned.1.call-update) | async-done | bytes 1048592 | tf_op jit(solution)/shard_map/all_gather | solution.py:133
  113.6 2.0 convolution_bitcast_fusion.2
  115.8 1.3 collective-permute-start.4
  117.1 4.0 collective-permute-start.3
  121.2 4.6 collective-permute-start.2
  125.8 1.3 collective-permute-start.5
  127.1 36.2 %all_gather.15 = bf16[512,512]{1,0:T(8,128)(2,1)} all-gather(bf16[32,512]{1,0:T(8,128)(2,1)S(1)} %copy-done.31), channel_id=1, replica_groups=mesh['dp'=16,'ctx'=8] {'dp'}, dimensions={0}, use_global_device_ids=true | all-gather | bytes 557056 | tf_op jit(solution)/shard_map/all_gather | solution.py:133
  163.4 2.8 fusion.49
  166.2 13.4 %all-gather.10.cloned.1.call-done = bf16[1,1024,1536]{2,1,0:T(8,128)(2,1)} async-done(((bf16[1,64,1536]{2,1,0:T(8,128)(2,1)}), bf16[1,1024,1536]{2,1,0:T(8,128)(2,1)}) %all-gather.10.cloned.1.call-update) | async-done | bytes 3145744 | tf_op jit(solution)/shard_map/all_gather | solution.py:132
  179.6 3.9 add_bitcast_fusion
  185.0 1.0 convolution_bitcast_fusion.6
  186.1 1.1 convolution_convert_fusion
  187.1 0.8 multiply_convert_fusion.3
  188.0 1.3 copy-done.35
  189.3 1.8 convolution_bitcast_fusion.1
  191.1 0.9 slice_select_fusion.15
  192.0 1.4 pad_add_fusion
  193.4 2.0 copy-done.2
  195.4 1.5 fusion.78
  197.0 1.3 collective-permute-start.6
  198.2 5.0 collective-permute-start.7
  203.2 1.5 fusion.86
  204.8 1.3 fusion.79
  206.1 1.3 collective-permute-start.8
  207.4 5.7 collective-permute-start.9
  213.1 26.5 %collective-permute-done.8 = f32[512,259]{0,1:T(8,128)S(1)} collective-permute-done((f32[512,259]{0,1:T(8,128)S(1)}, f32[512,259]{0,1:T(8,128)S(1)}, u32[]{:S(2)}, u32[]{:S(2)}) %collective-permute-start.8) | collective-permute-done | bytes 530464 | tf_op jit(solution)/shard_map/ppermute | solution.py:15
  239.5 2.9 fusion.76
  242.4 0.8 copy-done.30
  243.2 2.1 fusion.31
  245.4 5.7 fusion.32
  251.4 0.9 copy-done.12
  252.4 2.8 multiply_convert_fusion.1
  255.2 0.8 copy-done.20
  256.2 4.5 fusion.33
  260.8 1.0 copy-done.21
  261.9 3.7 convolution_bitcast_fusion
  265.6 0.9 slice_select_fusion.7
  266.5 1.2 pad_add_fusion.1
  267.7 10.9 %reduce-scatter.11.cloned.1.call-done = f32[32,512]{1,0:T(8,128)} async-done(((f32[512,512]{1,0:T(8,128)}), f32[32,512]{1,0:T(8,128)}) %reduce-scatter.11.cloned.1.call-update) | async-done | bytes 65552 | tf_op jit(solution)/shard_map/reduce_scatter | solution.py:152
  278.6 74.3 %reduce-scatter.9.cloned.1.call-done = f32[64,512]{1,0:T(8,128)} async-done(((f32[1024,512]{1,0:T(8,128)}), f32[64,512]{1,0:T(8,128)}) %reduce-scatter.9.cloned.1.call-update) | async-done | bytes 131088 | tf_op jit(solution)/shard_map/reduce_scatter | solution.py:152
  352.9 93.9 %reduce-scatter.7.cloned.1.call-done = f32[64,1536]{1,0:T(8,128)} async-done(((f32[1024,1536]{1,0:T(8,128)}), f32[64,1536]{1,0:T(8,128)}) %reduce-scatter.7.cloned.1.call-update) | async-done | bytes 393232 | tf_op jit(solution)/shard_map/reduce_scatter | solution.py:152
  446.8 93.0 %reduce-scatter.5.cloned.1.call-done = f32[64,1536]{1,0:T(8,128)} async-done(((f32[1024,1536]{1,0:T(8,128)}), f32[64,1536]{1,0:T(8,128)}) %reduce-scatter.5.cloned.1.call-update) | async-done | bytes 393232 | tf_op jit(solution)/shard_map/reduce_scatter | solution.py:152
  539.9 1.4 collective-permute-start.10
  541.3 4.0 collective-permute-start.11
  547.0 1.2 collective-permute-done.10
  548.2 0.9 collective-permute-done.11
  549.1 0.8 fusion.15
  549.9 73.7 %all-reduce.22 = (f32[512,3]{0,1:T(4,128)}, f32[2,1024]{1,0:T(2,128)}, f32[6,512]{1,0:T(8,128)}) all-reduce(f32[512,3]{0,1:T(4,128)S(1)} %fusion.15, f32[2,1024]{1,0:T(2,128)S(1)} %pad_maximum_fusion.22, f32[6,512]{1,0:T(8,128)S(1)} %fusion.55), channel_id=1, replica_groups=mesh['dp'=16,'ctx'=8] {'dp','ctx'}, use_global_device_ids=true, to_apply=%region_0.1 | all-reduce | flops 6656 | bytes 53248 | tf_op jit(solution)/shard_map/psum | solution.py:230
  623.7 2.1 pad_maximum_fusion.5
  625.7 1.6 copy.52
  627.3 1.5 copy.53
  (105 shorter events, 5.1 us)
Async XLA Ops:
  7.2 177.9 %copy-start = (f32[6,512]{1,0:T(8,128)S(1)}, f32[6,512]{1,0:T(8,128)}, u32[]{:S(2)}) copy-start(f32[6,512]{1,0:T(8,128)} %param.18) | copy-start | bytes 36868
  7.2 11.9 %copy-start.32 = (f32[2,1024]{1,0:T(2,128)S(1)}, f32[2,1024]{1,0:T(2,128)}, u32[]{:S(2)}) copy-start(f32[2,1024]{1,0:T(2,128)} %param.15) | copy-start | bytes 24580
  7.2 11.9 %copy-start.34 = (s32[1,512]{1,0:T(1,128)S(1)}, s32[1,512]{1,0:T(1,128)}, u32[]{:S(2)}) copy-start(s32[1,512]{1,0:T(1,128)} %param.12) | copy-start | bytes 6148
  7.2 60.3 %all-gather.8.cloned.1.call-start = ((), (), s32[]{:S(2)}) async-start(), calls=%async_computation.5 | async-start | bytes 3342336 | tf_op jit(solution)/shard_map/all_gather | solution.py:132
  9.1 104.5 %all-gather.6.cloned.1.call-start = ((), (), s32[]{:S(2)}) async-start(), calls=%async_computation.4 | async-start | bytes 1114112 | tf_op jit(solution)/shard_map/all_gather | solution.py:133
  9.8 169.8 %all-gather.10.cloned.1.call-start = ((), (), s32[]{:S(2)}) async-start(), calls=%async_computation.6 | async-start | bytes 3342336 | tf_op jit(solution)/shard_map/all_gather | solution.py:132
  10.6 268.1 %reduce-scatter.11.cloned.1.call-start = ((), (), s32[]{:S(2)}) async-start(), calls=%async_computation.10 | async-start | bytes 1114112 | tf_op jit(solution)/shard_map/reduce_scatter | solution.py:152
  13.7 101.8 %copy-start.3 = (bf16[512,512]{0,1:T(8,128)(2,1)}, bf16[512,512]{0,1:T(8,128)(2,1)S(1)}, u32[]{:S(2)}) copy-start(bf16[512,512]{0,1:T(8,128)(2,1)S(1)} %fusion.11) | copy-start | bytes 1572868
  13.8 6.4 collective-permute-start
  17.8 6.1 collective-permute-start.1
  27.9 39.5 %copy-start.26 = (bf16[512,512]{0,1:T(8,128)(2,1)}, bf16[512,512]{0,1:T(8,128)(2,1)S(1)}, u32[]{:S(2)}) copy-start(bf16[512,512]{0,1:T(8,128)(2,1)S(1)} %get-tuple-element.69) | copy-start | bytes 1572868
  28.0 43.2 %copy-start.28 = (bf16[512,512]{0,1:T(8,128)(2,1)}, bf16[512,512]{0,1:T(8,128)(2,1)S(1)}, u32[]{:S(2)}) copy-start(bf16[512,512]{0,1:T(8,128)(2,1)S(1)} %get-tuple-element.70) | copy-start | bytes 1572868
  71.2 1.4 copy-start.10
  73.0 40.6 %copy-start.8 = (bf16[512,512]{0,1:T(8,128)(2,1)}, bf16[512,512]{0,1:T(8,128)(2,1)S(1)}, u32[]{:S(2)}) copy-start(bf16[512,512]{0,1:T(8,128)(2,1)S(1)} %multiply_convert_fusion.5) | copy-start | bytes 1572868
  115.6 11.5 %copy-start.31 = (bf16[32,512]{1,0:T(8,128)(2,1)S(1)}, bf16[32,512]{1,0:T(8,128)(2,1)}, u32[]{:S(2)}) copy-start(bf16[32,512]{1,0:T(8,128)(2,1)} %param.17) | copy-start | bytes 98308
  115.8 63.9 %copy-start.6 = (bf16[512,512]{0,1:T(8,128)(2,1)}, bf16[512,512]{0,1:T(8,128)(2,1)S(1)}, u32[]{:S(2)}) copy-start(bf16[512,512]{0,1:T(8,128)(2,1)S(1)} %fusion.25) | copy-start | bytes 1572868
  115.8 47.5 %collective-permute-start.4 = (bf16[512,512]{0,1:T(8,128)(2,1)S(1)}, bf16[512,512]{0,1:T(8,128)(2,1)S(1)}, u32[]{:S(2)}, u32[]{:S(2)}) collective-permute-start(bf16[512,512]{0,1:T(8,128)(2,1)S(1)} %fusion.25), channel_id=1, source_target_pairs={{1,0},{2,1},{3,2},{4,3},{5,4},{6,5},{7,6},{9,8},{10,9},{11,10},{12... | collective-permute-start | bytes 1572872 | tf_op jit(solution)/shard_map/ppermute | solution.py:15
  117.1 46.3 %collective-permute-start.3 = (bf16[512,512]{0,1:T(8,128)(2,1)S(1)}, bf16[512,512]{0,1:T(8,128)(2,1)S(1)}, u32[]{:S(2)}, u32[]{:S(2)}) collective-permute-start(bf16[512,512]{0,1:T(8,128)(2,1)S(1)} %fusion.25), channel_id=1, source_target_pairs={{0,1},{1,2},{2,3},{3,4},{4,5},{5,6},{6,7},{8,9},{9,10},{10,11},{11... | collective-permute-start | bytes 1572872 | tf_op jit(solution)/shard_map/ppermute | solution.py:15
  121.2 42.2 %collective-permute-start.2 = (bf16[512,259]{0,1:T(8,128)(2,1)S(1)}, bf16[512,259]{0,1:T(8,128)(2,1)S(1)}, u32[]{:S(2)}, u32[]{:S(2)}) collective-permute-start(bf16[512,259]{0,1:T(8,128)(2,1)S(1)} %get-tuple-element.71), channel_id=1, source_target_pairs={{0,2},{1,3},{2,4},{3,5},{4,6},{5,7},{8,10},{9,11},{10,12},{11,13},... | collective-permute-start | bytes 795656 | tf_op jit(solution)/shard_map/ppermute | solution.py:15
  125.8 37.6 %collective-permute-start.5 = (bf16[512,259]{0,1:T(8,128)(2,1)S(1)}, bf16[512,259]{0,1:T(8,128)(2,1)S(1)}, u32[]{:S(2)}, u32[]{:S(2)}) collective-permute-start(bf16[512,259]{0,1:T(8,128)(2,1)S(1)} %get-tuple-element.72), channel_id=1, source_target_pairs={{2,0},{3,1},{4,2},{5,3},{6,4},{7,5},{10,8},{11,9},{12,10},{13,11},... | collective-permute-start | bytes 795656 | tf_op jit(solution)/shard_map/ppermute | solution.py:15
  166.2 17.3 %copy-start.13 = (bf16[512,512]{0,1:T(8,128)(2,1)}, bf16[512,512]{0,1:T(8,128)(2,1)S(1)}, u32[]{:S(2)}) copy-start(bf16[512,512]{0,1:T(8,128)(2,1)S(1)} %get-tuple-element.84) | copy-start | bytes 1572868
  183.5 1.0 copy-start.11
  184.6 1.5 copy-start.33
  187.1 2.2 copy-start.35
  187.9 3.2 copy-start.16
  187.9 3.2 copy-start.18
  193.4 2.0 copy-start.2
  197.0 42.6 %collective-permute-start.6 = (f32[512,512]{0,1:T(8,128)}, f32[512,512]{0,1:T(8,128)S(1)}, u32[]{:S(2)}, u32[]{:S(2)}) collective-permute-start(f32[512,512]{0,1:T(8,128)} %get-tuple-element.27), channel_id=1, source_target_pairs={{1,0},{2,1},{3,2},{4,3},{5,4},{6,5},{7,6},{9,8},{10,9},{11,10},{12... | collective-permute-start | bytes 3145736 | tf_op jit(solution)/shard_map/ppermute | solution.py:15
  198.2 41.3 %collective-permute-start.7 = (f32[512,512]{0,1:T(8,128)}, f32[512,512]{0,1:T(8,128)}, u32[]{:S(2)}, u32[]{:S(2)}) collective-permute-start(f32[512,512]{0,1:T(8,128)} %get-tuple-element.28), channel_id=1, source_target_pairs={{0,1},{1,2},{2,3},{3,4},{4,5},{5,6},{6,7},{8,9},{9,10},{10,11},{11... | collective-permute-start | bytes 3145736 | tf_op jit(solution)/shard_map/ppermute | solution.py:15
  204.7 148.2 %reduce-scatter.9.cloned.1.call-start = ((), (), s32[]{:S(2)}) async-start(), calls=%async_computation.9 | async-start | bytes 2228224 | tf_op jit(solution)/shard_map/reduce_scatter | solution.py:152
  206.1 33.4 %collective-permute-start.8 = (f32[512,259]{0,1:T(8,128)S(1)}, f32[512,259]{0,1:T(8,128)S(1)}, u32[]{:S(2)}, u32[]{:S(2)}) collective-permute-start(f32[512,259]{0,1:T(8,128)S(1)} %get-tuple-element.29), channel_id=1, source_target_pairs={{2,0},{3,1},{4,2},{5,3},{6,4},{7,5},{10,8},{11,9},{12,10},{13,11},... | collective-permute-start | bytes 1591304 | tf_op jit(solution)/shard_map/ppermute | solution.py:15
  207.4 35.8 %copy-start.9 = (bf16[512,512]{0,1:T(8,128)(2,1)S(1)}, bf16[512,512]{0,1:T(8,128)(2,1)}, u32[]{:S(2)}) copy-start(bf16[512,512]{0,1:T(8,128)(2,1)} %copy-done.8) | copy-start | bytes 1572868
  207.4 32.1 %collective-permute-start.9 = (f32[512,259]{0,1:T(8,128)S(1)}, f32[512,259]{0,1:T(8,128)S(1)}, u32[]{:S(2)}, u32[]{:S(2)}) collective-permute-start(f32[512,259]{0,1:T(8,128)S(1)} %get-tuple-element.30), channel_id=1, source_target_pairs={{0,2},{1,3},{2,4},{3,5},{4,6},{5,7},{8,10},{9,11},{10,12},{11,13},... | collective-permute-start | bytes 1591304 | tf_op jit(solution)/shard_map/ppermute | solution.py:15
  242.4 0.8 copy-start.30
  243.2 2.1 copy-start.7
  243.2 2.2 copy-start.14
  243.2 2.2 copy-start.15
  245.3 201.5 %reduce-scatter.7.cloned.1.call-start = ((), (), s32[]{:S(2)}) async-start(), calls=%async_computation.8 | async-start | bytes 6684672 | tf_op jit(solution)/shard_map/reduce_scatter | solution.py:152
  251.1 1.2 copy-start.12
  251.1 5.0 copy-start.4
  251.2 288.6 %reduce-scatter.5.cloned.1.call-start = ((), (), s32[]{:S(2)}) async-start(), calls=%async_computation.7 | async-start | bytes 6684672 | tf_op jit(solution)/shard_map/reduce_scatter | solution.py:152
  252.3 3.8 copy-start.27
  252.3 3.8 copy-start.29
  255.2 0.8 copy-start.20
  255.2 1.0 copy-start.23
  260.7 1.0 copy-start.21
  260.7 1.2 copy-start.24
  260.8 362.9 %all-reduce.26.cloned.1.call-start = ((), (), s32[]{:S(2)}) async-start(), calls=%async_computation.11 | async-start | bytes 1966080 | tf_op jit(solution)/shard_map/psum | solution.py:151
  267.7 278.9 %copy-start.17 = (bf16[512,512]{0,1:T(8,128)(2,1)S(1)}, bf16[512,512]{0,1:T(8,128)(2,1)}, u32[]{:S(2)}) copy-start(bf16[512,512]{0,1:T(8,128)(2,1)} %copy-done.16) | copy-start | bytes 1572868
  539.8 6.8 %copy-start.19 = (bf16[512,512]{0,1:T(8,128)(2,1)S(1)}, bf16[512,512]{0,1:T(8,128)(2,1)}, u32[]{:S(2)}) copy-start(bf16[512,512]{0,1:T(8,128)(2,1)} %copy-done.18) | copy-start | bytes 1572868
  539.8 6.9 %copy-start.22 = (bf16[512,512]{0,1:T(8,128)(2,1)S(1)}, bf16[512,512]{0,1:T(8,128)(2,1)}, u32[]{:S(2)}) copy-start(bf16[512,512]{0,1:T(8,128)(2,1)} %copy-done.20) | copy-start | bytes 1572868
  539.8 6.9 %copy-start.25 = (bf16[512,512]{0,1:T(8,128)(2,1)S(1)}, bf16[512,512]{0,1:T(8,128)(2,1)}, u32[]{:S(2)}) copy-start(bf16[512,512]{0,1:T(8,128)(2,1)} %copy-done.23) | copy-start | bytes 1572868
  539.9 9.2 %copy-start.5 = (f32[512,512]{0,1:T(8,128)S(1)}, f32[512,512]{0,1:T(8,128)}, u32[]{:S(2)}) copy-start(f32[512,512]{0,1:T(8,128)} %get-tuple-element.26) | copy-start | bytes 3145732
  539.9 8.3 %collective-permute-start.10 = (f32[512,131]{0,1:T(8,128)S(1)}, f32[512,131]{0,1:T(8,128)S(1)}, u32[]{:S(2)}, u32[]{:S(2)}) collective-permute-start(f32[512,131]{0,1:T(8,128)S(1)} %get-tuple-element.67), channel_id=1, source_target_pairs={{1,0},{2,1},{3,2},{4,3},{5,4},{6,5},{7,6},{9,8},{10,9},{11,10},{12... | collective-permute-start | bytes 804872 | tf_op jit(solution)/shard_map/ppermute | solution.py:15
  541.3 7.7 %collective-permute-start.11 = (f32[512,131]{0,1:T(8,128)S(1)}, f32[512,131]{0,1:T(8,128)S(1)}, u32[]{:S(2)}, u32[]{:S(2)}) collective-permute-start(f32[512,131]{0,1:T(8,128)S(1)} %get-tuple-element.68), channel_id=1, source_target_pairs={{0,1},{1,2},{2,3},{3,4},{4,5},{5,6},{6,7},{8,9},{9,10},{10,11},{11... | collective-permute-start | bytes 804872 | tf_op jit(solution)/shard_map/ppermute | solution.py:15
  549.1 79.7 %copy-start.1 = (f32[6,512]{1,0:T(8,128)S(1)}, f32[6,512]{1,0:T(8,128)}, u32[]{:S(2)}) copy-start(f32[6,512]{1,0:T(8,128)} %param.18) | copy-start | bytes 36868
Sparse Core Ops, SparseCore 0:
  11.0 56.4 all-gather.7
  69.9 43.6 all-gather.5
  116.0 63.5 all-gather.9
  204.8 73.7 reduce-scatter.10
  282.9 69.9 reduce-scatter.8
  357.5 89.2 reduce-scatter.6
  451.5 88.2 reduce-scatter.4
  542.8 71.9 all-reduce.25
where the time goes:
time: 637 us; the launch traced here: 636 us
  waiting for transfers between devices  400 us (63%)
  blocking collectives  110 us (17%)
  matrix products  38.1 us (6%)
  starting transfers between devices  35.7 us (6%)
  local copies, waits for them, and re-layouts  18.5 us (3%)
  other arithmetic  17.6 us (3%)
  between operations  15.4 us (2%)
    reduce_scatter x4, waiting for transfers between devices, reduce_grad(): return lax.psum_scatter(summed, 'dp', scatter_dimension=0, tiled=True)  272 us
    psum x1, blocking collectives, local(): lax.psum((grad_start_local, jnp.stack([bias_first, bias_second]), grad_en...  73.7 us
    all_gather x2, waiting for transfers between devices, layer_forward(): lax.all_gather(conv_shard, 'dp', axis=0, tiled=True)  52.9 us
    all_gather x1, waiting for transfers between devices, layer_forward(): lax.all_gather(mix_shard, 'dp', axis=0, tiled=True)  40.6 us
    all_gather x1, blocking collectives, layer_forward(): lax.all_gather(mix_shard, 'dp', axis=0, tiled=True)  36.2 us
    ppermute x12, starting transfers between devices, from_behind(): return lax.ppermute(array, axis, pairs)  35.2 us
    ppermute x12, waiting for transfers between devices, from_behind(): return lax.ppermute(array, axis, pairs)  33.3 us
    dot_general x6, matrix products, contract_rows(): lax.dot_general(left_op, right_op, (((1,), (1,)), ((), ())), precision=pr...  15.2 us
  transfers between devices with their start and end apart: 20, of which 12 were waited for; matrix products, arithmetic and copies ran while one was open for 7% of the time, Pallas kernels for 0%

commit v1 on v0

v1 whole, which is shorter than its diff:
```python
import functools

import jax
import jax.numpy as jnp
from jax import lax
from jax.experimental import pallas as pl
from jax.experimental.pallas import tpu as pltpu
from jax.sharding import PartitionSpec as P

BUCKETS = 4
highest = lax.Precision.HIGHEST
bf16 = jnp.bfloat16
f32 = jnp.float32


def dot(a, b, ca=1, cb=0, precision=None):
    return lax.dot_general(
        a, b, (((ca,), (cb,)), ((), ())), precision=precision, preferred_element_type=f32
    )


def split(x):
    hi = lax.reduce_precision(x, 8, 7)
    return hi.astype(bf16), (x - hi).astype(bf16)


def pad_to(x, rows, cols):
    return jnp.pad(x, ((0, rows - x.shape[0]), (0, cols - x.shape[1])))


def shift(x, n):
    total = x.shape[1]
    if n > 0:
        return jnp.pad(x[:, : total - n], ((0, 0), (n, 0)))
    return jnp.pad(x[:, -n:], ((0, 0), (0, -n)))


def tap_of(x, off, dilation, side):
    out = shift(x, side * dilation)
    for step in range(1, BUCKETS):
        out = jnp.where(off == step, shift(x, side * (dilation + step)), out)
    return out


def tap_back(x, off, dilation, side):
    out = 0.0
    for step in range(BUCKETS):
        out = out + shift(jnp.where(off == step, x, 0.0), -side * (dilation + step))
    return out


def exchange(x, axis):
    return lax.all_to_all(x, axis, 0, 0, tiled=True)


def nt(a, b):
    return dot(a, b, 1, 1)


def rolled(x, start, width):
    if start % 128 == 0:
        return x[:, start : start + width]
    return pltpu.roll(x, x.shape[1] - start, 1)[:, :width]


def valid_row(c, width, length):
    at = lax.broadcasted_iota(jnp.int32, (1, width), 1) + c * width
    return (at < length).astype(f32)


def forward_kernel(
    dil0, dil1, half,
    info, fields, a_cat, w_cat, mix, w_taps, bias1, e_pair,
    g0_out, du0_out, dv0_out, h1_out, s_out, gown_out, du1_out, dv1_out, packet,
    fpad, s_cat, prod, g_keep,
):
    i = pl.program_id(0)
    nb = fields.shape[0]
    bw = fields.shape[2]
    rows = gown_out.shape[0] // 2
    channels = mix.shape[0]
    pad0 = 256
    pad1 = dil1 + 128
    length = info[0]
    k = info[1]

    @pl.when(i == 0)
    def _():
        fpad[:, 0:pad0] = jnp.zeros((8, pad0), f32)
        fpad[:, pad0 + nb * bw :] = jnp.zeros((8, pad0), f32)
        prod[:, 0:pad1] = jnp.zeros((prod.shape[0], pad1), f32)
        prod[:, pad1 + nb * bw :] = jnp.zeros((prod.shape[0], pad1), f32)
        s_cat[...] = jnp.zeros(s_cat.shape, f32)
        s_cat[27:29, :] = jnp.ones((2, bw), f32)
        packet[:, 24:32, :] = jnp.zeros((nb, 8, bw), f32)
        for c in range(nb):
            block = fields[c].astype(f32)
            valid = valid_row(c, bw, length)
            at = slice(pad0 + c * bw, pad0 + (c + 1) * bw)
            fpad[0:half, at] = block[0:half] * valid
            fpad[half : 2 * half, at] = block[2 * half : 3 * half] * valid
            fpad[6:7, at] = block[6 * half : 6 * half + 1]
            fpad[7:8, at] = valid

    base = pl.multiple_of(i * bw, bw)
    near = fpad[:, pl.ds(pl.multiple_of(pad0 + base, 128), bw)]
    off = near[6:7]
    valid = near[7:8]
    behind = fpad[:, pl.ds(pl.multiple_of(base, 128), bw + 2 * dil0)]
    ahead = fpad[:, pl.ds(pl.multiple_of(pad0 + base, 128), bw + 2 * dil0)]
    left = rolled(behind, dil0, bw)
    right = rolled(ahead, dil0, bw)
    for step in range(1, BUCKETS):
        left = jnp.where(off == step, rolled(behind, dil0 - step, bw), left)
        right = jnp.where(off == step, rolled(ahead, dil0 + step, bw), right)
    for part, at in ((left, 0), (near, 3), (right, 6)):
        s_cat[at : at + half, :] = part[0:half]
        s_cat[9 + at : 9 + at + half, :] = part[half : 2 * half]
        s_cat[18 + at : 18 + at + half, :] = part[0:half]
    s_b = s_cat[...].astype(bf16)
    s_out[...] = s_b
    step_rows = 128
    for r in range(0, channels, step_rows):
        u = dot(a_cat[r : r + step_rows, :], s_b)
        v = dot(a_cat[channels + r : channels + r + step_rows, :], s_b)
        t = jnp.tanh(u)
        s = 0.5 * jnp.tanh(0.5 * v) + 0.5
        g = t * s
        g0_out[r : r + step_rows, :] = g.astype(bf16)
        du0_out[r : r + step_rows, :] = (s - g * t).astype(bf16)
        dv0_out[r : r + step_rows, :] = (g - g * s).astype(bf16)
    h1 = dot(mix[...], g0_out[...]) + dot(w_cat[...], s_b)
    h1 = (h1 * valid).astype(bf16)
    h1_out[...] = h1
    prod[:, pl.ds(pl.multiple_of(pad1 + base, 128), bw)] = dot(w_taps[...], h1)
    g_keep[:, pl.ds(base, bw)] = g0_out[pl.ds(pl.multiple_of(rows * k, rows), rows), :]

    @pl.when(i == nb - 1)
    def _():
        def body(c, carry):
            base = pl.multiple_of(c * bw, bw)
            off = fpad[6:7, pl.ds(pl.multiple_of(pad0 + base, 128), bw)]
            pair = 2 * rows
            window = bw + 128
            behind = prod[0:pair, pl.ds(pl.multiple_of(base, 128), window)]
            ahead = prod[2 * pair :, pl.ds(pl.multiple_of(pad1 + dil1 + base, 128), window)]
            left = rolled(behind, 128, bw)
            right = rolled(ahead, 0, bw)
            for step in range(1, BUCKETS):
                left = jnp.where(off == step, rolled(behind, 128 - step, bw), left)
                right = jnp.where(off == step, rolled(ahead, step, bw), right)
            centre = prod[pair : 2 * pair, pl.ds(pl.multiple_of(pad1 + base, 128), bw)]
            pre = left + centre + right + bias1[...]
            t = jnp.tanh(pre[:rows])
            s = 0.5 * jnp.tanh(0.5 * pre[rows:]) + 0.5
            g = t * s
            du1_out[:, pl.ds(base, bw)] = s - g * t
            dv1_out[:, pl.ds(base, bw)] = g - g * s
            gown_out[0:rows, pl.ds(base, bw)] = g_keep[:, pl.ds(base, bw)]
            gown_out[rows:, pl.ds(base, bw)] = g.astype(bf16)
            part = dot(e_pair[...], gown_out[:, pl.ds(base, bw)])
            part = part[0 : 2 * half] + part[8 : 8 + 2 * half]
            for d in range(nb):
                for h in range(half):
                    packet[d, pl.ds(h * nb + c, 1), :] = part[h : h + 1]
            packet[c, 24 : 24 + half, :] = part[half : 2 * half]
            return carry

        lax.fori_loop(0, nb, body, 0)


def backward_kernel(
    dil1, half,
    info, got, fields, flux, e_up, gown, du1, dv1, w_taps_t, mix_t,
    g0, du0, dv0, h1, s_in,
    coupled, packet,
    ends, d_cat, dz_pad, off_pad, d_e0, d_taps, acc_conv, acc_mix, acc_m, acc_s, acc_g, acc_b,
    dg, m_rows, share,
):
    i = pl.program_id(0)
    nb = fields.shape[0]
    bw = fields.shape[2]
    pair = gown.shape[0]
    rows = pair // 2
    channels = mix_t.shape[0]
    n_dp = packet.shape[0]
    pad1 = dil1 + 128
    length = info[0]
    k = info[1]

    @pl.when(i == 0)
    def _():
        for ref in (acc_conv, acc_mix, acc_m, acc_s, acc_g, acc_b, d_cat, m_rows, share):
            ref[...] = jnp.zeros(ref.shape, f32)
        dz_pad[:, 0:pad1] = jnp.zeros((pair, pad1), f32)
        dz_pad[:, pad1 + nb * bw :] = jnp.zeros((pair, pad1), f32)
        off_pad[:, 0:pad1] = jnp.full((8, pad1), -1.0, f32)
        off_pad[:, pad1 + nb * bw :] = jnp.full((8, pad1), -1.0, f32)
        total = got[0]
        for src in range(1, nb):
            total = total + got[src]
        ends[...] = total
        mine = valid_row(k, bw, length)
        for h in range(half):
            growth = jnp.exp(ends[pl.ds(h * nb + k, 1), :])
            coupled[0, h : h + 1, :] = (
                growth * flux[half + h : half + h + 1] + ends[24 + h : 25 + h, :]
            ) * mine

        def first(c, carry):
            base = pl.multiple_of(c * bw, bw)
            at = pl.multiple_of(pad1 + base, 128)
            block = fields[c].astype(f32)
            valid = valid_row(c, bw, length)
            off_pad[0:1, pl.ds(at, bw)] = block[6 * half : 6 * half + 1]
            flux2 = block[half : 2 * half] + block[3 * half : 4 * half]
            cot = (block[4 * half : 5 * half] + block[5 * half : 6 * half]) * valid
            for h in range(half):
                growth = jnp.exp(ends[pl.ds(h * nb + c, 1), :])
                d_cat[h : h + 1, :] = cot[h : h + 1] * growth * flux2[h : h + 1]
            d_cat[half : 2 * half, :] = cot
            full = d_cat[0:8, :]
            hi = full.astype(bf16).astype(f32)
            lo = full - hi
            d_cat[8:16, :] = lo
            d_cat[16:24, :] = hi
            d_gated = dot(e_up[...], d_cat[...].astype(bf16))
            acc_g[...] += nt(d_cat[8:24, :].astype(bf16), gown[:, pl.ds(base, bw)])
            d_e0[:, pl.ds(base, bw)] = d_gated[:rows]
            up = d_gated[rows : 2 * rows]
            dz_pad[0:rows, pl.ds(at, bw)] = up * du1[:, pl.ds(base, bw)]
            dz_pad[rows:, pl.ds(at, bw)] = up * dv1[:, pl.ds(base, bw)]
            return carry

        lax.fori_loop(0, nb, first, 0)

        def second(c, carry):
            base = pl.multiple_of(c * bw, bw)
            window = bw + 128
            ahead = dz_pad[:, pl.ds(pl.multiple_of(pad1 + dil1 + base, 128), window)]
            off_a = off_pad[0:1, pl.ds(pl.multiple_of(pad1 + dil1 + base, 128), window)]
            behind = dz_pad[:, pl.ds(base, window)]
            off_b = off_pad[0:1, pl.ds(base, window)]
            left = 0.0
            right = 0.0
            for step in range(BUCKETS):
                left = left + rolled(jnp.where(off_a == step, ahead, 0.0), step, bw)
                right = right + rolled(jnp.where(off_b == step, behind, 0.0), 128 - step, bw)
            centre = dz_pad[:, pl.ds(pl.multiple_of(pad1 + base, 128), bw)].astype(bf16)
            d_taps[0:pair, pl.ds(base, bw)] = left.astype(bf16)
            d_taps[pair : 2 * pair, pl.ds(base, bw)] = centre
            d_taps[2 * pair :, pl.ds(base, bw)] = right.astype(bf16)
            acc_b[...] += nt(jnp.ones((16, bw), bf16), centre)
            return carry

        lax.fori_loop(0, nb, second, 0)

    base = pl.multiple_of(i * bw, bw)
    d_blk = d_taps[:, pl.ds(base, bw)]
    acc_conv[...] += nt(d_blk, h1[...])
    field = (dot(w_taps_t[...], d_blk) * valid_row(i, bw, length)).astype(bf16)
    s_b = s_in[...]
    acc_mix[...] += nt(field, g0[...])
    acc_s[...] += nt(s_b, field)
    dg[...] = dot(mix_t[...], field)
    own = pl.ds(pl.multiple_of(rows * k, rows), rows)
    dg[own, :] = dg[own, :] + d_e0[:, pl.ds(base, bw)]
    up = dg[...]
    acc_m[:, 0:channels] += nt(s_b, (up * du0[...].astype(f32)).astype(bf16))
    acc_m[:, channels:] += nt(s_b, (up * dv0[...].astype(f32)).astype(bf16))

    @pl.when(i == nb - 1)
    def _():
        per_mix = channels // n_dp
        eighth = pair // n_dp
        m_rows[0:9, :] = acc_m[0:9, :] + acc_m[9:18, :]
        m_rows[9:10, :] = acc_m[27:28, :]
        starts = acc_s[3 : 3 + half, :] + acc_s[12 : 12 + half, :]
        share[0:1, 0:128] = acc_b[0:1, :]
        share[0 : 2 * half, 128:256] = acc_g[8 : 8 + 2 * half, :] + acc_g[0 : 2 * half, :]
        for j in range(n_dp):
            row = 64 * (j % (n_dp // 2)) + per_mix * (j // (n_dp // 2))
            packet[j, 0:per_mix, :] = acc_mix[row : row + per_mix, :].astype(bf16)
            for tap in range(3):
                at = per_mix + tap * eighth
                row = tap * pair + j * eighth
                packet[j, at : at + eighth, :] = acc_conv[row : row + eighth, :].astype(bf16)
            if j < channels // 128:
                share[1 : 1 + half, 0:128] = starts[:, 128 * j : 128 * (j + 1)]
            else:
                share[1 : 1 + half, 0:128] = jnp.zeros((half, 128), f32)
            at = per_mix + 3 * eighth
            cols = slice(128 * (j // 2), 128 * (j // 2) + 128)
            share[6:8, 0:128] = m_rows[8:10, cols]
            packet[j, at : at + 8, 0:128] = m_rows[0:8, cols].astype(bf16)
            packet[j, at : at + 8, 128:256] = share[:, 0:128].astype(bf16)
            packet[j, at : at + 8, 256:384] = share[:, 128:256].astype(bf16)
            packet[j, at : at + 8, 384:512] = jnp.zeros((8, 128), bf16)


def whole(shape):
    return pl.BlockSpec(shape, lambda i: (0,) * len(shape))


def columns(rows, width):
    return pl.BlockSpec((rows, width), lambda i: (0, i))


def local(
    light_flux,
    lengths,
    offsets,
    start_weight,
    conv_weight,
    gate_bias,
    mix_first,
    mix_last,
    end_weight,
    cotangent,
):
    n_dp = lax.axis_size("dp")
    n_ctx = lax.axis_size("ctx")
    half_dp = n_dp // 2
    dp = lax.axis_index("dp")
    k = lax.axis_index("ctx")
    low = dp < half_dp
    shard_len = light_flux.shape[2]
    half = light_flux.shape[1] // 2
    channels = start_weight.shape[0]
    epochs = shard_len * n_ctx
    dilations = (shard_len // 4, shard_len + shard_len // 2)
    rows = conv_weight.shape[1]
    last_rows = mix_last.shape[0]
    conv0, conv1 = conv_weight[0], conv_weight[1]
    part = rows // n_ctx
    n_e = 2 * half

    def strided(x):
        lead = x.shape[0]
        cols = x.shape[1]
        view = x.reshape(lead, cols // rows, n_ctx, part)
        return lax.dynamic_slice(
            view, (0, 0, k, 0), (lead, cols // rows, 1, part)
        ).reshape(lead, cols // n_ctx)

    flux_hi, flux_lo = split(light_flux[0])
    cot_hi, cot_lo = split(cotangent[0])
    n_in = 6 * half + 1
    inputs = jnp.concatenate(
        [flux_hi, flux_lo, cot_hi, cot_lo, offsets.astype(bf16)], axis=0
    )
    n_pad = -(-n_in // 8) * 8
    inputs = pad_to(inputs, n_pad, shard_len)

    sw_hi, sw_lo = split(start_weight)
    sw_pair = jnp.concatenate([sw_hi, sw_lo], axis=1)
    a_rows = []
    for tap in range(3):
        parts = dot(sw_pair, conv0[:, tap * channels : (tap + 1) * channels], 0, 1)
        a_rows.append(parts[:half] + parts[half:])
    a_own = jnp.concatenate(a_rows, axis=0)
    ew_last = lax.dynamic_slice(end_weight, (0, last_rows * dp), (n_e, last_rows))
    ew_skip = lax.dynamic_slice(
        end_weight, (0, rows * jnp.maximum(dp - half_dp, 0)), (n_e, rows)
    )
    ew_skip = jnp.where(low, 0.0, ew_skip)
    mix_last_k = strided(mix_last).astype(f32)
    mix_skip_k = lax.dynamic_slice(mix_first, (0, rows * k), (rows, rows)).astype(f32)
    e_own = jnp.concatenate(
        [
            dot(ew_skip, mix_skip_k, precision=highest),
            dot(ew_last, mix_last_k, precision=highest),
        ],
        axis=1,
    )
    a_hi, a_lo = split(a_own)
    e_hi, e_lo = split(e_own)
    a_block = pad_to(jnp.concatenate([a_hi, a_lo], axis=0), 20, rows).reshape(5, 4 * rows)
    small = jnp.concatenate(
        [pad_to(jnp.concatenate([e_hi, e_lo], axis=1), 8, 4 * rows), pad_to(a_block, 8, 4 * rows)],
        axis=1,
    )
    conv_k = lax.dynamic_slice(conv1, (part * k, 0), (part, 3 * channels))
    mix_k = lax.dynamic_slice(mix_first, (part * k, 0), (part, channels))
    packet = jnp.concatenate(
        [conv_k[:, tap * channels : (tap + 1) * channels] for tap in range(3)] + [mix_k, small],
        axis=0,
    )
    per = packet.shape[0]
    got = exchange(
        jnp.broadcast_to(packet[None], (n_dp, per, channels)).reshape(n_dp * per, channels), "dp"
    ).reshape(n_dp, per, channels)
    w_taps = got[:, : 3 * part].reshape(n_dp, 3, part, channels).transpose(1, 0, 2, 3)
    w_taps = w_taps.reshape(6 * rows, channels)
    mix_part = got[:half_dp, 3 * part : 4 * part].reshape(rows, channels)
    both = jnp.concatenate([inputs, mix_part], axis=0)
    ctx_got = exchange(
        jnp.broadcast_to(both[None], (n_ctx,) + both.shape).reshape(-1, channels), "ctx"
    ).reshape((n_ctx,) + both.shape)
    fields = ctx_got[:, :n_pad]
    mix_res = ctx_got[:, n_pad:].reshape(n_ctx, half_dp, part, channels).transpose(1, 0, 2, 3)
    mix_res = mix_res.reshape(channels, channels)
    e_k = got[:, 4 * part : 4 * part + n_e, : 4 * rows].astype(f32).sum(axis=0)
    e_cat = e_k[:, : 2 * rows] + e_k[:, 2 * rows :]
    a_all = got[:, 4 * part : 4 * part + 5, 4 * rows :].reshape(n_dp, 20, rows)
    a_all = a_all[:, :18].transpose(1, 0, 2).reshape(18, n_dp * rows)
    a_hi, a_lo = a_all[:9], a_all[9:]

    length = lengths[0]
    b_hi, b_lo = split(gate_bias[0][None])
    a_cat = jnp.concatenate(
        [a_hi, a_hi, a_lo, b_hi, b_lo, jnp.zeros((3, 2 * channels), bf16)], axis=0
    ).T
    gap = jnp.zeros((6, channels), bf16)
    w_cat = jnp.concatenate(
        [gap[:3], sw_hi.T, gap, sw_hi.T, gap, sw_lo.T, gap[:3], gap[:5]], axis=0
    ).T
    ec_hi, ec_lo = split(e_cat)
    gap = jnp.zeros((2, 2 * rows), bf16)
    e_pair = jnp.concatenate([ec_hi, gap, ec_lo, gap], axis=0)
    e_up = pad_to(jnp.concatenate([ec_hi, gap, ec_hi, gap, ec_lo], axis=0), 32, 2 * rows).T
    bias1 = strided(gate_bias[1][None]).T
    info = jnp.stack([length, k])
    pair = 2 * rows
    wide = epochs + 2 * (dilations[1] + 128)
    smem = pl.BlockSpec(memory_space=pltpu.SMEM)
    shapes = jax.ShapeDtypeStruct
    params = pltpu.CompilerParams(
        dimension_semantics=("arbitrary",), vmem_limit_bytes=60000 * 1024
    )
    forward = pl.pallas_call(
        functools.partial(forward_kernel, dilations[0], dilations[1], half),
        grid=(n_ctx,),
        in_specs=[
            smem,
            whole((n_ctx, n_pad, shard_len)),
            whole(a_cat.shape),
            whole(w_cat.shape),
            whole(mix_res.shape),
            whole(w_taps.shape),
            whole(bias1.shape),
            whole(e_pair.shape),
        ],
        out_specs=[columns(channels, shard_len)] * 4
        + [columns(32, shard_len), whole((pair, epochs)), whole((rows, epochs)),
           whole((rows, epochs)), whole((n_ctx, 32, shard_len))],
        out_shape=[shapes((channels, epochs), bf16)] * 4
        + [shapes((32, epochs), bf16), shapes((pair, epochs), bf16), shapes((rows, epochs), f32),
           shapes((rows, epochs), f32), shapes((n_ctx, 32, shard_len), f32)],
        scratch_shapes=[
            pltpu.VMEM((8, epochs + 512), f32),
            pltpu.VMEM((32, shard_len), f32),
            pltpu.VMEM((3 * pair, wide), f32),
            pltpu.VMEM((rows, epochs), bf16),
        ],
        compiler_params=params,
        name="layers_forward",
    )
    g0, du0, dv0, h1, s_all, g_own, du1, dv1, packed = forward(
        info, fields, a_cat, w_cat, mix_res, w_taps, bias1, e_pair
    )
    got = exchange(packed.reshape(n_ctx * 32, shard_len), "ctx").reshape(n_ctx, 32, shard_len)

    n_mix = channels // n_dp
    n_conv = 3 * pair // n_dp
    per = n_mix + n_conv + 8
    backward = pl.pallas_call(
        functools.partial(backward_kernel, dilations[1], half),
        grid=(n_ctx,),
        in_specs=[
            smem,
            whole((n_ctx, 32, shard_len)),
            whole((n_ctx, n_pad, shard_len)),
            whole((2 * half, shard_len)),
            whole((pair, 32)),
            whole((pair, epochs)),
            whole((rows, epochs)),
            whole((rows, epochs)),
            whole((channels, 3 * pair)),
            whole((channels, channels)),
        ]
        + [columns(channels, shard_len)] * 4
        + [columns(32, shard_len)],
        out_specs=[whole((1, half, shard_len)), whole((n_dp, per, channels))],
        out_shape=[shapes((1, half, shard_len), f32), shapes((n_dp, per, channels), bf16)],
        scratch_shapes=[
            pltpu.VMEM((32, shard_len), f32),
            pltpu.VMEM((32, shard_len), f32),
            pltpu.VMEM((pair, wide), f32),
            pltpu.VMEM((8, wide), f32),
            pltpu.VMEM((rows, epochs), f32),
            pltpu.VMEM((3 * pair, epochs), bf16),
            pltpu.VMEM((3 * pair, channels), f32),
            pltpu.VMEM((channels, channels), f32),
            pltpu.VMEM((32, 2 * channels), f32),
            pltpu.VMEM((32, channels), f32),
            pltpu.VMEM((16, pair), f32),
            pltpu.VMEM((16, pair), f32),
            pltpu.VMEM((channels, shard_len), f32),
            pltpu.VMEM((16, 2 * channels), f32),
            pltpu.VMEM((8, 256), f32),
        ],
        compiler_params=params,
        name="layers_backward",
    )
    coupled, packed = backward(
        info, got, fields, light_flux[0], e_up, g_own, du1, dv1, w_taps.T, mix_res.T,
        g0, du0, dv0, h1, s_all,
    )
    got = exchange(packed.reshape(n_dp * per, channels), "dp").reshape(n_dp, per, channels)
    got = got.astype(f32).sum(axis=0)
    mix_piece = got[:n_mix]
    conv_piece = got[n_mix : n_mix + n_conv].astype(bf16)
    smalls = got[n_mix + n_conv :]
    near = lax.dynamic_slice(smalls, (0, rows * (dp % 2)), (8, rows))
    far = lax.dynamic_slice(smalls, (6, 128 + rows * (dp % 2)), (2, rows))
    m_own = jnp.concatenate([near, far], axis=0)
    start_own = jnp.where(dp < channels // 128, smalls[1 : 1 + half, 128:256], 0.0)
    g_own_sum = smalls[: 2 * half, 256:384]
    bias1_own = smalls[0:1, 128:256]
    mo_hi, mo_lo = split(m_own)
    mo_pair = jnp.concatenate([mo_hi[:9], mo_lo[:9]], axis=0)
    start_t = 0.0
    for tap in range(3):
        up = dot(mo_pair, conv0[:, tap * channels : (tap + 1) * channels])
        start_t = start_t + up[half * tap : half * tap + half] + up[9 + half * tap : 9 + half * tap + half]
    spot = lax.dynamic_update_slice(
        jnp.zeros((half, channels), f32), start_own, (0, 128 * (dp % (channels // 128)))
    )
    start_t = start_t + spot
    end_last = dot(g_own_sum[:, rows:], mix_last_k, 1, 1, highest)
    end_skip = jnp.where(low, 0.0, dot(g_own_sum[:, :rows], mix_skip_k, 1, 1, highest))
    g_rows = jnp.concatenate([g_own_sum, bias1_own], axis=0)
    parts = jnp.concatenate(
        [
            m_own,
            pad_to(g_rows, 10, 2 * rows),
            pad_to(jnp.concatenate([end_last, end_skip], axis=1), 10, last_rows + rows),
        ],
        axis=1,
    )
    width = parts.shape[1]
    pack_rows = [
        conv_piece,
        mix_piece.astype(bf16),
        pad_to(parts, 10, channels).astype(bf16),
        start_t.astype(bf16),
    ]
    packed = jnp.concatenate(pack_rows, axis=0)
    per0 = packed.shape[0]
    per = -(-per0 // 8) * 8
    packed = pad_to(packed, per, channels)
    got = exchange(
        jnp.broadcast_to(packed[None], (n_ctx, per, channels)).reshape(n_ctx * per, channels), "ctx"
    ).reshape(n_ctx, per, channels)
    grad_conv1 = got[:, :n_conv].reshape(n_ctx, 3, part, channels).transpose(0, 2, 1, 3)
    grad_conv1 = grad_conv1.reshape(rows, 3 * channels).astype(f32)
    mix_rows = got[:, n_conv : n_conv + n_mix].astype(f32).sum(axis=0)
    base = n_conv + n_mix
    parts = got[:, base : base + 10, :width].astype(f32)
    start_t = got[:, base + 10 : base + 10 + half].astype(f32).sum(axis=0)
    m_own = parts[:, :, :rows].sum(axis=0)
    g_all = parts[:, : 2 * half, rows : 3 * rows]
    g0_all = g_all[:, :, :rows].transpose(1, 0, 2).reshape(2 * half, channels)
    g1_all = g_all[:, :, rows:].reshape(n_ctx, 2 * half, half_dp, part).transpose(1, 2, 0, 3)
    g1_all = g1_all.reshape(2 * half, channels)
    bias1_all = parts[:, 2 * half, rows : 3 * rows].reshape(n_ctx, n_dp, part).transpose(1, 0, 2)
    bias1_all = bias1_all.reshape(2 * channels)
    end_both = parts[:, : 2 * half, 3 * rows :].sum(axis=0)
    a_grad = m_own[:9].T
    grad_conv0 = jnp.concatenate(
        [
            dot(a_grad[:, half * tap : half * tap + half], start_weight, 1, 1, highest)
            for tap in range(3)
        ],
        axis=1,
    )
    grad_mix_last = dot(ew_last, g1_all, 0, 0, highest)
    skip_rows = dot(ew_skip, g0_all, 0, 0, highest)

    other = lax.ppermute(mix_rows, "dp", [(i + half_dp, i) for i in range(half_dp)])
    final = jnp.concatenate(
        [
            start_t.reshape(-1, 128),
            pad_to(end_both, 2 * half, 128),
            pad_to(m_own[9:10], 1, 128),
        ],
        axis=0,
    )
    per0 = final.shape[0]
    per = -(-per0 // 8) * 8
    final = pad_to(final, per, 128)
    got = exchange(
        jnp.broadcast_to(final[None], (n_dp, per, 128)).reshape(n_dp * per, 128), "dp"
    ).reshape(n_dp, per, 128)
    n_start = half * channels // 128
    grad_start = got[:, :n_start].sum(axis=0).reshape(half, channels).T
    ends = got[:, n_start : n_start + 2 * half]
    grad_end = ends[:, :, :last_rows].transpose(1, 0, 2).reshape(2 * half, channels)
    grad_end = grad_end + ends[half_dp:, :, last_rows : last_rows + rows].transpose(
        1, 0, 2
    ).reshape(2 * half, channels)
    bias0_all = got[:, n_start + 2 * half, :rows].reshape(2 * channels)
    grad_bias = jnp.stack([bias0_all, bias1_all])
    residual = jnp.concatenate([mix_rows, other], axis=0)
    grad_mix_first = jnp.where(low, residual, skip_rows)
    grad_conv = jnp.stack([grad_conv0, grad_conv1])
    return (coupled, grad_start, grad_conv, grad_bias, grad_mix_first, grad_mix_last, grad_end)


def solution(mesh):
    in_specs = (
        P("dp", None, "ctx"),
        P("dp"),
        P("dp", "ctx"),
        P(),
        P(None, "dp", None),
        P(),
        P("dp", None),
        P("dp", None),
        P(),
        P("dp", None, "ctx"),
    )
    out_specs = (
        P("dp", None, "ctx"),
        P(),
        P(None, "dp", None),
        P(),
        P("dp", None),
        P("dp", None),
        P(),
    )
    return jax.shard_map(local, mesh=mesh, in_specs=in_specs, out_specs=out_specs, check_vma=False)
```

time: 637 us -> 172 us (0.27)
  waiting for transfers between devices: 400 us -> 54.6 us
  blocking collectives: 110 us -> 0 us
  Pallas kernels: 0 us -> 48.5 us
  matrix products: 38.1 us -> 6.6 us
  between operations: 15.4 us -> 1.79 us
  other arithmetic: 17.6 us -> 7.81 us
    reduce_scatter x4 -> x0, waiting for transfers between devices: 272 us -> none  [reduce_grad(): return lax.psum_scatter(summed, 'dp', scatter_dimension=0, tiled=True)]
    all_gather x3 -> x0, waiting for transfers between devices: 93.5 us -> none  [the longest x2 52.9 us: layer_forward(): lax.all_gather(conv_shard, 'dp', axis=0, tiled=True)]
    psum x1 -> x0, blocking collectives: 73.7 us -> none  [local(): lax.psum((grad_start_local, jnp.stack([bias_first, bias_second]), grad_en...]
    all_to_all x0 -> x6, waiting for transfers between devices: none -> 51.1 us  [exchange(): return lax.all_to_all(x, axis, 0, 0, tiled=True)]
    pallas_call x0 -> x2, Pallas kernels: none -> 48.5 us  [the longest x1 25.7 us: local(): backward(info, got, fields, light_flux[0], e_up, g_own, du1, dv1, w_taps....]
    all_gather x1 -> x0, blocking collectives: 36.2 us -> none  [layer_forward(): lax.all_gather(mix_shard, 'dp', axis=0, tiled=True)]
    ppermute x12 -> x1, starting transfers between devices: 35.2 us -> 1.29 us  [local(): lax.ppermute(mix_rows, 'dp', [(i + half_dp, i) for i in range(half_dp)])]
    dot_general x17 -> x15, matrix products: 38.1 us -> 6.6 us  [dot(): lax.dot_general(a, b, (((ca,), (cb,)), ((), ())), precision=precision, pr...]
  transfers between devices with their start and end apart: 20 -> 7, of which waited for: 12 -> 6; matrix products, arithmetic and copies ran while one was open for 7% -> 9% of each run, Pallas kernels for 0% -> 0%
where the time goes in v1:
time: 172 us; the launch traced here: 171 us
  waiting for transfers between devices  54.6 us (32%)
  Pallas kernels  48.5 us (28%)
  starting transfers between devices  32.4 us (19%)
  local copies, waits for them, and re-layouts  18.9 us (11%)
  other arithmetic  7.81 us (5%)
  matrix products  6.6 us (4%)
  between operations  1.79 us (1%)
    all_to_all x6, waiting for transfers between devices, exchange(): return lax.all_to_all(x, axis, 0, 0, tiled=True)  51.1 us
    all_to_all x6, starting transfers between devices, exchange(): return lax.all_to_all(x, axis, 0, 0, tiled=True)  31.1 us
    pallas_call x1, Pallas kernels, local(): backward(info, got, fields, light_flux[0], e_up, g_own, du1, dv1, w_taps....  25.7 us
    pallas_call x1, Pallas kernels, local(): forward(info, fields, a_cat, w_cat, mix_res, w_taps, bias1, e_pair)  22.8 us
    dot_general x15, matrix products, dot(): lax.dot_general(a, b, (((ca,), (cb,)), ((), ())), precision=precision, pr...  6.6 us
    unnamed x21, local copies, waits for them, and re-layouts  3.63 us
    ppermute x1, waiting for transfers between devices, local(): lax.ppermute(mix_rows, 'dp', [(i + half_dp, i) for i in range(half_dp)])  3.5 us
  transfers between devices with their start and end apart: 7, of which 6 were waited for; matrix products, arithmetic and copies ran while one was open for 9% of the time, Pallas kernels for 0%

profile of v1, /device:TPU:1, one launch (start us, length us, event | category | flops | bytes accessed | tf_op | source)
XLA Modules:
  0.0 170.6 jit_solution(9498423060367658248)
XLA Ops:
  0.6 1.0 slice_bitcast_fusion.3
  1.7 0.7 reduce-precision_convert_fusion.2
  2.7 0.1 fusion.21
  2.8 0.9 copy.59
  3.8 0.7 constant_dynamic-update-slice_fusion.1
  4.6 0.9 fusion.36
  5.5 0.9 fusion.30
  6.5 0.9 broadcast_in_dim.44
  7.4 9.1 %all-to-all-start = ((bf16[16,40,512]{2,1,0:T(8,128)(2,1)}), bf16[16,40,512]{2,1,0:T(8,128)(2,1)S(1)}, u32[]{:S(2)}, u32[]{:S(2)}) async-start(bf16[16,40,512]{2,1,0:T(8,128)(2,1)} %broadcast_in_dim.44), calls=%async_computation | async-start | bytes 1310720 | tf_op jit(solution)/shard_map/all_to_all | solution.py:53
  16.5 0.8 slice_reduce_fusion.5
  17.3 0.7 convert_element_type.121
  18.1 0.7 transpose_reshape.4.bias1
  18.8 0.3 concatenate.79
  19.1 0.8 copy.63
  20.5 0.7 fusion.46
  21.2 0.7 fusion.26
  21.9 0.2 concatenate.69
  22.2 0.6 pad_add_fusion.info
  22.7 6.1 %all-to-all-done = bf16[16,40,512]{2,1,0:T(8,128)(2,1)S(1)} async-done(((bf16[16,40,512]{2,1,0:T(8,128)(2,1)}), bf16[16,40,512]{2,1,0:T(8,128)(2,1)S(1)}, u32[]{:S(2)}, u32[]{:S(2)}) %all-to-all-start) | async-done | bytes 655392 | tf_op jit(solution)/shard_map/all_to_all | solution.py:53
  29.3 0.4 concatenate.78
  29.6 0.8 copy.62
  30.5 0.9 broadcast_in_dim.45
  31.4 4.8 %all-to-all-start.1 = ((bf16[8,88,512]{2,1,0:T(8,128)(2,1)}), bf16[8,88,512]{2,1,0:T(8,128)(2,1)S(1)}, u32[]{:S(2)}, u32[]{:S(2)}) async-start(bf16[8,88,512]{2,1,0:T(8,128)(2,1)} %broadcast_in_dim.45), calls=%async_computation.1 | async-start | bytes 1441792 | tf_op jit(solution)/shard_map/all_to_all | solution.py:53
  36.2 0.8 copy.65
  37.0 0.6 pad_maximum_fusion.7.e_pair
  37.6 10.8 %all-to-all-done.1 = bf16[8,88,512]{2,1,0:T(8,128)(2,1)S(1)} async-done(((bf16[8,88,512]{2,1,0:T(8,128)(2,1)}), bf16[8,88,512]{2,1,0:T(8,128)(2,1)S(1)}, u32[]{:S(2)}, u32[]{:S(2)}) %all-to-all-start.1) | async-done | bytes 720928 | tf_op jit(solution)/shard_map/all_to_all | solution.py:53
  48.5 0.8 copy.64
  49.4 0.7 slice.282.fields
  50.0 22.8 %layers_forward.1 = (bf16[512,4096]{1,0:T(8,128)(2,1)}, bf16[512,4096]{1,0:T(8,128)(2,1)}, bf16[512,4096]{1,0:T(8,128)(2,1)}, bf16[512,4096]{1,0:T(8,128)(2,1)},...) custom-call(s32[2]{0:T(128)} %pad_add_fusion.info, ...), custom_call_target="tpu_custom_call" | custom-call | tf_op jit(solution)/shard_map/layers_forward/pallas_call | solution.py:459
  72.9 3.5 %all-to-all-start.2 = ((f32[8,32,512]{2,1,0:T(8,128)}), f32[8,32,512]{2,1,0:T(8,128)S(1)}, u32[]{:S(2)}, u32[]{:S(2)}) async-start(f32[8,32,512]{2,1,0:T(8,128)} %get-tuple-element.18), calls=%async_computation.2 | async-start | bytes 1048576 | tf_op jit(solution)/shard_map/all_to_all | solution.py:53
  76.4 0.6 copy.86
  77.1 0.9 copy.68
  78.0 0.1 copy.67
  78.1 0.6 pad_bitcast_fusion.e_up
  78.8 1.0 copy.69
  79.8 6.8 %all-to-all-done.2.got = f32[8,32,512]{2,1,0:T(8,128)S(1)} async-done(((f32[8,32,512]{2,1,0:T(8,128)}), f32[8,32,512]{2,1,0:T(8,128)S(1)}, u32[]{:S(2)}, u32[]{:S(2)}) %all-to-all-start.2) | async-done | bytes 524320 | tf_op jit(solution)/shard_map/all_to_all | solution.py:53
  86.5 0.8 copy-done.2
  87.3 25.7 %layers_backward.1 = (f32[1,3,512]{2,1,0:T(4,128)}, bf16[16,64,512]{2,1,0:T(8,128)(2,1)}) custom-call(s32[2]{0:T(128)} %pad_add_fusion.info, f32[8,32,512]{2,1,0:T(8,128)} %copy-done.2, bf16[8,24,512]{2,1,0:T(8,128)(2,1)} %slice.282.fields, f32[6,512]{1,0:T(8,128)} %bitcast.89, bf16[128,32]{1,0:T(8,128)(2,1)} %pad_bitcast_fusion.e_up, ...), custom_call_target="tpu_custom_call" | custom-call | tf_op jit(solution)/shard_map/layers_backward/pallas_call | solution.py:506
  113.0 5.5 %all-to-all-start.3 = ((bf16[16,64,512]{2,1,0:T(8,128)(2,1)}), bf16[16,64,512]{2,1,0:T(8,128)(2,1)S(1)}, u32[]{:S(2)}, u32[]{:S(2)}) async-start(bf16[16,64,512]{2,1,0:T(8,128)(2,1)} %get-tuple-element.28), calls=%async_computation.3 | async-start | bytes 2097152 | tf_op jit(solution)/shard_map/all_to_all | solution.py:53
  118.5 17.2 %all-to-all-done.3 = bf16[16,64,512]{2,1,0:T(8,128)(2,1)S(1)} async-done(((bf16[16,64,512]{2,1,0:T(8,128)(2,1)}), bf16[16,64,512]{2,1,0:T(8,128)(2,1)S(1)}, u32[]{:S(2)}, u32[]{:S(2)}) %all-to-all-start.3) | async-done | bytes 1048608 | tf_op jit(solution)/shard_map/all_to_all | solution.py:53
  135.7 0.1 convert_reduce_fusion
  135.9 0.2 convolution_convert_fusion
  136.1 0.9 fusion
  137.3 0.1 fusion.19
  137.4 0.1 fusion.15
  137.5 0.1 fusion.11
  137.9 0.9 broadcast_in_dim.50
  138.8 3.5 %all-to-all-start.4 = ((bf16[8,72,512]{2,1,0:T(8,128)(2,1)}), bf16[8,72,512]{2,1,0:T(8,128)(2,1)S(1)}, u32[]{:S(2)}, u32[]{:S(2)}) async-start(bf16[8,72,512]{2,1,0:T(8,128)(2,1)} %broadcast_in_dim.50), calls=%async_computation.4 | async-start | bytes 1179648 | tf_op jit(solution)/shard_map/all_to_all | solution.py:53
  142.3 0.6 copy.76
  142.9 10.2 %all-to-all-done.4 = bf16[8,72,512]{2,1,0:T(8,128)(2,1)S(1)} async-done(((bf16[8,72,512]{2,1,0:T(8,128)(2,1)}), bf16[8,72,512]{2,1,0:T(8,128)(2,1)S(1)}, u32[]{:S(2)}, u32[]{:S(2)}) %all-to-all-start.4) | async-done | bytes 589856 | tf_op jit(solution)/shard_map/all_to_all | solution.py:53
  153.3 0.3 fusion.76
  153.7 0.3 fusion.78
  154.0 0.3 fusion.80
  154.4 0.7 broadcast_in_dim.51
  155.1 4.7 %all-to-all-start.5 = ((f32[16,24,128]{2,1,0:T(8,128)}), f32[16,24,128]{2,1,0:T(8,128)S(1)}, u32[]{:S(2)}, u32[]{:S(2)}) async-start(f32[16,24,128]{2,1,0:T(8,128)} %broadcast_in_dim.51), calls=%async_computation.5 | async-start | bytes 393216 | tf_op jit(solution)/shard_map/all_to_all | solution.py:53
  159.8 1.3 collective-permute-start
  161.4 0.1 reshape.135
  161.6 0.9 fusion.65
  162.6 0.9 pad_maximum_fusion
  163.9 3.5 %collective-permute-done = f32[32,512]{1,0:T(8,128)S(1)} collective-permute-done((f32[32,512]{1,0:T(8,128)S(1)}, f32[32,512]{1,0:T(8,128)S(1)}, u32[]{:S(2)}, u32[]{:S(2)}) %collective-permute-start) | collective-permute-done | bytes 65568 | tf_op jit(solution)/shard_map/ppermute | solution.py:581
  167.4 1.0 maximum_select_fusion
  168.8 0.6 reshape.132
  169.4 0.6 add.122
  170.0 0.6 pad_maximum_fusion.4
  (100 shorter events, 3.0 us)
Async XLA Ops:
  7.4 21.5 %all-to-all-start = ((bf16[16,40,512]{2,1,0:T(8,128)(2,1)}), bf16[16,40,512]{2,1,0:T(8,128)(2,1)S(1)}, u32[]{:S(2)}, u32[]{:S(2)}) async-start(bf16[16,40,512]{2,1,0:T(8,128)(2,1)} %broadcast_in_dim.44), calls=%async_computation | async-start | bytes 1310720 | tf_op jit(solution)/shard_map/all_to_all | solution.py:53
  31.4 45.0 %copy-start.4 = (f32[1,6,512]{2,0,1:T(1,128)S(1)}, f32[1,6,512]{2,0,1:T(1,128)}, u32[]{:S(2)}) copy-start(f32[1,6,512]{2,0,1:T(1,128)} %param.10) | copy-start | bytes 36868
  31.4 17.1 %all-to-all-start.1 = ((bf16[8,88,512]{2,1,0:T(8,128)(2,1)}), bf16[8,88,512]{2,1,0:T(8,128)(2,1)S(1)}, u32[]{:S(2)}, u32[]{:S(2)}) async-start(bf16[8,88,512]{2,1,0:T(8,128)(2,1)} %broadcast_in_dim.45), calls=%async_computation.1 | async-start | bytes 1441792 | tf_op jit(solution)/shard_map/all_to_all | solution.py:53
  37.0 40.1 %copy-start.1 = (bf16[3,16,8,512]{3,2,1,0:T(8,128)(2,1)S(1)}, bf16[3,16,8,512]{3,2,1,0:T(8,128)(2,1)}, u32[]{:S(2)}) copy-start(bf16[3,16,8,512]{3,2,1,0:T(8,128)(2,1)} %copy.65) | copy-start | bytes 1179652
  49.3 29.4 %copy-start = (bf16[8,8,8,512]{3,2,0,1:T(8,128)(2,1)S(1)}, bf16[8,8,8,512]{3,2,0,1:T(8,128)(2,1)}, u32[]{:S(2)}) copy-start(bf16[8,8,8,512]{3,2,0,1:T(8,128)(2,1)} %copy.64) | copy-start | bytes 1572868
  72.9 13.7 %all-to-all-start.2 = ((f32[8,32,512]{2,1,0:T(8,128)}), f32[8,32,512]{2,1,0:T(8,128)S(1)}, u32[]{:S(2)}, u32[]{:S(2)}) async-start(f32[8,32,512]{2,1,0:T(8,128)} %get-tuple-element.18), calls=%async_computation.2 | async-start | bytes 1048576 | tf_op jit(solution)/shard_map/all_to_all | solution.py:53
  86.5 0.8 copy-start.2
  113.0 29.4 %copy-start.6 = (f32[1,3,512]{2,1,0:T(4,128)S(1)}, f32[1,3,512]{2,1,0:T(4,128)}, u32[]{:S(2)}) copy-start(f32[1,3,512]{2,1,0:T(4,128)} %get-tuple-element.50) | copy-start | bytes 18436
  113.0 40.3 %copy-start.3 = (f32[512,3]{0,1:T(4,128)S(1)}, f32[512,3]{0,1:T(4,128)}, u32[]{:S(2)}) copy-start(f32[512,3]{0,1:T(4,128)} %param.13) | copy-start | bytes 18436
  113.0 48.6 %copy-start.5 = (f32[6,512]{1,0:T(8,128)S(1)}, f32[6,512]{1,0:T(8,128)}, u32[]{:S(2)}) copy-start(f32[6,512]{1,0:T(8,128)} %param.18) | copy-start | bytes 36868
  113.0 22.7 %all-to-all-start.3 = ((bf16[16,64,512]{2,1,0:T(8,128)(2,1)}), bf16[16,64,512]{2,1,0:T(8,128)(2,1)S(1)}, u32[]{:S(2)}, u32[]{:S(2)}) async-start(bf16[16,64,512]{2,1,0:T(8,128)(2,1)} %get-tuple-element.28), calls=%async_computation.3 | async-start | bytes 2097152 | tf_op jit(solution)/shard_map/all_to_all | solution.py:53
  138.8 14.4 %all-to-all-start.4 = ((bf16[8,72,512]{2,1,0:T(8,128)(2,1)}), bf16[8,72,512]{2,1,0:T(8,128)(2,1)S(1)}, u32[]{:S(2)}, u32[]{:S(2)}) async-start(bf16[8,72,512]{2,1,0:T(8,128)(2,1)} %broadcast_in_dim.50), calls=%async_computation.4 | async-start | bytes 1179648 | tf_op jit(solution)/shard_map/all_to_all | solution.py:53
  155.1 13.2 %all-to-all-start.5 = ((f32[16,24,128]{2,1,0:T(8,128)}), f32[16,24,128]{2,1,0:T(8,128)S(1)}, u32[]{:S(2)}, u32[]{:S(2)}) async-start(f32[16,24,128]{2,1,0:T(8,128)} %broadcast_in_dim.51), calls=%async_computation.5 | async-start | bytes 393216 | tf_op jit(solution)/shard_map/all_to_all | solution.py:53
  159.8 7.5 %collective-permute-start = (f32[32,512]{1,0:T(8,128)S(1)}, f32[32,512]{1,0:T(8,128)S(1)}, u32[]{:S(2)}, u32[]{:S(2)}) collective-permute-start(f32[32,512]{1,0:T(8,128)S(1)} %convert_reduce_fusion.1), channel_id=1, source_target_pairs={{64,0},{72,8},{80,16},{88,24},{96,32},{104,40},{112,48},{120,56},{... | collective-permute-start | bytes 196616 | tf_op jit(solution)/shard_map/ppermute | solution.py:581

commit v2 on v1

--- a/solution.py
+++ b/solution.py
@@ -63,6 +63,16 @@
     return pltpu.roll(x, x.shape[1] - start, 1)[:, :width]
 
 
+def steps_apart(shape):
+    return (
+        lax.broadcasted_iota(jnp.int32, shape, 0) - lax.broadcasted_iota(jnp.int32, shape, 1)
+    ).astype(f32)
+
+
+def one_hot(apart, target):
+    return jnp.where(apart == target, 1.0, 0.0).astype(bf16)
+
+
 def valid_row(c, width, length):
     at = lax.broadcasted_iota(jnp.int32, (1, width), 1) + c * width
     return (at < length).astype(f32)
@@ -70,9 +80,9 @@
 
 def forward_kernel(
     dil0, dil1, half,
-    info, fields, a_cat, w_cat, mix, w_taps, bias1, e_pair,
-    g0_out, du0_out, dv0_out, h1_out, s_out, gown_out, du1_out, dv1_out, packet,
-    fpad, s_cat, prod, g_keep,
+    info, fields, a_cat, w_hi, w_lo, mix, w_taps, bias1, e_pair,
+    g0_out, du0_out, dv0_out, s_out, gown_out, du1_out, dv1_out, packet,
+    fpad, s_cat, prod, centre, pre_s, g_keep, w_mix, w_start,
 ):
     i = pl.program_id(0)
     nb = fields.shape[0]
@@ -88,13 +98,18 @@
     def _():
         fpad[:, 0:pad0] = jnp.zeros((8, pad0), f32)
         fpad[:, pad0 + nb * bw :] = jnp.zeros((8, pad0), f32)
-        prod[:, 0:pad1] = jnp.zeros((prod.shape[0], pad1), f32)
-        prod[:, pad1 + nb * bw :] = jnp.zeros((prod.shape[0], pad1), f32)
+        prod[:, 0:pad1] = jnp.zeros((prod.shape[0], pad1), bf16)
+        prod[:, pad1 + nb * bw :] = jnp.zeros((prod.shape[0], pad1), bf16)
+        w_mix[...] = dot(w_taps[...], mix[...]).astype(bf16)
+        full = dot(w_taps[...], w_hi[...]) + dot(w_taps[...], w_lo[...])
+        top = full.astype(bf16).astype(f32)
+        col = lax.broadcasted_iota(jnp.int32, full.shape, 1)
+        w_start[...] = jnp.where(col < 18, top, full - top).astype(bf16)
         s_cat[...] = jnp.zeros(s_cat.shape, f32)
         s_cat[27:29, :] = jnp.ones((2, bw), f32)
         packet[:, 24:32, :] = jnp.zeros((nb, 8, bw), f32)
         for c in range(nb):
-            block = fields[c].astype(f32)
+            block = fields[c ^ k].astype(f32)
             valid = valid_row(c, bw, length)
             at = slice(pad0 + c * bw, pad0 + (c + 1) * bw)
             fpad[0:half, at] = block[0:half] * valid
@@ -126,31 +141,40 @@
         t = jnp.tanh(u)
         s = 0.5 * jnp.tanh(0.5 * v) + 0.5
         g = t * s
-        g0_out[r : r + step_rows, :] = g.astype(bf16)
+        g0_out[r : r + step_rows, :] = (g * valid).astype(bf16)
         du0_out[r : r + step_rows, :] = (s - g * t).astype(bf16)
         dv0_out[r : r + step_rows, :] = (g - g * s).astype(bf16)
-    h1 = dot(mix[...], g0_out[...]) + dot(w_cat[...], s_b)
-    h1 = (h1 * valid).astype(bf16)
-    h1_out[...] = h1
-    prod[:, pl.ds(pl.multiple_of(pad1 + base, 128), bw)] = dot(w_taps[...], h1)
+    pair = 2 * rows
+    g_b = g0_out[...]
+    for tap in range(3):
+        at = slice(tap * pair, (tap + 1) * pair)
+        part = dot(w_mix[at, :], g_b) + dot(w_start[at, :], s_b)
+        if tap == 1:
+            centre[:, pl.ds(base, bw)] = part
+        else:
+            to = tap // 2 * pair
+            cols = pl.ds(pl.multiple_of(pad1 + base, 128), bw)
+            prod[to : to + pair, cols] = part.astype(bf16)
     g_keep[:, pl.ds(base, bw)] = g0_out[pl.ds(pl.multiple_of(rows * k, rows), rows), :]
 
     @pl.when(i == nb - 1)
     def _():
+        apart = steps_apart((256, 128))
+
         def body(c, carry):
             base = pl.multiple_of(c * bw, bw)
             off = fpad[6:7, pl.ds(pl.multiple_of(pad0 + base, 128), bw)]
-            pair = 2 * rows
-            window = bw + 128
-            behind = prod[0:pair, pl.ds(pl.multiple_of(base, 128), window)]
-            ahead = prod[2 * pair :, pl.ds(pl.multiple_of(pad1 + dil1 + base, 128), window)]
-            left = rolled(behind, 128, bw)
-            right = rolled(ahead, 0, bw)
-            for step in range(1, BUCKETS):
-                left = jnp.where(off == step, rolled(behind, 128 - step, bw), left)
-                right = jnp.where(off == step, rolled(ahead, step, bw), right)
-            centre = prod[pair : 2 * pair, pl.ds(pl.multiple_of(pad1 + base, 128), bw)]
-            pre = left + centre + right + bias1[...]
+            for tile in range(bw // 128):
+                lane = slice(tile * 128, (tile + 1) * 128)
+                behind = prod[0:pair, pl.ds(pl.multiple_of(base + tile * 128, 128), 256)]
+                ahead = prod[
+                    pair:,
+                    pl.ds(pl.multiple_of(pad1 + dil1 + base + tile * 128, 128), 256),
+                ]
+                pre_s[:, lane] = dot(behind, one_hot(apart, 128.0 - off[:, lane])) + dot(
+                    ahead, one_hot(apart, off[:, lane])
+                )
+            pre = pre_s[...] + centre[:, pl.ds(base, bw)] + bias1[...]
             t = jnp.tanh(pre[:rows])
             s = 0.5 * jnp.tanh(0.5 * pre[rows:]) + 0.5
             g = t * s
@@ -171,18 +195,18 @@
 
 def backward_kernel(
     dil1, half,
-    info, got, fields, flux, e_up, gown, du1, dv1, w_taps_t, mix_t,
-    g0, du0, dv0, h1, s_in,
+    info, got, fields, flux, e_up, gown, du1, dv1, w_taps, w_taps_t, mix, w_mix_t, w_start,
+    g0, du0, dv0, s_in,
     coupled, packet,
-    ends, d_cat, dz_pad, off_pad, d_e0, d_taps, acc_conv, acc_mix, acc_m, acc_s, acc_g, acc_b,
-    dg, m_rows, share,
+    ends, d_cat, dz_pad, off_pad, d_e0, d_taps, acc_q, acc_mix, acc_m, acc_s, acc_g, acc_b,
+    dg, m_rows, share, acc_conv, small,
 ):
     i = pl.program_id(0)
     nb = fields.shape[0]
     bw = fields.shape[2]
     pair = gown.shape[0]
     rows = pair // 2
-    channels = mix_t.shape[0]
+    channels = mix.shape[0]
     n_dp = packet.shape[0]
     pad1 = dil1 + 128
     length = info[0]
@@ -190,10 +214,10 @@
 
     @pl.when(i == 0)
     def _():
-        for ref in (acc_conv, acc_mix, acc_m, acc_s, acc_g, acc_b, d_cat, m_rows, share):
+        for ref in (acc_q, acc_m, acc_s, acc_g, acc_b, d_cat, m_rows, share, small):
             ref[...] = jnp.zeros(ref.shape, f32)
-        dz_pad[:, 0:pad1] = jnp.zeros((pair, pad1), f32)
-        dz_pad[:, pad1 + nb * bw :] = jnp.zeros((pair, pad1), f32)
+        dz_pad[:, 0:pad1] = jnp.zeros((pair, pad1), bf16)
+        dz_pad[:, pad1 + nb * bw :] = jnp.zeros((pair, pad1), bf16)
         off_pad[:, 0:pad1] = jnp.full((8, pad1), -1.0, f32)
         off_pad[:, pad1 + nb * bw :] = jnp.full((8, pad1), -1.0, f32)
         total = got[0]
@@ -210,7 +234,7 @@
         def first(c, carry):
             base = pl.multiple_of(c * bw, bw)
             at = pl.multiple_of(pad1 + base, 128)
-            block = fields[c].astype(f32)
+            block = fields[c ^ k].astype(f32)
             valid = valid_row(c, bw, length)
             off_pad[0:1, pl.ds(at, bw)] = block[6 * half : 6 * half + 1]
             flux2 = block[half : 2 * half] + block[3 * half : 4 * half]
@@ -228,28 +252,29 @@
             acc_g[...] += nt(d_cat[8:24, :].astype(bf16), gown[:, pl.ds(base, bw)])
             d_e0[:, pl.ds(base, bw)] = d_gated[:rows]
             up = d_gated[rows : 2 * rows]
-            dz_pad[0:rows, pl.ds(at, bw)] = up * du1[:, pl.ds(base, bw)]
-            dz_pad[rows:, pl.ds(at, bw)] = up * dv1[:, pl.ds(base, bw)]
+            dz_pad[0:rows, pl.ds(at, bw)] = (up * du1[:, pl.ds(base, bw)]).astype(bf16)
+            dz_pad[rows:, pl.ds(at, bw)] = (up * dv1[:, pl.ds(base, bw)]).astype(bf16)
             return carry
 
         lax.fori_loop(0, nb, first, 0)
+
+        apart = steps_apart((128, 256))
 
         def second(c, carry):
             base = pl.multiple_of(c * bw, bw)
-            window = bw + 128
-            ahead = dz_pad[:, pl.ds(pl.multiple_of(pad1 + dil1 + base, 128), window)]
-            off_a = off_pad[0:1, pl.ds(pl.multiple_of(pad1 + dil1 + base, 128), window)]
-            behind = dz_pad[:, pl.ds(base, window)]
-            off_b = off_pad[0:1, pl.ds(base, window)]
-            left = 0.0
-            right = 0.0
-            for step in range(BUCKETS):
-                left = left + rolled(jnp.where(off_a == step, ahead, 0.0), step, bw)
-                right = right + rolled(jnp.where(off_b == step, behind, 0.0), 128 - step, bw)
-            centre = dz_pad[:, pl.ds(pl.multiple_of(pad1 + base, 128), bw)].astype(bf16)
-            d_taps[0:pair, pl.ds(base, bw)] = left.astype(bf16)
+            valid = valid_row(c, bw, length)
+            for tile in range(bw // 128):
+                lane = pl.ds(pl.multiple_of(base + tile * 128, 128), 128)
+                late = pl.ds(pl.multiple_of(pad1 + dil1 + base + tile * 128, 128), 256)
+                early = pl.ds(pl.multiple_of(base + tile * 128, 128), 256)
+                left = nt(dz_pad[:, late], one_hot(apart, -off_pad[0:1, late]))
+                right = nt(dz_pad[:, early], one_hot(apart, off_pad[0:1, early] - 128.0))
+                d_taps[0:pair, lane] = left.astype(bf16)
+                d_taps[2 * pair :, lane] = (
+                    right * valid[:, tile * 128 : (tile + 1) * 128]
+                ).astype(bf16)
+            centre = dz_pad[:, pl.ds(pl.multiple_of(pad1 + base, 128), bw)]
             d_taps[pair : 2 * pair, pl.ds(base, bw)] = centre
-            d_taps[2 * pair :, pl.ds(base, bw)] = right.astype(bf16)
             acc_b[...] += nt(jnp.ones((16, bw), bf16), centre)
             return carry
 
@@ -257,12 +282,10 @@
 
     base = pl.multiple_of(i * bw, bw)
     d_blk = d_taps[:, pl.ds(base, bw)]
-    acc_conv[...] += nt(d_blk, h1[...])
-    field = (dot(w_taps_t[...], d_blk) * valid_row(i, bw, length)).astype(bf16)
     s_b = s_in[...]
-    acc_mix[...] += nt(field, g0[...])
-    acc_s[...] += nt(s_b, field)
-    dg[...] = dot(mix_t[...], field)
+    acc_q[...] += nt(d_blk, g0[...])
+    acc_s[...] += nt(s_b, d_blk)
+    dg[...] = dot(w_mix_t[...], d_blk)
     own = pl.ds(pl.multiple_of(rows * k, rows), rows)
     dg[own, :] = dg[own, :] + d_e0[:, pl.ds(base, bw)]
     up = dg[...]
@@ -273,10 +296,24 @@
     def _():
         per_mix = channels // n_dp
         eighth = pair // n_dp
+        q = acc_q[...]
+        q_hi = q.astype(bf16)
+        q_lo = (q - q_hi.astype(f32)).astype(bf16)
+        small[0:half, :] = acc_s[3 : 3 + half, :] + acc_s[12 : 12 + half, :]
+        seen = small[0:8, :]
+        seen_hi = seen.astype(bf16).astype(f32)
+        small[8:16, :] = seen - seen_hi
+        small[16:24, :] = seen
+        d_start = small[...].astype(bf16)
+        acc_conv[...] = nt(q_hi, mix[...]) + nt(q_lo, mix[...]) + dot(d_start, w_start[...], 0, 0)
+        acc_mix[...] = dot(w_taps_t[...], q_hi) + dot(w_taps_t[...], q_lo)
+        starts = dot(d_start, w_taps[...])
+        starts = starts[0:half] + starts[8 : 8 + half]
         m_rows[0:9, :] = acc_m[0:9, :] + acc_m[9:18, :]
         m_rows[9:10, :] = acc_m[27:28, :]
-        starts = acc_s[3 : 3 + half, :] + acc_s[12 : 12 + half, :]
-        share[0:1, 0:128] = acc_b[0:1, :]
+        bias = acc_b[0:1, :]
+        share[0:1, 0:128] = bias
+        share[6:7, 128:256] = bias - bias.astype(bf16).astype(f32)
         share[0 : 2 * half, 128:256] = acc_g[8 : 8 + 2 * half, :] + acc_g[0 : 2 * half, :]
         for j in range(n_dp):
             row = 64 * (j % (n_dp // 2)) + per_mix * (j // (n_dp // 2))
@@ -292,10 +329,13 @@
             at = per_mix + 3 * eighth
             cols = slice(128 * (j // 2), 128 * (j // 2) + 128)
             share[6:8, 0:128] = m_rows[8:10, cols]
+            low = m_rows[0:10, cols]
+            low = low - low.astype(bf16).astype(f32)
+            share[4:6, 0:128] = low[8:10]
             packet[j, at : at + 8, 0:128] = m_rows[0:8, cols].astype(bf16)
             packet[j, at : at + 8, 128:256] = share[:, 0:128].astype(bf16)
             packet[j, at : at + 8, 256:384] = share[:, 128:256].astype(bf16)
-            packet[j, at : at + 8, 384:512] = jnp.zeros((8, 128), bf16)
+            packet[j, at : at + 8, 384:512] = low[0:8].astype(bf16)
 
 
 def whole(shape):
@@ -352,6 +392,17 @@
     n_pad = -(-n_in // 8) * 8
     inputs = pad_to(inputs, n_pad, shard_len)
 
+    fields = inputs[None]
+    while fields.shape[0] < n_ctx:
+        hop = fields.shape[0]
+        other = lax.ppermute(fields, "ctx", [(c, c ^ hop) for c in range(n_ctx)])
+        fields = jnp.concatenate([fields, other], axis=0)
+    half_rows = rows // 2
+    mix_far = lax.ppermute(
+        mix_first[half_rows:], "dp", [(i, i + half_dp) for i in range(half_dp)]
+    )
+    mix_send = jnp.where(low, mix_first[:half_rows], mix_far)
+
     sw_hi, sw_lo = split(start_weight)
     sw_pair = jnp.concatenate([sw_hi, sw_lo], axis=1)
     a_rows = []
@@ -381,9 +432,8 @@
         axis=1,
     )
     conv_k = lax.dynamic_slice(conv1, (part * k, 0), (part, 3 * channels))
-    mix_k = lax.dynamic_slice(mix_first, (part * k, 0), (part, channels))
     packet = jnp.concatenate(
-        [conv_k[:, tap * channels : (tap + 1) * channels] for tap in range(3)] + [mix_k, small],
+        [conv_k[:, tap * channels : (tap + 1) * channels] for tap in range(3)] + [small, mix_send],
         axis=0,
     )
     per = packet.shape[0]
@@ -392,17 +442,11 @@
     ).reshape(n_dp, per, channels)
     w_taps = got[:, : 3 * part].reshape(n_dp, 3, part, channels).transpose(1, 0, 2, 3)
     w_taps = w_taps.reshape(6 * rows, channels)
-    mix_part = got[:half_dp, 3 * part : 4 * part].reshape(rows, channels)
-    both = jnp.concatenate([inputs, mix_part], axis=0)
-    ctx_got = exchange(
-        jnp.broadcast_to(both[None], (n_ctx,) + both.shape).reshape(-1, channels), "ctx"
-    ).reshape((n_ctx,) + both.shape)
-    fields = ctx_got[:, :n_pad]
-    mix_res = ctx_got[:, n_pad:].reshape(n_ctx, half_dp, part, channels).transpose(1, 0, 2, 3)
+    mix_res = got[:, 4 * part :].reshape(2, half_dp, half_rows, channels).transpose(1, 0, 2, 3)
     mix_res = mix_res.reshape(channels, channels)
-    e_k = got[:, 4 * part : 4 * part + n_e, : 4 * rows].astype(f32).sum(axis=0)
+    e_k = got[:, 3 * part : 3 * part + n_e, : 4 * rows].astype(f32).sum(axis=0)
     e_cat = e_k[:, : 2 * rows] + e_k[:, 2 * rows :]
-    a_all = got[:, 4 * part : 4 * part + 5, 4 * rows :].reshape(n_dp, 20, rows)
+    a_all = got[:, 3 * part : 3 * part + 5, 4 * rows :].reshape(n_dp, 20, rows)
     a_all = a_all[:, :18].transpose(1, 0, 2).reshape(18, n_dp * rows)
     a_hi, a_lo = a_all[:9], a_all[9:]
 
@@ -411,10 +455,14 @@
     a_cat = jnp.concatenate(
         [a_hi, a_hi, a_lo, b_hi, b_lo, jnp.zeros((3, 2 * channels), bf16)], axis=0
     ).T
-    gap = jnp.zeros((6, channels), bf16)
-    w_cat = jnp.concatenate(
-        [gap[:3], sw_hi.T, gap, sw_hi.T, gap, sw_lo.T, gap[:3], gap[:5]], axis=0
-    ).T
+    w_hi, w_lo = (
+        jnp.concatenate([jnp.pad(x, ((0, 0), (3, 6 - half)))] * 3 + [jnp.zeros((channels, 5), bf16)], axis=1)
+        for x in (sw_hi, sw_lo)
+    )
+    gap = jnp.zeros((8 - half, channels), bf16)
+    w_start = jnp.concatenate(
+        [sw_hi.T, gap, sw_hi.T, gap, sw_lo.T, gap, jnp.zeros((8, channels), bf16)], axis=0
+    )
     ec_hi, ec_lo = split(e_cat)
     gap = jnp.zeros((2, 2 * rows), bf16)
     e_pair = jnp.concatenate([ec_hi, gap, ec_lo, gap], axis=0)
@@ -435,29 +483,34 @@
             smem,
             whole((n_ctx, n_pad, shard_len)),
             whole(a_cat.shape),
-            whole(w_cat.shape),
+            whole(w_hi.shape),
+            whole(w_lo.shape),
             whole(mix_res.shape),
             whole(w_taps.shape),
             whole(bias1.shape),
             whole(e_pair.shape),
         ],
-        out_specs=[columns(channels, shard_len)] * 4
+        out_specs=[columns(channels, shard_len)] * 3
         + [columns(32, shard_len), whole((pair, epochs)), whole((rows, epochs)),
            whole((rows, epochs)), whole((n_ctx, 32, shard_len))],
-        out_shape=[shapes((channels, epochs), bf16)] * 4
+        out_shape=[shapes((channels, epochs), bf16)] * 3
         + [shapes((32, epochs), bf16), shapes((pair, epochs), bf16), shapes((rows, epochs), f32),
            shapes((rows, epochs), f32), shapes((n_ctx, 32, shard_len), f32)],
         scratch_shapes=[
             pltpu.VMEM((8, epochs + 512), f32),
             pltpu.VMEM((32, shard_len), f32),
-            pltpu.VMEM((3 * pair, wide), f32),
+            pltpu.VMEM((2 * pair, wide), bf16),
+            pltpu.VMEM((pair, epochs), f32),
+            pltpu.VMEM((pair, shard_len), f32),
             pltpu.VMEM((rows, epochs), bf16),
+            pltpu.VMEM((3 * pair, channels), bf16),
+            pltpu.VMEM((3 * pair, 32), bf16),
         ],
         compiler_params=params,
         name="layers_forward",
     )
-    g0, du0, dv0, h1, s_all, g_own, du1, dv1, packed = forward(
-        info, fields, a_cat, w_cat, mix_res, w_taps, bias1, e_pair
+    g0, du0, dv0, s_all, g_own, du1, dv1, packed = forward(
+        info, fields, a_cat, w_hi, w_lo, mix_res, w_taps, bias1, e_pair
     )
     got = exchange(packed.reshape(n_ctx * 32, shard_len), "ctx").reshape(n_ctx, 32, shard_len)
 
@@ -476,48 +529,55 @@
             whole((pair, epochs)),
             whole((rows, epochs)),
             whole((rows, epochs)),
+            whole((3 * pair, channels)),
             whole((channels, 3 * pair)),
             whole((channels, channels)),
+            whole((channels, 3 * pair)),
+            whole((32, channels)),
         ]
-        + [columns(channels, shard_len)] * 4
+        + [columns(channels, shard_len)] * 3
         + [columns(32, shard_len)],
         out_specs=[whole((1, half, shard_len)), whole((n_dp, per, channels))],
         out_shape=[shapes((1, half, shard_len), f32), shapes((n_dp, per, channels), bf16)],
         scratch_shapes=[
             pltpu.VMEM((32, shard_len), f32),
             pltpu.VMEM((32, shard_len), f32),
-            pltpu.VMEM((pair, wide), f32),
+            pltpu.VMEM((pair, wide), bf16),
             pltpu.VMEM((8, wide), f32),
             pltpu.VMEM((rows, epochs), f32),
             pltpu.VMEM((3 * pair, epochs), bf16),
             pltpu.VMEM((3 * pair, channels), f32),
             pltpu.VMEM((channels, channels), f32),
             pltpu.VMEM((32, 2 * channels), f32),
-            pltpu.VMEM((32, channels), f32),
+            pltpu.VMEM((32, 3 * pair), f32),
             pltpu.VMEM((16, pair), f32),
             pltpu.VMEM((16, pair), f32),
             pltpu.VMEM((channels, shard_len), f32),
             pltpu.VMEM((16, 2 * channels), f32),
             pltpu.VMEM((8, 256), f32),
+            pltpu.VMEM((3 * pair, channels), f32),
+            pltpu.VMEM((32, 3 * pair), f32),
         ],
         compiler_params=params,
         name="layers_backward",
     )
     coupled, packed = backward(
-        info, got, fields, light_flux[0], e_up, g_own, du1, dv1, w_taps.T, mix_res.T,
-        g0, du0, dv0, h1, s_all,
+        info, got, fields, light_flux[0], e_up, g_own, du1, dv1, w_taps, w_taps.T, mix_res,
+        dot(mix_res, w_taps, 0, 1).astype(bf16), w_start, g0, du0, dv0, s_all,
     )
     got = exchange(packed.reshape(n_dp * per, channels), "dp").reshape(n_dp, per, channels)
     got = got.astype(f32).sum(axis=0)
     mix_piece = got[:n_mix]
     conv_piece = got[n_mix : n_mix + n_conv].astype(bf16)
     smalls = got[n_mix + n_conv :]
-    near = lax.dynamic_slice(smalls, (0, rows * (dp % 2)), (8, rows))
-    far = lax.dynamic_slice(smalls, (6, 128 + rows * (dp % 2)), (2, rows))
-    m_own = jnp.concatenate([near, far], axis=0)
+    m_first = smalls[:, :128] + smalls[:, 384:]
+    m_rest = smalls[4:6, 128:256] + smalls[6:8, 128:256]
+    m_own = lax.dynamic_slice(
+        jnp.concatenate([m_first, m_rest], axis=0), (0, rows * (dp % 2)), (10, rows)
+    )
     start_own = jnp.where(dp < channels // 128, smalls[1 : 1 + half, 128:256], 0.0)
     g_own_sum = smalls[: 2 * half, 256:384]
-    bias1_own = smalls[0:1, 128:256]
+    bias1_own = smalls[0:1, 128:256] + smalls[6:7, 256:384]
     mo_hi, mo_lo = split(m_own)
     mo_pair = jnp.concatenate([mo_hi[:9], mo_lo[:9]], axis=0)
     start_t = 0.0
@@ -540,11 +600,14 @@
         axis=1,
     )
     width = parts.shape[1]
+    parts_hi, parts_lo = split(parts)
+    start_hi, start_lo = split(start_t)
     pack_rows = [
         conv_piece,
         mix_piece.astype(bf16),
-        pad_to(parts, 10, channels).astype(bf16),
-        start_t.astype(bf16),
+        pad_to(jnp.concatenate([parts_hi, parts_lo[:, : 3 * rows]], axis=1), 10, channels),
+        start_hi,
+        start_lo,
     ]
     packed = jnp.concatenate(pack_rows, axis=0)
     per0 = packed.shape[0]
@@ -557,8 +620,13 @@
     grad_conv1 = grad_conv1.reshape(rows, 3 * channels).astype(f32)
     mix_rows = got[:, n_conv : n_conv + n_mix].astype(f32).sum(axis=0)
     base = n_conv + n_mix
-    parts = got[:, base : base + 10, :width].astype(f32)
-    start_t = got[:, base + 10 : base + 10 + half].astype(f32).sum(axis=0)
+    parts = got[:, base : base + 10].astype(f32)
+    parts_lo = parts[:, :, width : width + 3 * rows]
+    parts = jnp.concatenate(
+        [parts[:, :, : 3 * rows] + parts_lo, parts[:, :, 3 * rows : width]], axis=2
+    )
+    start_t = got[:, base + 10 : base + 10 + 2 * half].astype(f32).sum(axis=0)
+    start_t = start_t[:half] + start_t[half:]
     m_own = parts[:, :, :rows].sum(axis=0)
     g_all = parts[:, : 2 * half, rows : 3 * rows]
     g0_all = g_all[:, :, :rows].transpose(1, 0, 2).reshape(2 * half, channels)

time: 172 us -> 158 us (0.919)
  waiting for transfers between devices: 54.6 us -> 41.2 us
  Pallas kernels: 48.5 us -> 38.7 us
  starting transfers between devices: 32.4 us -> 36.8 us
  matrix products: 6.6 us -> 8.93 us
    all_to_all x6 -> x5, waiting for transfers between devices: 51.1 us -> 29.5 us  [exchange(): return lax.all_to_all(x, axis, 0, 0, tiled=True)]
    ppermute x0 -> x4, starting transfers between devices: none -> 10.6 us  [the longest x1 5.47 us: local(): lax.ppermute(mix_first[half_rows:], 'dp', [(i, i + half_dp) for i in rang...]
    pallas_call x2, Pallas kernels: 48.5 us -> 38.7 us  [the longest x1 20.3 us: local(): backward(info, got, fields, light_flux[0], e_up, g_own, du1, dv1, w_taps,...]
    ppermute x0 -> x4, waiting for transfers between devices: none -> 8.14 us  [the longest x3 8.14 us: local(): other = lax.ppermute(fields, 'ctx', [(c, c ^ hop) for c in range(n_ctx)])]
    all_to_all x6 -> x5, starting transfers between devices: 31.1 us -> 24.9 us  [exchange(): return lax.all_to_all(x, axis, 0, 0, tiled=True)]
    concatenate x2 -> x5, local copies, waits for them, and re-layouts: 1.04 us -> 4.08 us  [the longest x1 2.46 us: local(): jnp.concatenate([sw_hi.T, gap, sw_hi.T, gap, sw_lo.T, gap, jnp.zeros((8,...]
    dot_general x15 -> x16, matrix products: 6.6 us -> 8.93 us  [dot(): lax.dot_general(a, b, (((ca,), (cb,)), ((), ())), precision=precision, pr...]
    reshape x5 -> x1, local copies, waits for them, and re-layouts: 2.02 us -> 0.12 us  [local(): a_all = got[:, 3 * part:3 * part + 5, 4 * rows:].reshape(n_dp, 20, rows)]
  transfers between devices with their start and end apart: 7 -> 10, of which waited for: 6 -> 6; matrix products, arithmetic and copies ran while one was open for 9% -> 15% of each run, Pallas kernels for 0% -> 0%
where the time goes in v2:
time: 158 us; the launch traced here: 157 us
  waiting for transfers between devices  41.2 us (26%)
  Pallas kernels  38.7 us (24%)
  starting transfers between devices  36.8 us (23%)
  local copies, waits for them, and re-layouts  20.4 us (13%)
  matrix products  8.93 us (6%)
  other arithmetic  8.88 us (6%)
  between operations  1.88 us (1%)
    all_to_all x5, waiting for transfers between devices, exchange(): return lax.all_to_all(x, axis, 0, 0, tiled=True)  29.5 us
    all_to_all x5, starting transfers between devices, exchange(): return lax.all_to_all(x, axis, 0, 0, tiled=True)  24.9 us
    pallas_call x1, Pallas kernels, local(): backward(info, got, fields, light_flux[0], e_up, g_own, du1, dv1, w_taps,...  20.3 us
    pallas_call x1, Pallas kernels, local(): forward(info, fields, a_cat, w_hi, w_lo, mix_res, w_taps, bias1, e_pair)  18.3 us
    dot_general x16, matrix products, dot(): lax.dot_general(a, b, (((ca,), (cb,)), ((), ())), precision=precision, pr...  8.93 us
    ppermute x3, waiting for transfers between devices, local(): other = lax.ppermute(fields, 'ctx', [(c, c ^ hop) for c in range(n_ctx)])  8.14 us
    ppermute x1, starting transfers between devices, local(): lax.ppermute(mix_first[half_rows:], 'dp', [(i, i + half_dp) for i in rang...  5.47 us
    ppermute x3, starting transfers between devices, local(): other = lax.ppermute(fields, 'ctx', [(c, c ^ hop) for c in range(n_ctx)])  5.13 us
  transfers between devices with their start and end apart: 10, of which 6 were waited for; matrix products, arithmetic and copies ran while one was open for 15% of the time, Pallas kernels for 0%

profile of v2, /device:TPU:1, one launch (start us, length us, event | category | flops | bytes accessed | tf_op | source)
XLA Modules:
  0.0 156.8 jit_solution(16971105812989414622)
XLA Ops:
  0.6 0.8 slice.255
  1.4 5.5 %collective-permute-start.3 = (bf16[32,512]{1,0:T(8,128)(2,1)S(1)}, bf16[32,512]{1,0:T(8,128)(2,1)S(1)}, u32[]{:S(2)}, u32[]{:S(2)}) collective-permute-start(bf16[32,512]{1,0:T(8,128)(2,1)S(1)} %slice.255), channel_id=1, source_target_pairs={{0,64},{8,72},{16,80},{24,88},{32,96},{40,104},{48,112},{56,120},{... | collective-permute-start | bytes 98312 | tf_op jit(solution)/shard_map/ppermute | solution.py:401
  6.9 1.1 slice_bitcast_fusion.2
  8.0 0.7 reduce-precision_convert_fusion.3
  8.9 0.1 fusion.11
  9.0 0.9 copy.57
  10.1 0.7 fusion.15
  10.8 0.7 fusion.31
  11.5 0.9 fusion.26
  12.4 0.9 fusion.20
  13.4 0.7 convert_element_type.133
  14.1 0.2 concatenate.83
  14.3 0.8 select_dynamic-update-slice_fusion
  15.1 1.1 broadcast_in_dim.45
  16.2 6.1 %all-to-all-start = ((bf16[16,64,512]{2,1,0:T(8,128)(2,1)}), bf16[16,64,512]{2,1,0:T(8,128)(2,1)S(1)}, u32[]{:S(2)}, u32[]{:S(2)}) async-start(bf16[16,64,512]{2,1,0:T(8,128)(2,1)} %broadcast_in_dim.45), calls=%async_computation | async-start | bytes 2097152 | tf_op jit(solution)/shard_map/all_to_all | solution.py:53
  22.4 1.4 collective-permute-start
  23.9 1.2 collective-permute-done
  25.1 2.9 %collective-permute-start.1 = (bf16[2,24,512]{2,1,0:T(8,128)(2,1)S(1)}, bf16[2,24,512]{2,1,0:T(8,128)(2,1)S(1)}, u32[]{:S(2)}, u32[]{:S(2)}) collective-permute-start(bf16[2,24,512]{2,1,0:T(8,128)(2,1)S(1)} %pad_maximum_fusion.3), channel_id=1, source_target_pairs={{0,2},{1,3},{2,0},{3,1},{4,6},{5,7},{6,4},{7,5},{8,10},{9,11},{10,... | collective-permute-start | bytes 147464 | tf_op jit(solution)/shard_map/ppermute | solution.py:398
  28.2 0.7 transpose_reshape.4.bias1
  28.9 0.8 copy.63.w_hi
  29.7 0.8 copy.64.w_lo
  31.1 0.8 collective-permute-start.2
  31.9 0.6 pad_add_fusion.info
  32.5 7.0 %collective-permute-done.2 = bf16[4,24,512]{2,1,0:T(8,128)(2,1)S(1)} collective-permute-done((bf16[4,24,512]{2,1,0:T(8,128)(2,1)S(1)}, bf16[4,24,512]{2,1,0:T(8,128)(2,1)S(1)}, u32[]{:S(2)}, u32[]{:S(2)}) %collective-permute-start.2) | collective-permute-done | bytes 98336 | tf_op jit(solution)/shard_map/ppermute | solution.py:398
  39.5 0.7 pad_maximum_fusion.1.fields
  40.3 0.8 copy.61
  41.6 0.4 concatenate.94
  41.9 0.9 copy.60
  42.8 0.8 copy.62
  43.6 0.6 pad_maximum_fusion.10.e_pair
  44.2 18.3 %layers_forward.1 = (bf16[512,4096]{1,0:T(8,128)(2,1)}, bf16[512,4096]{1,0:T(8,128)(2,1)}, bf16[512,4096]{1,0:T(8,128)(2,1)}, bf16[32,4096]{1,0:T(8,128)(2,1)}, ...) custom-call(s32[2]{0:T(128)} %pad_add_fusion.info, ...), custom_call_target="tpu_custom_call" | custom-call | tf_op jit(solution)/shard_map/layers_forward/pallas_call | solution.py:512
  62.6 4.0 %all-to-all-start.1 = ((f32[8,32,512]{2,1,0:T(8,128)}), f32[8,32,512]{2,1,0:T(8,128)S(1)}, u32[]{:S(2)}, u32[]{:S(2)}) async-start(f32[8,32,512]{2,1,0:T(8,128)} %get-tuple-element.17), calls=%async_computation.1 | async-start | bytes 1048576 | tf_op jit(solution)/shard_map/all_to_all | solution.py:53
  66.6 0.6 copy.84
  67.2 2.5 %concatenate.99.w_start = bf16[32,512]{1,0:T(8,128)(2,1)} concatenate(bf16[3,512]{1,0:T(4,128)(2,1)S(1)} %bitcast.87, bf16[5,512]{1,0:T(8,128)(2,1)S(1)} %broadcast_in_dim.48, bf16[3,512]{1,0:T(4,128)(2,1)S(1)} %bitcast.88, bf16[5,512]{1,0:T(8,128)(2,1)S(1)} %broadcast_in_dim.48, bf16[3,512]{1,0:T(4,128)(2,1)S(1)} %bitcast.89, bf16[5,512]{1,0:T(8,128)(2,1)S(1)} %broadcast_in_dim.48, ...), dimensions={0} | concatenate | bytes 65536 | tf_op jit(solution)/shard_map/concatenate | solution.py:463
  69.7 1.9 %copy.67 = bf16[384,512]{0,1:T(8,128)(2,1)} copy(bf16[384,512]{1,0:T(8,128)(2,1)} %bitcast.73) | data formatting | bytes 786432 | tf_op jit(solution)/shard_map/reshape | solution.py:444
  71.8 0.6 pad_bitcast_fusion.e_up
  72.4 2.2 %convolution_convert_fusion.w_mix_t = bf16[512,384]{1,0:T(8,128)(2,1)} fusion(bf16[512,512]{1,0:T(8,128)(2,1)S(1)} %bitcast.78, bf16[384,512]{1,0:T(8,128)(2,1)} %bitcast.74), kind=kOutput, calls=%fused_computation.1 | convolution fusion | flops 201523200 | bytes 1310720 | tf_op jit(solution)/shard_map/dot_general | solution.py:17
  74.7 2.1 %all-to-all-done.1.got = f32[8,32,512]{2,1,0:T(8,128)S(1)} async-done(((f32[8,32,512]{2,1,0:T(8,128)}), f32[8,32,512]{2,1,0:T(8,128)S(1)}, u32[]{:S(2)}, u32[]{:S(2)}) %all-to-all-start.1) | async-done | bytes 524320 | tf_op jit(solution)/shard_map/all_to_all | solution.py:53
  76.8 0.8 copy-done.1
  77.6 20.3 %layers_backward.1 = (f32[1,3,512]{2,1,0:T(4,128)}, bf16[16,64,512]{2,1,0:T(8,128)(2,1)}) custom-call(s32[2]{0:T(128)} %pad_add_fusion.info, f32[8,32,512]{2,1,0:T(8,128)} %copy-done.1, bf16[8,24,512]{2,1,0:T(8,128)(2,1)} %pad_maximum_fusion.1.fields, f32[6,512]{1,0:T(8,128)} %bitcast.90, bf16[128,32]{1,0:T(8,128)(2,1)} %pad_bitcast_fusion.e_up, ...), custom_call_target="tpu_custom_call" | custom-call | tf_op jit(solution)/shard_map/layers_backward/pallas_call | solution.py:564
  97.9 6.6 %all-to-all-start.2 = ((bf16[16,64,512]{2,1,0:T(8,128)(2,1)}), bf16[16,64,512]{2,1,0:T(8,128)(2,1)S(1)}, u32[]{:S(2)}, u32[]{:S(2)}) async-start(bf16[16,64,512]{2,1,0:T(8,128)(2,1)} %get-tuple-element.26), calls=%async_computation.2 | async-start | bytes 2097152 | tf_op jit(solution)/shard_map/all_to_all | solution.py:53
  104.5 17.2 %all-to-all-done.2 = bf16[16,64,512]{2,1,0:T(8,128)(2,1)S(1)} async-done(((bf16[16,64,512]{2,1,0:T(8,128)(2,1)}), bf16[16,64,512]{2,1,0:T(8,128)(2,1)S(1)}, u32[]{:S(2)}, u32[]{:S(2)}) %all-to-all-start.2) | async-done | bytes 1048608 | tf_op jit(solution)/shard_map/all_to_all | solution.py:53
  121.7 0.1 convert_reduce_fusion
  122.0 0.1 fusion.9
  122.4 0.2 fusion.18
  122.6 0.9 convolution_select_fusion
  123.9 0.9 broadcast_in_dim.51
  124.8 3.5 %all-to-all-start.3 = ((bf16[8,72,512]{2,1,0:T(8,128)(2,1)}), bf16[8,72,512]{2,1,0:T(8,128)(2,1)S(1)}, u32[]{:S(2)}, u32[]{:S(2)}) async-start(bf16[8,72,512]{2,1,0:T(8,128)(2,1)} %broadcast_in_dim.51), calls=%async_computation.3 | async-start | bytes 1179648 | tf_op jit(solution)/shard_map/all_to_all | solution.py:53
  128.3 0.6 copy.74
  128.9 10.2 %all-to-all-done.3 = bf16[8,72,512]{2,1,0:T(8,128)(2,1)S(1)} async-done(((bf16[8,72,512]{2,1,0:T(8,128)(2,1)}), bf16[8,72,512]{2,1,0:T(8,128)(2,1)S(1)}, u32[]{:S(2)}, u32[]{:S(2)}) %all-to-all-start.3) | async-done | bytes 589856 | tf_op jit(solution)/shard_map/all_to_all | solution.py:53
  139.5 0.3 fusion.57
  139.8 0.3 fusion.59
  140.2 0.3 fusion.61
  140.6 0.7 broadcast_in_dim.52
  141.3 4.7 %all-to-all-start.4 = ((f32[16,24,128]{2,1,0:T(8,128)}), f32[16,24,128]{2,1,0:T(8,128)S(1)}, u32[]{:S(2)}, u32[]{:S(2)}) async-start(f32[16,24,128]{2,1,0:T(8,128)} %broadcast_in_dim.52), calls=%async_computation.4 | async-start | bytes 393216 | tf_op jit(solution)/shard_map/all_to_all | solution.py:53
  146.1 1.3 collective-permute-start.4
  147.5 0.1 reshape.124
  147.7 1.0 fusion.46
  148.7 0.9 pad_maximum_fusion
  150.0 3.5 %collective-permute-done.4 = f32[32,512]{1,0:T(8,128)S(1)} collective-permute-done((f32[32,512]{1,0:T(8,128)S(1)}, f32[32,512]{1,0:T(8,128)S(1)}, u32[]{:S(2)}, u32[]{:S(2)}) %collective-permute-start.4) | collective-permute-done | bytes 65568 | tf_op jit(solution)/shard_map/ppermute | solution.py:649
  153.5 1.1 maximum_select_fusion
  155.0 0.6 reshape.121
  155.6 0.6 add.132
  156.2 0.6 pad_maximum_fusion.7
  (114 shorter events, 3.7 us)
Async XLA Ops:
  0.6 27.4 %copy-start.6 = (f32[2,1024]{1,0:T(2,128)S(1)}, f32[2,1024]{1,0:T(2,128)}, u32[]{:S(2)}) copy-start(f32[2,1024]{1,0:T(2,128)} %param.15) | copy-start | bytes 24580
  1.4 12.9 %collective-permute-start.3 = (bf16[32,512]{1,0:T(8,128)(2,1)S(1)}, bf16[32,512]{1,0:T(8,128)(2,1)S(1)}, u32[]{:S(2)}, u32[]{:S(2)}) collective-permute-start(bf16[32,512]{1,0:T(8,128)(2,1)S(1)} %slice.255), channel_id=1, source_target_pairs={{0,64},{8,72},{16,80},{24,88},{32,96},{40,104},{48,112},{56,120},{... | collective-permute-start | bytes 98312 | tf_op jit(solution)/shard_map/ppermute | solution.py:401
  16.2 24.0 %all-to-all-start = ((bf16[16,64,512]{2,1,0:T(8,128)(2,1)}), bf16[16,64,512]{2,1,0:T(8,128)(2,1)S(1)}, u32[]{:S(2)}, u32[]{:S(2)}) async-start(bf16[16,64,512]{2,1,0:T(8,128)(2,1)} %broadcast_in_dim.45), calls=%async_computation | async-start | bytes 2097152 | tf_op jit(solution)/shard_map/all_to_all | solution.py:53
  22.4 2.8 %collective-permute-start = (bf16[1,24,512]{2,1,0:T(8,128)(2,1)S(1)}, bf16[1,24,512]{2,1,0:T(8,128)(2,1)S(1)}, u32[]{:S(2)}, u32[]{:S(2)}) collective-permute-start(bf16[1,24,512]{2,1,0:T(8,128)(2,1)S(1)} %pad_bitcast_fusion.1), channel_id=1, source_target_pairs={{0,1},{1,0},{2,3},{3,2},{4,5},{5,4},{6,7},{7,6},{8,9},{9,8},{10,11... | collective-permute-start | bytes 73736 | tf_op jit(solution)/shard_map/ppermute | solution.py:398
  25.1 6.0 %collective-permute-start.1 = (bf16[2,24,512]{2,1,0:T(8,128)(2,1)S(1)}, bf16[2,24,512]{2,1,0:T(8,128)(2,1)S(1)}, u32[]{:S(2)}, u32[]{:S(2)}) collective-permute-start(bf16[2,24,512]{2,1,0:T(8,128)(2,1)S(1)} %pad_maximum_fusion.3), channel_id=1, source_target_pairs={{0,2},{1,3},{2,0},{3,1},{4,6},{5,7},{6,4},{7,5},{8,10},{9,11},{10,... | collective-permute-start | bytes 147464 | tf_op jit(solution)/shard_map/ppermute | solution.py:398
  31.1 8.4 %collective-permute-start.2 = (bf16[4,24,512]{2,1,0:T(8,128)(2,1)S(1)}, bf16[4,24,512]{2,1,0:T(8,128)(2,1)S(1)}, u32[]{:S(2)}, u32[]{:S(2)}) collective-permute-start(bf16[4,24,512]{2,1,0:T(8,128)(2,1)S(1)} %pad_maximum_fusion.2), channel_id=1, source_target_pairs={{0,4},{1,5},{2,6},{3,7},{4,0},{5,1},{6,2},{7,3},{8,12},{9,13},{10,... | collective-permute-start | bytes 294920 | tf_op jit(solution)/shard_map/ppermute | solution.py:398
  32.5 34.1 %copy-start.3 = (f32[1,6,512]{2,0,1:T(1,128)S(1)}, f32[1,6,512]{2,0,1:T(1,128)}, u32[]{:S(2)}) copy-start(f32[1,6,512]{2,0,1:T(1,128)} %param.10) | copy-start | bytes 36868
  41.1 31.3 %copy-start = (bf16[8,2,32,512]{3,2,1,0:T(8,128)(2,1)S(1)}, bf16[8,2,32,512]{3,2,1,0:T(8,128)(2,1)}, u32[]{:S(2)}) copy-start(bf16[8,2,32,512]{3,2,1,0:T(8,128)(2,1)} %copy.61) | copy-start | bytes 1572868
  62.6 14.2 %all-to-all-start.1 = ((f32[8,32,512]{2,1,0:T(8,128)}), f32[8,32,512]{2,1,0:T(8,128)S(1)}, u32[]{:S(2)}, u32[]{:S(2)}) async-start(f32[8,32,512]{2,1,0:T(8,128)} %get-tuple-element.17), calls=%async_computation.1 | async-start | bytes 1048576 | tf_op jit(solution)/shard_map/all_to_all | solution.py:53
  76.8 0.8 copy-start.1
  97.9 30.4 %copy-start.5 = (f32[1,3,512]{2,1,0:T(4,128)S(1)}, f32[1,3,512]{2,1,0:T(4,128)}, u32[]{:S(2)}) copy-start(f32[1,3,512]{2,1,0:T(4,128)} %get-tuple-element.48) | copy-start | bytes 18436
  97.9 41.6 %copy-start.2 = (f32[512,3]{0,1:T(4,128)S(1)}, f32[512,3]{0,1:T(4,128)}, u32[]{:S(2)}) copy-start(f32[512,3]{0,1:T(4,128)} %param.13) | copy-start | bytes 18436
  97.9 23.8 %all-to-all-start.2 = ((bf16[16,64,512]{2,1,0:T(8,128)(2,1)}), bf16[16,64,512]{2,1,0:T(8,128)(2,1)S(1)}, u32[]{:S(2)}, u32[]{:S(2)}) async-start(bf16[16,64,512]{2,1,0:T(8,128)(2,1)} %get-tuple-element.26), calls=%async_computation.2 | async-start | bytes 2097152 | tf_op jit(solution)/shard_map/all_to_all | solution.py:53
  104.5 43.2 %copy-start.4 = (f32[6,512]{1,0:T(8,128)S(1)}, f32[6,512]{1,0:T(8,128)}, u32[]{:S(2)}) copy-start(f32[6,512]{1,0:T(8,128)} %param.18) | copy-start | bytes 36868
  124.8 14.4 %all-to-all-start.3 = ((bf16[8,72,512]{2,1,0:T(8,128)(2,1)}), bf16[8,72,512]{2,1,0:T(8,128)(2,1)S(1)}, u32[]{:S(2)}, u32[]{:S(2)}) async-start(bf16[8,72,512]{2,1,0:T(8,128)(2,1)} %broadcast_in_dim.51), calls=%async_computation.3 | async-start | bytes 1179648 | tf_op jit(solution)/shard_map/all_to_all | solution.py:53
  141.3 13.3 %all-to-all-start.4 = ((f32[16,24,128]{2,1,0:T(8,128)}), f32[16,24,128]{2,1,0:T(8,128)S(1)}, u32[]{:S(2)}, u32[]{:S(2)}) async-start(f32[16,24,128]{2,1,0:T(8,128)} %broadcast_in_dim.52), calls=%async_computation.4 | async-start | bytes 393216 | tf_op jit(solution)/shard_map/all_to_all | solution.py:53
  146.1 7.4 %collective-permute-start.4 = (f32[32,512]{1,0:T(8,128)S(1)}, f32[32,512]{1,0:T(8,128)S(1)}, u32[]{:S(2)}, u32[]{:S(2)}) collective-permute-start(f32[32,512]{1,0:T(8,128)S(1)} %convert_reduce_fusion.1), channel_id=1, source_target_pairs={{64,0},{72,8},{80,16},{88,24},{96,32},{104,40},{112,48},{120,56},{... | collective-permute-start | bytes 196616 | tf_op jit(solution)/shard_map/ppermute | solution.py:649

commit v3 on v2

--- a/solution.py
+++ b/solution.py
@@ -76,6 +76,86 @@
 def valid_row(c, width, length):
     at = lax.broadcasted_iota(jnp.int32, (1, width), 1) + c * width
     return (at < length).astype(f32)
+
+
+def packet_kernel(
+    info, conv, mix_first, mix_far, mix_last, start, ends,
+    packet,
+    sw, low_rows, ew, turn,
+):
+    dp = info[0]
+    k = info[1]
+    n_dp, per, channels = packet.shape
+    half = start.shape[0]
+    rows = mix_first.shape[0]
+    last_rows = mix_last.shape[0]
+    n_e = ends.shape[0]
+    part = (per - 8 - rows // 2) // 3
+    upper = dp >= n_dp // 2
+
+    group = conv[1, pl.ds(pl.multiple_of((k // 2) * 2 * part, 2 * part), 2 * part), :].astype(f32)
+    mine = jnp.where(k % 2 == 1, group[part:], group[:part]).astype(bf16)
+
+    sw[...] = jnp.zeros(sw.shape, f32)
+    sw[0:half, :] = start[...]
+    full = sw[...]
+    sw_hi = full.astype(bf16)
+    sw_lo = (full - sw_hi.astype(f32)).astype(bf16)
+    turn[...] = jnp.zeros(turn.shape, f32)
+    for tap in range(3):
+        block = conv[0, :, tap * channels : (tap + 1) * channels]
+        one = nt(sw_hi, block) + nt(sw_lo, block)
+        turn[half * tap : half * (tap + 1), 0:rows] = one[0:half]
+    a_t = turn[...]
+    a_hi = a_t[0:16].astype(bf16).astype(f32)
+    a_lo = a_t[0:16] - a_hi
+    lane = lax.broadcasted_iota(jnp.int32, (8, 128), 1)
+    row = lax.broadcasted_iota(jnp.int32, (8, 128), 0)
+    near = jnp.where(lane < rows, a_hi[0:8], pltpu.roll(a_lo[0:8], rows, 1))
+    far = jnp.where(row == 0, a_hi[8:16], pltpu.roll(a_lo[8:16], 1, 0))
+
+    ew[...] = jnp.zeros(ew.shape, f32)
+    ew[0:n_e, :] = ends[...]
+    e_all = ew[...]
+    wide = lax.broadcasted_iota(jnp.int32, (8, 128), 1)
+
+    def product(shift, count, source, keep):
+        moved = pltpu.roll(e_all, lax.rem(channels - shift, channels), 1)[:, 0:128]
+        moved = jnp.where(jnp.logical_and(wide < count, keep), moved, 0.0)
+        hi = moved.astype(bf16)
+        low = (moved - hi.astype(f32)).astype(bf16)
+        low_rows[...] = jnp.zeros(low_rows.shape, bf16)
+        low_rows[0:count, :] = source[...]
+        out = dot(hi, low_rows[...]) + dot(low, low_rows[...])
+        out_hi = out.astype(bf16)
+        return out_hi, (out - out_hi.astype(f32)).astype(bf16)
+
+    at = lax.broadcasted_iota(jnp.int32, (channels, 128), 0)
+    col = lax.broadcasted_iota(jnp.int32, (channels, 128), 1)
+    m = col - rows
+    pick0 = jnp.where(jnp.logical_and(col < rows, at == rows * k + col), 1.0, 0.0).astype(bf16)
+    target = (m >> 3) * rows + part * k + (m & 7)
+    pick1 = jnp.where(jnp.logical_and(m >= 0, at == target), 1.0, 0.0).astype(bf16)
+    e0_hi, e0_lo = product(
+        rows * jnp.maximum(dp - n_dp // 2, 0), rows, mix_first, upper
+    )
+    e1_hi, e1_lo = product(last_rows * dp, last_rows, mix_last, dp >= 0)
+    e_hi = dot(e0_hi, pick0) + dot(e1_hi, pick1)
+    e_lo = dot(e0_lo, pick0) + dot(e1_lo, pick1)
+
+    send = jnp.where(upper, mix_far[...].astype(f32), mix_first[0 : rows // 2, :].astype(f32))
+    send = send.astype(bf16)
+    base = 3 * part
+    for j in range(n_dp):
+        for tap in range(3):
+            packet[j, tap * part : (tap + 1) * part, :] = mine[
+                :, tap * channels : (tap + 1) * channels
+            ]
+        packet[j, base : base + 8, 0:128] = e_hi.astype(bf16)
+        packet[j, base : base + 8, 128:256] = e_lo.astype(bf16)
+        packet[j, base : base + 8, 256:384] = near.astype(bf16)
+        packet[j, base : base + 8, 384:512] = far.astype(bf16)
+        packet[j, base + 8 :, :] = send
 
 
 def forward_kernel(
@@ -106,7 +186,7 @@
         col = lax.broadcasted_iota(jnp.int32, full.shape, 1)
         w_start[...] = jnp.where(col < 18, top, full - top).astype(bf16)
         s_cat[...] = jnp.zeros(s_cat.shape, f32)
-        s_cat[27:29, :] = jnp.ones((2, bw), f32)
+        s_cat[27:29, :] = jnp.ones((2, g0_out.shape[1]), f32)
         packet[:, 24:32, :] = jnp.zeros((nb, 8, bw), f32)
         for c in range(nb):
             block = fields[c ^ k].astype(f32)
@@ -117,17 +197,18 @@
             fpad[6:7, at] = block[6 * half : 6 * half + 1]
             fpad[7:8, at] = valid
 
-    base = pl.multiple_of(i * bw, bw)
-    near = fpad[:, pl.ds(pl.multiple_of(pad0 + base, 128), bw)]
+    mw = g0_out.shape[1]
+    base = pl.multiple_of(i * mw, mw)
+    near = fpad[:, pl.ds(pl.multiple_of(pad0 + base, 128), mw)]
     off = near[6:7]
     valid = near[7:8]
-    behind = fpad[:, pl.ds(pl.multiple_of(base, 128), bw + 2 * dil0)]
-    ahead = fpad[:, pl.ds(pl.multiple_of(pad0 + base, 128), bw + 2 * dil0)]
-    left = rolled(behind, dil0, bw)
-    right = rolled(ahead, dil0, bw)
+    behind = fpad[:, pl.ds(pl.multiple_of(base, 128), mw + 2 * dil0)]
+    ahead = fpad[:, pl.ds(pl.multiple_of(pad0 + base, 128), mw + 2 * dil0)]
+    left = rolled(behind, dil0, mw)
+    right = rolled(ahead, dil0, mw)
     for step in range(1, BUCKETS):
-        left = jnp.where(off == step, rolled(behind, dil0 - step, bw), left)
-        right = jnp.where(off == step, rolled(ahead, dil0 + step, bw), right)
+        left = jnp.where(off == step, rolled(behind, dil0 - step, mw), left)
+        right = jnp.where(off == step, rolled(ahead, dil0 + step, mw), right)
     for part, at in ((left, 0), (near, 3), (right, 6)):
         s_cat[at : at + half, :] = part[0:half]
         s_cat[9 + at : 9 + at + half, :] = part[half : 2 * half]
@@ -150,14 +231,14 @@
         at = slice(tap * pair, (tap + 1) * pair)
         part = dot(w_mix[at, :], g_b) + dot(w_start[at, :], s_b)
         if tap == 1:
-            centre[:, pl.ds(base, bw)] = part
+            centre[:, pl.ds(base, mw)] = part
         else:
             to = tap // 2 * pair
-            cols = pl.ds(pl.multiple_of(pad1 + base, 128), bw)
+            cols = pl.ds(pl.multiple_of(pad1 + base, 128), mw)
             prod[to : to + pair, cols] = part.astype(bf16)
-    g_keep[:, pl.ds(base, bw)] = g0_out[pl.ds(pl.multiple_of(rows * k, rows), rows), :]
-
-    @pl.when(i == nb - 1)
+    g_keep[:, pl.ds(base, mw)] = g0_out[pl.ds(pl.multiple_of(rows * k, rows), rows), :]
+
+    @pl.when(i == pl.num_programs(0) - 1)
     def _():
         apart = steps_apart((256, 128))
 
@@ -190,7 +271,7 @@
             packet[c, 24 : 24 + half, :] = part[half : 2 * half]
             return carry
 
-        lax.fori_loop(0, nb, body, 0)
+        lax.fori_loop(0, nb, body, 0, unroll=2)
 
 
 def backward_kernel(
@@ -256,7 +337,7 @@
             dz_pad[rows:, pl.ds(at, bw)] = (up * dv1[:, pl.ds(base, bw)]).astype(bf16)
             return carry
 
-        lax.fori_loop(0, nb, first, 0)
+        lax.fori_loop(0, nb, first, 0, unroll=2)
 
         apart = steps_apart((128, 256))
 
@@ -278,35 +359,35 @@
             acc_b[...] += nt(jnp.ones((16, bw), bf16), centre)
             return carry
 
-        lax.fori_loop(0, nb, second, 0)
-
-    base = pl.multiple_of(i * bw, bw)
-    d_blk = d_taps[:, pl.ds(base, bw)]
+        lax.fori_loop(0, nb, second, 0, unroll=2)
+
+    mw = g0.shape[1]
+    base = pl.multiple_of(i * mw, mw)
+    d_blk = d_taps[:, pl.ds(base, mw)]
     s_b = s_in[...]
     acc_q[...] += nt(d_blk, g0[...])
     acc_s[...] += nt(s_b, d_blk)
     dg[...] = dot(w_mix_t[...], d_blk)
     own = pl.ds(pl.multiple_of(rows * k, rows), rows)
-    dg[own, :] = dg[own, :] + d_e0[:, pl.ds(base, bw)]
+    dg[own, :] = dg[own, :] + d_e0[:, pl.ds(base, mw)]
     up = dg[...]
     acc_m[:, 0:channels] += nt(s_b, (up * du0[...].astype(f32)).astype(bf16))
     acc_m[:, channels:] += nt(s_b, (up * dv0[...].astype(f32)).astype(bf16))
 
-    @pl.when(i == nb - 1)
+    @pl.when(i == pl.num_programs(0) - 1)
     def _():
         per_mix = channels // n_dp
         eighth = pair // n_dp
         q = acc_q[...]
         q_hi = q.astype(bf16)
-        q_lo = (q - q_hi.astype(f32)).astype(bf16)
         small[0:half, :] = acc_s[3 : 3 + half, :] + acc_s[12 : 12 + half, :]
         seen = small[0:8, :]
         seen_hi = seen.astype(bf16).astype(f32)
         small[8:16, :] = seen - seen_hi
         small[16:24, :] = seen
         d_start = small[...].astype(bf16)
-        acc_conv[...] = nt(q_hi, mix[...]) + nt(q_lo, mix[...]) + dot(d_start, w_start[...], 0, 0)
-        acc_mix[...] = dot(w_taps_t[...], q_hi) + dot(w_taps_t[...], q_lo)
+        acc_conv[...] = nt(q_hi, mix[...]) + dot(d_start, w_start[...], 0, 0)
+        acc_mix[...] = dot(w_taps_t[...], q_hi)
         starts = dot(d_start, w_taps[...])
         starts = starts[0:half] + starts[8 : 8 + half]
         m_rows[0:9, :] = acc_m[0:9, :] + acc_m[9:18, :]
@@ -383,6 +464,34 @@
             view, (0, 0, k, 0), (lead, cols // rows, 1, part)
         ).reshape(lead, cols // n_ctx)
 
+    half_rows = rows // 2
+    mix_far = lax.ppermute(
+        mix_first[half_rows:], "dp", [(i, i + half_dp) for i in range(half_dp)]
+    )
+    sw_hi, sw_lo = split(start_weight)
+    ew_last = lax.dynamic_slice(end_weight, (0, last_rows * dp), (n_e, last_rows))
+    ew_skip = lax.dynamic_slice(
+        end_weight, (0, rows * jnp.maximum(dp - half_dp, 0)), (n_e, rows)
+    )
+    ew_skip = jnp.where(low, 0.0, ew_skip)
+    mix_last_k = strided(mix_last).astype(f32)
+    mix_skip_k = lax.dynamic_slice(mix_first, (0, rows * k), (rows, rows)).astype(f32)
+    per = 3 * part + 8 + half_rows
+    smem = pl.BlockSpec(memory_space=pltpu.SMEM)
+    packets = pl.pallas_call(
+        packet_kernel,
+        in_specs=[smem] + [pl.BlockSpec(memory_space=pltpu.VMEM)] * 6,
+        out_specs=pl.BlockSpec(memory_space=pltpu.VMEM),
+        out_shape=jax.ShapeDtypeStruct((n_dp, per, channels), bf16),
+        scratch_shapes=[
+            pltpu.VMEM((16, channels), f32),
+            pltpu.VMEM((128, channels), bf16),
+            pltpu.VMEM((8, channels), f32),
+            pltpu.VMEM((16, 128), f32),
+        ],
+        name="weight_packets",
+    )(jnp.stack([dp, k]), conv_weight, mix_first, mix_far, mix_last, start_weight.T, end_weight)
+    got = exchange(packets.reshape(n_dp * per, channels), "dp").reshape(n_dp, per, channels)
     flux_hi, flux_lo = split(light_flux[0])
     cot_hi, cot_lo = split(cotangent[0])
     n_in = 6 * half + 1
@@ -397,58 +506,30 @@
         hop = fields.shape[0]
         other = lax.ppermute(fields, "ctx", [(c, c ^ hop) for c in range(n_ctx)])
         fields = jnp.concatenate([fields, other], axis=0)
-    half_rows = rows // 2
-    mix_far = lax.ppermute(
-        mix_first[half_rows:], "dp", [(i, i + half_dp) for i in range(half_dp)]
-    )
-    mix_send = jnp.where(low, mix_first[:half_rows], mix_far)
-
-    sw_hi, sw_lo = split(start_weight)
-    sw_pair = jnp.concatenate([sw_hi, sw_lo], axis=1)
-    a_rows = []
-    for tap in range(3):
-        parts = dot(sw_pair, conv0[:, tap * channels : (tap + 1) * channels], 0, 1)
-        a_rows.append(parts[:half] + parts[half:])
-    a_own = jnp.concatenate(a_rows, axis=0)
-    ew_last = lax.dynamic_slice(end_weight, (0, last_rows * dp), (n_e, last_rows))
-    ew_skip = lax.dynamic_slice(
-        end_weight, (0, rows * jnp.maximum(dp - half_dp, 0)), (n_e, rows)
-    )
-    ew_skip = jnp.where(low, 0.0, ew_skip)
-    mix_last_k = strided(mix_last).astype(f32)
-    mix_skip_k = lax.dynamic_slice(mix_first, (0, rows * k), (rows, rows)).astype(f32)
-    e_own = jnp.concatenate(
-        [
-            dot(ew_skip, mix_skip_k, precision=highest),
-            dot(ew_last, mix_last_k, precision=highest),
-        ],
-        axis=1,
-    )
-    a_hi, a_lo = split(a_own)
-    e_hi, e_lo = split(e_own)
-    a_block = pad_to(jnp.concatenate([a_hi, a_lo], axis=0), 20, rows).reshape(5, 4 * rows)
-    small = jnp.concatenate(
-        [pad_to(jnp.concatenate([e_hi, e_lo], axis=1), 8, 4 * rows), pad_to(a_block, 8, 4 * rows)],
-        axis=1,
-    )
-    conv_k = lax.dynamic_slice(conv1, (part * k, 0), (part, 3 * channels))
-    packet = jnp.concatenate(
-        [conv_k[:, tap * channels : (tap + 1) * channels] for tap in range(3)] + [small, mix_send],
-        axis=0,
-    )
-    per = packet.shape[0]
-    got = exchange(
-        jnp.broadcast_to(packet[None], (n_dp, per, channels)).reshape(n_dp * per, channels), "dp"
-    ).reshape(n_dp, per, channels)
     w_taps = got[:, : 3 * part].reshape(n_dp, 3, part, channels).transpose(1, 0, 2, 3)
     w_taps = w_taps.reshape(6 * rows, channels)
     mix_res = got[:, 4 * part :].reshape(2, half_dp, half_rows, channels).transpose(1, 0, 2, 3)
     mix_res = mix_res.reshape(channels, channels)
     e_k = got[:, 3 * part : 3 * part + n_e, : 4 * rows].astype(f32).sum(axis=0)
     e_cat = e_k[:, : 2 * rows] + e_k[:, 2 * rows :]
-    a_all = got[:, 3 * part : 3 * part + 5, 4 * rows :].reshape(n_dp, 20, rows)
-    a_all = a_all[:, :18].transpose(1, 0, 2).reshape(18, n_dp * rows)
+    a_got = got[:, 3 * part : 4 * part, 4 * rows :]
+    a_all = jnp.concatenate(
+        [
+            a_got[:, :, :rows],
+            a_got[:, 0:1, 2 * rows : 3 * rows],
+            a_got[:, :, rows : 2 * rows],
+            a_got[:, 1:2, 2 * rows : 3 * rows],
+        ],
+        axis=1,
+    )
+    a_all = a_all.transpose(1, 0, 2).reshape(18, n_dp * rows)
     a_hi, a_lo = a_all[:9], a_all[9:]
+
+    gap = jnp.zeros((8 - half, channels), bf16)
+    w_start = jnp.concatenate(
+        [sw_hi.T, gap, sw_hi.T, gap, sw_lo.T, gap, jnp.zeros((8, channels), bf16)], axis=0
+    )
+    fields, w_start = lax.optimization_barrier((fields, w_start))
 
     length = lengths[0]
     b_hi, b_lo = split(gate_bias[0][None])
@@ -459,10 +540,6 @@
         jnp.concatenate([jnp.pad(x, ((0, 0), (3, 6 - half)))] * 3 + [jnp.zeros((channels, 5), bf16)], axis=1)
         for x in (sw_hi, sw_lo)
     )
-    gap = jnp.zeros((8 - half, channels), bf16)
-    w_start = jnp.concatenate(
-        [sw_hi.T, gap, sw_hi.T, gap, sw_lo.T, gap, jnp.zeros((8, channels), bf16)], axis=0
-    )
     ec_hi, ec_lo = split(e_cat)
     gap = jnp.zeros((2, 2 * rows), bf16)
     e_pair = jnp.concatenate([ec_hi, gap, ec_lo, gap], axis=0)
@@ -470,6 +547,7 @@
     bias1 = strided(gate_bias[1][None]).T
     info = jnp.stack([length, k])
     pair = 2 * rows
+    main = 2 * shard_len
     wide = epochs + 2 * (dilations[1] + 128)
     smem = pl.BlockSpec(memory_space=pltpu.SMEM)
     shapes = jax.ShapeDtypeStruct
@@ -478,7 +556,7 @@
     )
     forward = pl.pallas_call(
         functools.partial(forward_kernel, dilations[0], dilations[1], half),
-        grid=(n_ctx,),
+        grid=(epochs // main,),
         in_specs=[
             smem,
             whole((n_ctx, n_pad, shard_len)),
@@ -490,15 +568,15 @@
             whole(bias1.shape),
             whole(e_pair.shape),
         ],
-        out_specs=[columns(channels, shard_len)] * 3
-        + [columns(32, shard_len), whole((pair, epochs)), whole((rows, epochs)),
+        out_specs=[columns(channels, main)] * 3
+        + [columns(32, main), whole((pair, epochs)), whole((rows, epochs)),
            whole((rows, epochs)), whole((n_ctx, 32, shard_len))],
         out_shape=[shapes((channels, epochs), bf16)] * 3
         + [shapes((32, epochs), bf16), shapes((pair, epochs), bf16), shapes((rows, epochs), f32),
            shapes((rows, epochs), f32), shapes((n_ctx, 32, shard_len), f32)],
         scratch_shapes=[
             pltpu.VMEM((8, epochs + 512), f32),
-            pltpu.VMEM((32, shard_len), f32),
+            pltpu.VMEM((32, main), f32),
             pltpu.VMEM((2 * pair, wide), bf16),
             pltpu.VMEM((pair, epochs), f32),
             pltpu.VMEM((pair, shard_len), f32),
@@ -519,7 +597,7 @@
     per = n_mix + n_conv + 8
     backward = pl.pallas_call(
         functools.partial(backward_kernel, dilations[1], half),
-        grid=(n_ctx,),
+        grid=(epochs // main,),
         in_specs=[
             smem,
             whole((n_ctx, 32, shard_len)),
@@ -535,8 +613,8 @@
             whole((channels, 3 * pair)),
             whole((32, channels)),
         ]
-        + [columns(channels, shard_len)] * 3
-        + [columns(32, shard_len)],
+        + [columns(channels, main)] * 3
+        + [columns(32, main)],
         out_specs=[whole((1, half, shard_len)), whole((n_dp, per, channels))],
         out_shape=[shapes((1, half, shard_len), f32), shapes((n_dp, per, channels), bf16)],
         scratch_shapes=[
@@ -552,7 +630,7 @@
             pltpu.VMEM((32, 3 * pair), f32),
             pltpu.VMEM((16, pair), f32),
             pltpu.VMEM((16, pair), f32),
-            pltpu.VMEM((channels, shard_len), f32),
+            pltpu.VMEM((channels, main), f32),
             pltpu.VMEM((16, 2 * channels), f32),
             pltpu.VMEM((8, 256), f32),
             pltpu.VMEM((3 * pair, channels), f32),

time: 158 us -> 152 us (0.962)
  local copies, waits for them, and re-layouts: 20.4 us -> 17 us
  matrix products: 8.93 us -> 6.78 us
  waiting for transfers between devices: 41.2 us -> 43.2 us
  Pallas kernels: 38.7 us -> 36.8 us
    all_to_all x5, waiting for transfers between devices: 29.5 us -> 32.8 us  [exchange(): return lax.all_to_all(x, axis, 0, 0, tiled=True)]
    pallas_call x1, Pallas kernels: 20.3 us -> 17.6 us  [local(): backward(info, got, fields, light_flux[0], e_up, g_own, du1, dv1, w_taps,...]
    pallas_call x0 -> x1, Pallas kernels: none -> 2.54 us  [local(): pl.pallas_call(packet_kernel, in_specs=[smem] + [pl.BlockSpec(memory_spac...]
    dot_general x16 -> x11, matrix products: 8.93 us -> 6.78 us  [dot(): lax.dot_general(a, b, (((ca,), (cb,)), ((), ())), precision=precision, pr...]
    pallas_call x1, Pallas kernels: 18.3 us -> 16.6 us  [local(): forward(info, fields, a_cat, w_hi, w_lo, mix_res, w_taps, bias1, e_pair)]
    transpose x4 -> x0, local copies, waits for them, and re-layouts: 1.66 us -> none  [the longest x1 0.83 us: local(): got[:, 4 * part:].reshape(2, half_dp, half_rows, channels)]
  transfers between devices with their start and end apart: 10 -> 10, of which waited for: 6 -> 5; matrix products, arithmetic and copies ran while one was open for 15% -> 13% of each run, Pallas kernels for 0% -> 2%
where the time goes in v3:
time: 152 us; the launch traced here: 151 us
  waiting for transfers between devices  43.2 us (28%)
  starting transfers between devices  36.8 us (24%)
  Pallas kernels  36.8 us (24%)
  local copies, waits for them, and re-layouts  17 us (11%)
  other arithmetic  8.61 us (6%)
  matrix products  6.78 us (4%)
  between operations  1.82 us (1%)
    all_to_all x5, waiting for transfers between devices, exchange(): return lax.all_to_all(x, axis, 0, 0, tiled=True)  32.8 us
    all_to_all x5, starting transfers between devices, exchange(): return lax.all_to_all(x, axis, 0, 0, tiled=True)  24.9 us
    pallas_call x1, Pallas kernels, local(): backward(info, got, fields, light_flux[0], e_up, g_own, du1, dv1, w_taps,...  17.6 us
    pallas_call x1, Pallas kernels, local(): forward(info, fields, a_cat, w_hi, w_lo, mix_res, w_taps, bias1, e_pair)  16.6 us
    ppermute x3, waiting for transfers between devices, local(): other = lax.ppermute(fields, 'ctx', [(c, c ^ hop) for c in range(n_ctx)])  6.92 us
    dot_general x11, matrix products, dot(): lax.dot_general(a, b, (((ca,), (cb,)), ((), ())), precision=precision, pr...  6.78 us
    ppermute x1, starting transfers between devices, local(): lax.ppermute(mix_first[half_rows:], 'dp', [(i, i + half_dp) for i in rang...  5.47 us
    ppermute x3, starting transfers between devices, local(): other = lax.ppermute(fields, 'ctx', [(c, c ^ hop) for c in range(n_ctx)])  5.21 us
  transfers between devices with their start and end apart: 10, of which 5 were waited for; matrix products, arithmetic and copies ran while one was open for 13% of the time, Pallas kernels for 2%

profile of v3, /device:TPU:1, one launch (start us, length us, event | category | flops | bytes accessed | tf_op | source)
XLA Modules:
  0.0 151.1 jit_solution(3234800446745596816)
XLA Ops:
  0.6 0.8 slice.215
  1.4 5.5 %collective-permute-start.3 = (bf16[32,512]{1,0:T(8,128)(2,1)S(1)}, bf16[32,512]{1,0:T(8,128)(2,1)S(1)}, u32[]{:S(2)}, u32[]{:S(2)}) collective-permute-start(bf16[32,512]{1,0:T(8,128)(2,1)S(1)} %slice.215), channel_id=1, source_target_pairs={{0,64},{8,72},{16,80},{24,88},{32,96},{40,104},{48,112},{56,120},{... | collective-permute-start | bytes 98312 | tf_op jit(solution)/shard_map/ppermute | solution.py:468
  6.9 0.7 fusion.9
  7.6 0.7 fusion.17
  8.3 0.7 convert_element_type.115
  9.0 0.2 concatenate.65
  9.2 1.4 collective-permute-start
  10.6 0.6 pad_add_fusion.1.info
  11.2 0.6 copy-done.7
  11.8 2.5 %weight_packets.1 = bf16[16,64,512]{2,1,0:T(8,128)(2,1)} custom-call(s32[2]{0:T(128)} %pad_add_fusion.1.info, bf16[2,64,1536]{2,1,0:T(8,128)(2,1)} %conv.1, bf16[64,512]{1,0:T(8,128)(2,1)} %mix_first.1, bf16[32,512]{1,0:T(8,128)(2,1)} %copy-done.7, bf16[32,512]{1,0:T(8,128)(2,1)} %mix_last.1, f32[3,512]{1,0:T(4,128)} %bitcast.83, f32[6,512]{1,0:T(8,128)} %ends.1), custom_call_target="tpu_custom_call" | custom-call | tf_op jit(solution)/shard_map/weight_packets/pallas_call | solution.py:481
  14.3 6.7 %all-to-all-start = ((bf16[16,64,512]{2,1,0:T(8,128)(2,1)}), bf16[16,64,512]{2,1,0:T(8,128)(2,1)S(1)}, u32[]{:S(2)}, u32[]{:S(2)}) async-start(bf16[16,64,512]{2,1,0:T(8,128)(2,1)} %weight_packets.1), calls=%async_computation | async-start | bytes 2097152 | tf_op jit(solution)/shard_map/all_to_all | solution.py:53
  21.0 0.7 fusion.18
  21.9 3.0 %collective-permute-start.1 = (bf16[2,24,512]{2,1,0:T(8,128)(2,1)S(1)}, bf16[2,24,512]{2,1,0:T(8,128)(2,1)S(1)}, u32[]{:S(2)}, u32[]{:S(2)}) collective-permute-start(bf16[2,24,512]{2,1,0:T(8,128)(2,1)S(1)} %pad_maximum_fusion.3), channel_id=1, source_target_pairs={{0,2},{1,3},{2,0},{3,1},{4,6},{5,7},{6,4},{7,5},{8,10},{9,11},{10,... | collective-permute-start | bytes 147464 | tf_op jit(solution)/shard_map/ppermute | solution.py:507
  25.1 0.7 transpose_reshape.4.bias1
  26.5 0.8 copy.66.w_hi
  27.2 0.8 copy.67.w_lo
  28.0 2.4 %concatenate.69.w_start = bf16[32,512]{1,0:T(8,128)(2,1)} concatenate(bf16[3,512]{1,0:T(4,128)(2,1)S(1)} %bitcast.86, bf16[5,512]{1,0:T(8,128)(2,1)S(1)} %broadcast_in_dim.38, bf16[3,512]{1,0:T(4,128)(2,1)S(1)} %bitcast.87, bf16[5,512]{1,0:T(8,128)(2,1)S(1)} %broadcast_in_dim.38, bf16[3,512]{1,0:T(4,128)(2,1)S(1)} %bitcast.88, bf16[5,512]{1,0:T(8,128)(2,1)S(1)} %broadcast_in_dim.38, ...), dimensions={0} | concatenate | bytes 65536 | tf_op jit(solution)/shard_map/concatenate | solution.py:529
  30.4 0.8 collective-permute-start.2
  31.3 0.6 pad_add_fusion.info
  31.9 6.9 %collective-permute-done.2 = bf16[4,24,512]{2,1,0:T(8,128)(2,1)S(1)} collective-permute-done((bf16[4,24,512]{2,1,0:T(8,128)(2,1)S(1)}, bf16[4,24,512]{2,1,0:T(8,128)(2,1)S(1)}, u32[]{:S(2)}, u32[]{:S(2)}) %collective-permute-start.2) | collective-permute-done | bytes 98336 | tf_op jit(solution)/shard_map/ppermute | solution.py:507
  38.8 0.7 pad_maximum_fusion.1.fields
  39.9 0.4 concatenate.71
  40.3 0.9 copy.63
  41.2 0.8 copy.65
  42.0 0.8 copy.64
  42.9 0.6 pad_maximum_fusion.7.e_pair
  43.5 16.6 %layers_forward.1 = (bf16[512,4096]{1,0:T(8,128)(2,1)}, bf16[512,4096]{1,0:T(8,128)(2,1)}, bf16[512,4096]{1,0:T(8,128)(2,1)}, bf16[32,4096]{1,0:T(8,128)(2,1)}, ...) custom-call(s32[2]{0:T(128)} %pad_add_fusion.info, ...), custom_call_target="tpu_custom_call" | custom-call | tf_op jit(solution)/shard_map/layers_forward/pallas_call | solution.py:590
  60.1 3.5 %all-to-all-start.1 = ((f32[8,32,512]{2,1,0:T(8,128)}), f32[8,32,512]{2,1,0:T(8,128)S(1)}, u32[]{:S(2)}, u32[]{:S(2)}) async-start(f32[8,32,512]{2,1,0:T(8,128)} %get-tuple-element.20), calls=%async_computation.1 | async-start | bytes 1048576 | tf_op jit(solution)/shard_map/all_to_all | solution.py:53
  63.6 0.6 copy.88
  64.3 0.9 copy.70
  65.2 0.1 copy.69
  65.3 0.6 pad_bitcast_fusion.e_up
  66.0 2.3 %convolution_convert_fusion.w_mix_t = bf16[512,384]{1,0:T(8,128)(2,1)} fusion(bf16[512,512]{1,0:T(8,128)(2,1)} %bitcast.75, bf16[384,512]{1,0:T(8,128)(2,1)S(1)} %bitcast.73), kind=kOutput, calls=%fused_computation.1 | convolution fusion | flops 201523200 | bytes 1310720 | tf_op jit(solution)/shard_map/dot_general | solution.py:17
  68.3 5.5 %all-to-all-done.1.got = f32[8,32,512]{2,1,0:T(8,128)S(1)} async-done(((f32[8,32,512]{2,1,0:T(8,128)}), f32[8,32,512]{2,1,0:T(8,128)S(1)}, u32[]{:S(2)}, u32[]{:S(2)}) %all-to-all-start.1) | async-done | bytes 524320 | tf_op jit(solution)/shard_map/all_to_all | solution.py:53
  73.8 0.8 copy-done.1
  74.6 17.6 %layers_backward.1 = (f32[1,3,512]{2,1,0:T(4,128)}, bf16[16,64,512]{2,1,0:T(8,128)(2,1)}) custom-call(s32[2]{0:T(128)} %pad_add_fusion.info, f32[8,32,512]{2,1,0:T(8,128)} %copy-done.1, bf16[8,24,512]{2,1,0:T(8,128)(2,1)} %pad_maximum_fusion.1.fields, f32[6,512]{1,0:T(8,128)} %bitcast.85, bf16[128,32]{1,0:T(8,128)(2,1)} %pad_bitcast_fusion.e_up, ...), custom_call_target="tpu_custom_call" | custom-call | tf_op jit(solution)/shard_map/layers_backward/pallas_call | solution.py:642
  92.3 6.5 %all-to-all-start.2 = ((bf16[16,64,512]{2,1,0:T(8,128)(2,1)}), bf16[16,64,512]{2,1,0:T(8,128)(2,1)S(1)}, u32[]{:S(2)}, u32[]{:S(2)}) async-start(bf16[16,64,512]{2,1,0:T(8,128)(2,1)} %get-tuple-element.30), calls=%async_computation.2 | async-start | bytes 2097152 | tf_op jit(solution)/shard_map/all_to_all | solution.py:53
  98.7 0.1 copy.71
  98.9 17.0 %all-to-all-done.2 = bf16[16,64,512]{2,1,0:T(8,128)(2,1)S(1)} async-done(((bf16[16,64,512]{2,1,0:T(8,128)(2,1)}), bf16[16,64,512]{2,1,0:T(8,128)(2,1)S(1)}, u32[]{:S(2)}, u32[]{:S(2)}) %all-to-all-start.2) | async-done | bytes 1048608 | tf_op jit(solution)/shard_map/all_to_all | solution.py:53
  115.9 0.1 convert_reduce_fusion
  116.2 0.1 fusion.5
  116.3 0.1 fusion.3
  116.5 0.1 fusion.1
  116.7 0.2 fusion.12
  116.9 0.9 convolution_select_fusion
  118.2 0.9 broadcast_in_dim.44
  119.0 3.5 %all-to-all-start.3 = ((bf16[8,72,512]{2,1,0:T(8,128)(2,1)}), bf16[8,72,512]{2,1,0:T(8,128)(2,1)S(1)}, u32[]{:S(2)}, u32[]{:S(2)}) async-start(bf16[8,72,512]{2,1,0:T(8,128)(2,1)} %broadcast_in_dim.44), calls=%async_computation.3 | async-start | bytes 1179648 | tf_op jit(solution)/shard_map/all_to_all | solution.py:53
  122.6 0.6 copy.78
  123.2 10.2 %all-to-all-done.3 = bf16[8,72,512]{2,1,0:T(8,128)(2,1)S(1)} async-done(((bf16[8,72,512]{2,1,0:T(8,128)(2,1)}), bf16[8,72,512]{2,1,0:T(8,128)(2,1)S(1)}, u32[]{:S(2)}, u32[]{:S(2)}) %all-to-all-start.3) | async-done | bytes 589856 | tf_op jit(solution)/shard_map/all_to_all | solution.py:53
  133.7 0.3 fusion.37
  134.1 0.3 fusion.39
  134.4 0.3 fusion.41
  134.9 0.7 broadcast_in_dim.45
  135.5 4.7 %all-to-all-start.4 = ((f32[16,24,128]{2,1,0:T(8,128)}), f32[16,24,128]{2,1,0:T(8,128)S(1)}, u32[]{:S(2)}, u32[]{:S(2)}) async-start(f32[16,24,128]{2,1,0:T(8,128)} %broadcast_in_dim.45), calls=%async_computation.4 | async-start | bytes 393216 | tf_op jit(solution)/shard_map/all_to_all | solution.py:53
  140.3 1.3 collective-permute-start.4
  141.6 0.1 reshape.113
  141.8 0.1 reshape.114
  142.0 0.9 pad_maximum_fusion
  142.9 1.0 fusion.25
  144.2 3.5 %collective-permute-done.4 = f32[32,512]{1,0:T(8,128)S(1)} collective-permute-done((f32[32,512]{1,0:T(8,128)S(1)}, f32[32,512]{1,0:T(8,128)S(1)}, u32[]{:S(2)}, u32[]{:S(2)}) %collective-permute-start.4) | collective-permute-done | bytes 65568 | tf_op jit(solution)/shard_map/ppermute | solution.py:727
  147.8 1.0 maximum_select_fusion
  149.2 0.6 reshape.111
  149.8 0.6 add.110
  150.4 0.6 pad_maximum_fusion.5
  (103 shorter events, 2.7 us)
Async XLA Ops:
  0.6 24.3 %copy-start.9 = (f32[2,1024]{1,0:T(2,128)S(1)}, f32[2,1024]{1,0:T(2,128)}, u32[]{:S(2)}) copy-start(f32[2,1024]{1,0:T(2,128)} %param.15) | copy-start | bytes 24580
  1.4 9.7 %collective-permute-start.3 = (bf16[32,512]{1,0:T(8,128)(2,1)S(1)}, bf16[32,512]{1,0:T(8,128)(2,1)S(1)}, u32[]{:S(2)}, u32[]{:S(2)}) collective-permute-start(bf16[32,512]{1,0:T(8,128)(2,1)S(1)} %slice.215), channel_id=1, source_target_pairs={{0,64},{8,72},{16,80},{24,88},{32,96},{40,104},{48,112},{56,120},{... | collective-permute-start | bytes 98312 | tf_op jit(solution)/shard_map/ppermute | solution.py:468
  9.2 12.7 %collective-permute-start = (bf16[1,24,512]{2,1,0:T(8,128)(2,1)S(1)}, bf16[1,24,512]{2,1,0:T(8,128)(2,1)S(1)}, u32[]{:S(2)}, u32[]{:S(2)}) collective-permute-start(bf16[1,24,512]{2,1,0:T(8,128)(2,1)S(1)} %pad_bitcast_fusion.1), channel_id=1, source_target_pairs={{0,1},{1,0},{2,3},{3,2},{4,5},{5,4},{6,7},{7,6},{8,9},{9,8},{10,11... | collective-permute-start | bytes 73736 | tf_op jit(solution)/shard_map/ppermute | solution.py:507
  11.2 0.6 copy-start.7
  14.3 25.1 %all-to-all-start = ((bf16[16,64,512]{2,1,0:T(8,128)(2,1)}), bf16[16,64,512]{2,1,0:T(8,128)(2,1)S(1)}, u32[]{:S(2)}, u32[]{:S(2)}) async-start(bf16[16,64,512]{2,1,0:T(8,128)(2,1)} %weight_packets.1), calls=%async_computation | async-start | bytes 2097152 | tf_op jit(solution)/shard_map/all_to_all | solution.py:53
  21.9 8.5 %collective-permute-start.1 = (bf16[2,24,512]{2,1,0:T(8,128)(2,1)S(1)}, bf16[2,24,512]{2,1,0:T(8,128)(2,1)S(1)}, u32[]{:S(2)}, u32[]{:S(2)}) collective-permute-start(bf16[2,24,512]{2,1,0:T(8,128)(2,1)S(1)} %pad_maximum_fusion.3), channel_id=1, source_target_pairs={{0,2},{1,3},{2,0},{3,1},{4,6},{5,7},{6,4},{7,5},{8,10},{9,11},{10,... | collective-permute-start | bytes 147464 | tf_op jit(solution)/shard_map/ppermute | solution.py:507
  30.4 8.3 %collective-permute-start.2 = (bf16[4,24,512]{2,1,0:T(8,128)(2,1)S(1)}, bf16[4,24,512]{2,1,0:T(8,128)(2,1)S(1)}, u32[]{:S(2)}, u32[]{:S(2)}) collective-permute-start(bf16[4,24,512]{2,1,0:T(8,128)(2,1)S(1)} %pad_maximum_fusion.2), channel_id=1, source_target_pairs={{0,4},{1,5},{2,6},{3,7},{4,0},{5,1},{6,2},{7,3},{8,12},{9,13},{10,... | collective-permute-start | bytes 294920 | tf_op jit(solution)/shard_map/ppermute | solution.py:507
  31.9 31.8 %copy-start.5 = (f32[1,6,512]{2,0,1:T(1,128)S(1)}, f32[1,6,512]{2,0,1:T(1,128)}, u32[]{:S(2)}) copy-start(f32[1,6,512]{2,0,1:T(1,128)} %param.10) | copy-start | bytes 36868
  42.0 22.3 %copy-start = (bf16[16,3,8,512]{3,2,0,1:T(8,128)(2,1)S(1)}, bf16[16,3,8,512]{3,2,0,1:T(8,128)(2,1)}, u32[]{:S(2)}) copy-start(bf16[16,3,8,512]{3,2,0,1:T(8,128)(2,1)} %copy.65) | copy-start | bytes 1179652
  60.1 13.7 %all-to-all-start.1 = ((f32[8,32,512]{2,1,0:T(8,128)}), f32[8,32,512]{2,1,0:T(8,128)S(1)}, u32[]{:S(2)}, u32[]{:S(2)}) async-start(f32[8,32,512]{2,1,0:T(8,128)} %get-tuple-element.20), calls=%async_computation.1 | async-start | bytes 1048576 | tf_op jit(solution)/shard_map/all_to_all | solution.py:53
  73.8 0.8 copy-start.1
  74.6 24.1 %copy-start.4 = (bf16[32,512]{1,0:T(8,128)(2,1)S(1)}, bf16[32,512]{1,0:T(8,128)(2,1)}, u32[]{:S(2)}) copy-start(bf16[32,512]{1,0:T(8,128)(2,1)} %mix_last.1) | copy-start | bytes 98308
  74.6 24.3 %copy-start.2 = (bf16[2,64,1536]{2,1,0:T(8,128)(2,1)S(1)}, bf16[2,64,1536]{2,1,0:T(8,128)(2,1)}, u32[]{:S(2)}) copy-start(bf16[2,64,1536]{2,1,0:T(8,128)(2,1)} %conv.1) | copy-start | bytes 1179652
  92.2 30.3 %copy-start.8 = (f32[1,3,512]{2,1,0:T(4,128)S(1)}, f32[1,3,512]{2,1,0:T(4,128)}, u32[]{:S(2)}) copy-start(f32[1,3,512]{2,1,0:T(4,128)} %get-tuple-element.52) | copy-start | bytes 18436
  92.3 41.5 %copy-start.3 = (f32[512,3]{0,1:T(4,128)S(1)}, f32[512,3]{0,1:T(4,128)}, u32[]{:S(2)}) copy-start(f32[512,3]{0,1:T(4,128)} %param.13) | copy-start | bytes 18436
  92.3 23.7 %all-to-all-start.2 = ((bf16[16,64,512]{2,1,0:T(8,128)(2,1)}), bf16[16,64,512]{2,1,0:T(8,128)(2,1)S(1)}, u32[]{:S(2)}, u32[]{:S(2)}) async-start(bf16[16,64,512]{2,1,0:T(8,128)(2,1)} %get-tuple-element.30), calls=%async_computation.2 | async-start | bytes 2097152 | tf_op jit(solution)/shard_map/all_to_all | solution.py:53
  118.2 24.8 %copy-start.6 = (f32[6,512]{1,0:T(8,128)S(1)}, f32[6,512]{1,0:T(8,128)}, u32[]{:S(2)}) copy-start(f32[6,512]{1,0:T(8,128)} %ends.1) | copy-start | bytes 36868
  119.0 14.4 %all-to-all-start.3 = ((bf16[8,72,512]{2,1,0:T(8,128)(2,1)}), bf16[8,72,512]{2,1,0:T(8,128)(2,1)S(1)}, u32[]{:S(2)}, u32[]{:S(2)}) async-start(bf16[8,72,512]{2,1,0:T(8,128)(2,1)} %broadcast_in_dim.44), calls=%async_computation.3 | async-start | bytes 1179648 | tf_op jit(solution)/shard_map/all_to_all | solution.py:53
  135.5 13.3 %all-to-all-start.4 = ((f32[16,24,128]{2,1,0:T(8,128)}), f32[16,24,128]{2,1,0:T(8,128)S(1)}, u32[]{:S(2)}, u32[]{:S(2)}) async-start(f32[16,24,128]{2,1,0:T(8,128)} %broadcast_in_dim.45), calls=%async_computation.4 | async-start | bytes 393216 | tf_op jit(solution)/shard_map/all_to_all | solution.py:53
  140.3 7.4 %collective-permute-start.4 = (f32[32,512]{1,0:T(8,128)S(1)}, f32[32,512]{1,0:T(8,128)S(1)}, u32[]{:S(2)}, u32[]{:S(2)}) collective-permute-start(f32[32,512]{1,0:T(8,128)S(1)} %convert_reduce_fusion.1), channel_id=1, source_target_pairs={{64,0},{72,8},{80,16},{88,24},{96,32},{104,40},{112,48},{120,56},{... | collective-permute-start | bytes 196616 | tf_op jit(solution)/shard_map/ppermute | solution.py:727

commit v4 on v3

--- a/solution.py
+++ b/solution.py
@@ -160,8 +160,8 @@
 
 def forward_kernel(
     dil0, dil1, half,
-    info, fields, a_cat, w_hi, w_lo, mix, w_taps, bias1, e_pair,
-    g0_out, du0_out, dv0_out, s_out, gown_out, du1_out, dv1_out, packet,
+    info, fields, a_cat, w_hi, w_lo, weights, bias1, e_pair,
+    g0_out, du0_out, dv0_out, s_out, gown_out, du1_out, dv1_out, packet, mix, w_taps,
     fpad, s_cat, prod, centre, pre_s, g_keep, w_mix, w_start,
 ):
     i = pl.program_id(0)
@@ -180,6 +180,15 @@
         fpad[:, pad0 + nb * bw :] = jnp.zeros((8, pad0), f32)
         prod[:, 0:pad1] = jnp.zeros((prod.shape[0], pad1), bf16)
         prod[:, pad1 + nb * bw :] = jnp.zeros((prod.shape[0], pad1), bf16)
+        n_dp = weights.shape[0]
+        part = 2 * rows // n_dp
+        half_rows = rows // 2
+        for j in range(n_dp):
+            for tap in range(3):
+                to = tap * 2 * rows + j * part
+                w_taps[to : to + part, :] = weights[j, tap * part : (tap + 1) * part, :]
+            to = rows * (j % (n_dp // 2)) + half_rows * (j // (n_dp // 2))
+            mix[to : to + half_rows, :] = weights[j, 4 * part :, :]
         w_mix[...] = dot(w_taps[...], mix[...]).astype(bf16)
         full = dot(w_taps[...], w_hi[...]) + dot(w_taps[...], w_lo[...])
         top = full.astype(bf16).astype(f32)
@@ -506,10 +515,7 @@
         hop = fields.shape[0]
         other = lax.ppermute(fields, "ctx", [(c, c ^ hop) for c in range(n_ctx)])
         fields = jnp.concatenate([fields, other], axis=0)
-    w_taps = got[:, : 3 * part].reshape(n_dp, 3, part, channels).transpose(1, 0, 2, 3)
-    w_taps = w_taps.reshape(6 * rows, channels)
-    mix_res = got[:, 4 * part :].reshape(2, half_dp, half_rows, channels).transpose(1, 0, 2, 3)
-    mix_res = mix_res.reshape(channels, channels)
+    weights = got
     e_k = got[:, 3 * part : 3 * part + n_e, : 4 * rows].astype(f32).sum(axis=0)
     e_cat = e_k[:, : 2 * rows] + e_k[:, 2 * rows :]
     a_got = got[:, 3 * part : 4 * part, 4 * rows :]
@@ -563,17 +569,18 @@
             whole(a_cat.shape),
             whole(w_hi.shape),
             whole(w_lo.shape),
-            whole(mix_res.shape),
-            whole(w_taps.shape),
+            whole(weights.shape),
             whole(bias1.shape),
             whole(e_pair.shape),
         ],
         out_specs=[columns(channels, main)] * 3
         + [columns(32, main), whole((pair, epochs)), whole((rows, epochs)),
-           whole((rows, epochs)), whole((n_ctx, 32, shard_len))],
+           whole((rows, epochs)), whole((n_ctx, 32, shard_len)),
+           whole((channels, channels)), whole((3 * pair, channels))],
         out_shape=[shapes((channels, epochs), bf16)] * 3
         + [shapes((32, epochs), bf16), shapes((pair, epochs), bf16), shapes((rows, epochs), f32),
-           shapes((rows, epochs), f32), shapes((n_ctx, 32, shard_len), f32)],
+           shapes((rows, epochs), f32), shapes((n_ctx, 32, shard_len), f32),
+           shapes((channels, channels), bf16), shapes((3 * pair, channels), bf16)],
         scratch_shapes=[
             pltpu.VMEM((8, epochs + 512), f32),
             pltpu.VMEM((32, main), f32),
@@ -587,8 +594,8 @@
         compiler_params=params,
         name="layers_forward",
     )
-    g0, du0, dv0, s_all, g_own, du1, dv1, packed = forward(
-        info, fields, a_cat, w_hi, w_lo, mix_res, w_taps, bias1, e_pair
+    g0, du0, dv0, s_all, g_own, du1, dv1, packed, mix_res, w_taps = forward(
+        info, fields, a_cat, w_hi, w_lo, weights, bias1, e_pair
     )
     got = exchange(packed.reshape(n_ctx * 32, shard_len), "ctx").reshape(n_ctx, 32, shard_len)
 

time: 152 us -> 151 us (level)
    reshape x4 -> x0, local copies, waits for them, and re-layouts: 2.56 us -> none  [the longest x1 0.92 us: local(): w_taps = w_taps.reshape(6 * rows, channels)]
    pallas_call x0 -> x1, local copies, waits for them, and re-layouts: none -> 1.91 us  [local(): forward(info, fields, a_cat, w_hi, w_lo, weights, bias1, e_pair)]
where the time goes in v4:
time: 151 us; the launch traced here: 150 us
  waiting for transfers between devices  42.1 us (28%)
  Pallas kernels  37.3 us (25%)
  starting transfers between devices  37 us (25%)
  local copies, waits for them, and re-layouts  16.3 us (11%)
  other arithmetic  8.61 us (6%)
  matrix products  6.89 us (5%)
  between operations  1.81 us (1%)
    all_to_all x5, waiting for transfers between devices, exchange(): return lax.all_to_all(x, axis, 0, 0, tiled=True)  31.7 us
    all_to_all x5, starting transfers between devices, exchange(): return lax.all_to_all(x, axis, 0, 0, tiled=True)  25 us
    pallas_call x1, Pallas kernels, local(): backward(info, got, fields, light_flux[0], e_up, g_own, du1, dv1, w_taps,...  17.7 us
    pallas_call x1, Pallas kernels, local(): forward(info, fields, a_cat, w_hi, w_lo, weights, bias1, e_pair)  17.1 us
    ppermute x3, waiting for transfers between devices, local(): other = lax.ppermute(fields, 'ctx', [(c, c ^ hop) for c in range(n_ctx)])  6.92 us
    dot_general x11, matrix products, dot(): lax.dot_general(a, b, (((ca,), (cb,)), ((), ())), precision=precision, pr...  6.89 us
    ppermute x1, starting transfers between devices, local(): lax.ppermute(mix_first[half_rows:], 'dp', [(i, i + half_dp) for i in rang...  5.47 us
    ppermute x3, starting transfers between devices, local(): other = lax.ppermute(fields, 'ctx', [(c, c ^ hop) for c in range(n_ctx)])  5.21 us
  transfers between devices with their start and end apart: 10, of which 5 were waited for; matrix products, arithmetic and copies ran while one was open for 13% of the time, Pallas kernels for 2%

profile of v4, /device:TPU:1, one launch (start us, length us, event | category | flops | bytes accessed | tf_op | source)
XLA Modules:
  0.0 150.0 jit_solution(15790337405693260190)
XLA Ops:
  0.6 0.8 slice.209
  1.4 5.5 %collective-permute-start.3 = (bf16[32,512]{1,0:T(8,128)(2,1)S(1)}, bf16[32,512]{1,0:T(8,128)(2,1)S(1)}, u32[]{:S(2)}, u32[]{:S(2)}) collective-permute-start(bf16[32,512]{1,0:T(8,128)(2,1)S(1)} %slice.209), channel_id=1, source_target_pairs={{0,64},{8,72},{16,80},{24,88},{32,96},{40,104},{48,112},{56,120},{... | collective-permute-start | bytes 98312 | tf_op jit(solution)/shard_map/ppermute | solution.py:477
  6.9 0.7 fusion.9
  7.6 0.7 fusion.17
  8.3 0.7 convert_element_type.115
  9.0 0.2 concatenate.65
  9.2 1.4 collective-permute-start
  10.6 0.6 pad_add_fusion.1.info
  11.2 0.6 copy-done.7
  11.8 2.5 %weight_packets.1 = bf16[16,64,512]{2,1,0:T(8,128)(2,1)} custom-call(s32[2]{0:T(128)} %pad_add_fusion.1.info, bf16[2,64,1536]{2,1,0:T(8,128)(2,1)} %conv.1, bf16[64,512]{1,0:T(8,128)(2,1)} %mix_first.1, bf16[32,512]{1,0:T(8,128)(2,1)} %copy-done.7, bf16[32,512]{1,0:T(8,128)(2,1)} %mix_last.1, f32[3,512]{1,0:T(4,128)} %bitcast.66, f32[6,512]{1,0:T(8,128)} %ends.1), custom_call_target="tpu_custom_call" | custom-call | tf_op jit(solution)/shard_map/weight_packets/pallas_call | solution.py:490
  14.3 6.8 %all-to-all-start = ((bf16[16,64,512]{2,1,0:T(8,128)(2,1)}), bf16[16,64,512]{2,1,0:T(8,128)(2,1)S(1)}, u32[]{:S(2)}, u32[]{:S(2)}) async-start(bf16[16,64,512]{2,1,0:T(8,128)(2,1)} %weight_packets.1), calls=%async_computation | async-start | bytes 2097152 | tf_op jit(solution)/shard_map/all_to_all | solution.py:53
  21.1 0.7 fusion.18
  22.1 3.0 %collective-permute-start.1 = (bf16[2,24,512]{2,1,0:T(8,128)(2,1)S(1)}, bf16[2,24,512]{2,1,0:T(8,128)(2,1)S(1)}, u32[]{:S(2)}, u32[]{:S(2)}) collective-permute-start(bf16[2,24,512]{2,1,0:T(8,128)(2,1)S(1)} %pad_maximum_fusion.3), channel_id=1, source_target_pairs={{0,2},{1,3},{2,0},{3,1},{4,6},{5,7},{6,4},{7,5},{8,10},{9,11},{10,... | collective-permute-start | bytes 147464 | tf_op jit(solution)/shard_map/ppermute | solution.py:516
  25.2 0.7 transpose_reshape.4.bias1
  26.6 0.8 copy.60.w_hi
  27.4 0.8 copy.61.w_lo
  28.1 2.4 %concatenate.69.w_start = bf16[32,512]{1,0:T(8,128)(2,1)} concatenate(bf16[3,512]{1,0:T(4,128)(2,1)S(1)} %bitcast.69, bf16[5,512]{1,0:T(8,128)(2,1)S(1)} %broadcast_in_dim.38, bf16[3,512]{1,0:T(4,128)(2,1)S(1)} %bitcast.70, bf16[5,512]{1,0:T(8,128)(2,1)S(1)} %broadcast_in_dim.38, bf16[3,512]{1,0:T(4,128)(2,1)S(1)} %bitcast.71, bf16[5,512]{1,0:T(8,128)(2,1)S(1)} %broadcast_in_dim.38, ...), dimensions={0} | concatenate | bytes 65536 | tf_op jit(solution)/shard_map/concatenate | solution.py:535
  30.6 0.8 collective-permute-start.2
  31.4 0.6 pad_add_fusion.info
  32.0 6.9 %collective-permute-done.2 = bf16[4,24,512]{2,1,0:T(8,128)(2,1)S(1)} collective-permute-done((bf16[4,24,512]{2,1,0:T(8,128)(2,1)S(1)}, bf16[4,24,512]{2,1,0:T(8,128)(2,1)S(1)}, u32[]{:S(2)}, u32[]{:S(2)}) %collective-permute-start.2) | collective-permute-done | bytes 98336 | tf_op jit(solution)/shard_map/ppermute | solution.py:516
  38.9 0.7 pad_maximum_fusion.1.fields
  39.8 0.1 slice.215
  39.9 0.1 slice.217
  40.1 0.4 concatenate.71
  40.4 0.9 copy.59
  41.3 0.6 pad_maximum_fusion.7.e_pair
  41.9 17.1 %layers_forward.1 = (bf16[512,4096]{1,0:T(8,128)(2,1)}, bf16[512,4096]{1,0:T(8,128)(2,1)}, bf16[512,4096]{1,0:T(8,128)(2,1)}, bf16[32,4096]{1,0:T(8,128)(2,1)}, ...) custom-call(s32[2]{0:T(128)} %pad_add_fusion.info, ...), custom_call_target="tpu_custom_call" | custom-call | tf_op jit(solution)/shard_map/layers_forward/pallas_call | solution.py:597
  59.0 3.5 %all-to-all-start.1 = ((f32[8,32,512]{2,1,0:T(8,128)}), f32[8,32,512]{2,1,0:T(8,128)S(1)}, u32[]{:S(2)}, u32[]{:S(2)}) async-start(f32[8,32,512]{2,1,0:T(8,128)} %get-tuple-element.22), calls=%async_computation.1 | async-start | bytes 1048576 | tf_op jit(solution)/shard_map/all_to_all | solution.py:53
  62.6 0.6 copy.82
  63.3 1.9 %copy.64 = bf16[384,512]{0,1:T(8,128)(2,1)} copy(bf16[384,512]{1,0:T(8,128)(2,1)} %get-tuple-element.26.w_taps) | data formatting | bytes 786432 | tf_op jit(solution)/shard_map/layers_forward/pallas_call | solution.py:597
  65.2 0.1 copy.63
  65.3 0.6 pad_bitcast_fusion.e_up
  65.9 2.4 %convolution_convert_fusion.w_mix_t = bf16[512,384]{1,0:T(8,128)(2,1)} fusion(bf16[512,512]{1,0:T(8,128)(2,1)} %get-tuple-element.27.mix, bf16[384,512]{1,0:T(8,128)(2,1)} %get-tuple-element.26.w_taps), kind=kOutput, calls=%fused_computation.1 | convolution fusion | flops 201523200 | bytes 1310720 | tf_op jit(solution)/shard_map/dot_general | solution.py:17
  68.3 4.4 %all-to-all-done.1.got = f32[8,32,512]{2,1,0:T(8,128)S(1)} async-done(((f32[8,32,512]{2,1,0:T(8,128)}), f32[8,32,512]{2,1,0:T(8,128)S(1)}, u32[]{:S(2)}, u32[]{:S(2)}) %all-to-all-start.1) | async-done | bytes 524320 | tf_op jit(solution)/shard_map/all_to_all | solution.py:53
  72.8 0.8 copy-done.1
  73.6 17.7 %layers_backward.1 = (f32[1,3,512]{2,1,0:T(4,128)}, bf16[16,64,512]{2,1,0:T(8,128)(2,1)}) custom-call(s32[2]{0:T(128)} %pad_add_fusion.info, f32[8,32,512]{2,1,0:T(8,128)} %copy-done.1, bf16[8,24,512]{2,1,0:T(8,128)(2,1)} %pad_maximum_fusion.1.fields, f32[6,512]{1,0:T(8,128)} %bitcast.68, bf16[128,32]{1,0:T(8,128)(2,1)} %pad_bitcast_fusion.e_up, ...), custom_call_target="tpu_custom_call" | custom-call | tf_op jit(solution)/shard_map/layers_backward/pallas_call | solution.py:649
  91.2 6.5 %all-to-all-start.2 = ((bf16[16,64,512]{2,1,0:T(8,128)(2,1)}), bf16[16,64,512]{2,1,0:T(8,128)(2,1)S(1)}, u32[]{:S(2)}, u32[]{:S(2)}) async-start(bf16[16,64,512]{2,1,0:T(8,128)(2,1)} %get-tuple-element.34), calls=%async_computation.2 | async-start | bytes 2097152 | tf_op jit(solution)/shard_map/all_to_all | solution.py:53
  97.7 0.1 copy.65
  97.9 17.0 %all-to-all-done.2 = bf16[16,64,512]{2,1,0:T(8,128)(2,1)S(1)} async-done(((bf16[16,64,512]{2,1,0:T(8,128)(2,1)}), bf16[16,64,512]{2,1,0:T(8,128)(2,1)S(1)}, u32[]{:S(2)}, u32[]{:S(2)}) %all-to-all-start.2) | async-done | bytes 1048608 | tf_op jit(solution)/shard_map/all_to_all | solution.py:53
  114.9 0.1 convert_reduce_fusion
  115.2 0.1 fusion.5
  115.3 0.1 fusion.3
  115.4 0.1 fusion.1
  115.7 0.2 fusion.12
  115.9 0.9 convolution_select_fusion
  117.1 0.9 broadcast_in_dim.44
  118.0 3.5 %all-to-all-start.3 = ((bf16[8,72,512]{2,1,0:T(8,128)(2,1)}), bf16[8,72,512]{2,1,0:T(8,128)(2,1)S(1)}, u32[]{:S(2)}, u32[]{:S(2)}) async-start(bf16[8,72,512]{2,1,0:T(8,128)(2,1)} %broadcast_in_dim.44), calls=%async_computation.3 | async-start | bytes 1179648 | tf_op jit(solution)/shard_map/all_to_all | solution.py:53
  121.5 0.6 copy.72
  122.1 10.2 %all-to-all-done.3 = bf16[8,72,512]{2,1,0:T(8,128)(2,1)S(1)} async-done(((bf16[8,72,512]{2,1,0:T(8,128)(2,1)}), bf16[8,72,512]{2,1,0:T(8,128)(2,1)S(1)}, u32[]{:S(2)}, u32[]{:S(2)}) %all-to-all-start.3) | async-done | bytes 589856 | tf_op jit(solution)/shard_map/all_to_all | solution.py:53
  132.7 0.3 fusion.37
  133.0 0.3 fusion.39
  133.4 0.3 fusion.41
  133.8 0.7 broadcast_in_dim.45
  134.5 4.7 %all-to-all-start.4 = ((f32[16,24,128]{2,1,0:T(8,128)}), f32[16,24,128]{2,1,0:T(8,128)S(1)}, u32[]{:S(2)}, u32[]{:S(2)}) async-start(f32[16,24,128]{2,1,0:T(8,128)} %broadcast_in_dim.45), calls=%async_computation.4 | async-start | bytes 393216 | tf_op jit(solution)/shard_map/all_to_all | solution.py:53
  139.3 1.3 collective-permute-start.4
  140.6 0.1 reshape.97
  140.8 0.1 reshape.98
  141.0 0.9 pad_maximum_fusion
  141.9 1.0 fusion.25
  143.2 3.5 %collective-permute-done.4 = f32[32,512]{1,0:T(8,128)S(1)} collective-permute-done((f32[32,512]{1,0:T(8,128)S(1)}, f32[32,512]{1,0:T(8,128)S(1)}, u32[]{:S(2)}, u32[]{:S(2)}) %collective-permute-start.4) | collective-permute-done | bytes 65568 | tf_op jit(solution)/shard_map/ppermute | solution.py:734
  146.7 1.1 maximum_select_fusion
  148.2 0.6 reshape.95
  148.8 0.6 add.110
  149.4 0.6 pad_maximum_fusion.5
  (99 shorter events, 2.5 us)
Async XLA Ops:
  0.6 24.4 %copy-start.9 = (f32[2,1024]{1,0:T(2,128)S(1)}, f32[2,1024]{1,0:T(2,128)}, u32[]{:S(2)}) copy-start(f32[2,1024]{1,0:T(2,128)} %param.15) | copy-start | bytes 24580
  1.4 9.7 %collective-permute-start.3 = (bf16[32,512]{1,0:T(8,128)(2,1)S(1)}, bf16[32,512]{1,0:T(8,128)(2,1)S(1)}, u32[]{:S(2)}, u32[]{:S(2)}) collective-permute-start(bf16[32,512]{1,0:T(8,128)(2,1)S(1)} %slice.209), channel_id=1, source_target_pairs={{0,64},{8,72},{16,80},{24,88},{32,96},{40,104},{48,112},{56,120},{... | collective-permute-start | bytes 98312 | tf_op jit(solution)/shard_map/ppermute | solution.py:477
  9.2 12.8 %collective-permute-start = (bf16[1,24,512]{2,1,0:T(8,128)(2,1)S(1)}, bf16[1,24,512]{2,1,0:T(8,128)(2,1)S(1)}, u32[]{:S(2)}, u32[]{:S(2)}) collective-permute-start(bf16[1,24,512]{2,1,0:T(8,128)(2,1)S(1)} %pad_bitcast_fusion.1), channel_id=1, source_target_pairs={{0,1},{1,0},{2,3},{3,2},{4,5},{5,4},{6,7},{7,6},{8,9},{9,8},{10,11... | collective-permute-start | bytes 73736 | tf_op jit(solution)/shard_map/ppermute | solution.py:516
  11.2 0.6 copy-start.7
  14.3 48.3 %copy-start.5 = (f32[1,6,512]{2,0,1:T(1,128)S(1)}, f32[1,6,512]{2,0,1:T(1,128)}, u32[]{:S(2)}) copy-start(f32[1,6,512]{2,0,1:T(1,128)} %param.10) | copy-start | bytes 36868
  14.3 25.3 %all-to-all-start = ((bf16[16,64,512]{2,1,0:T(8,128)(2,1)}), bf16[16,64,512]{2,1,0:T(8,128)(2,1)S(1)}, u32[]{:S(2)}, u32[]{:S(2)}) async-start(bf16[16,64,512]{2,1,0:T(8,128)(2,1)} %weight_packets.1), calls=%async_computation | async-start | bytes 2097152 | tf_op jit(solution)/shard_map/all_to_all | solution.py:53
  22.1 8.5 %collective-permute-start.1 = (bf16[2,24,512]{2,1,0:T(8,128)(2,1)S(1)}, bf16[2,24,512]{2,1,0:T(8,128)(2,1)S(1)}, u32[]{:S(2)}, u32[]{:S(2)}) collective-permute-start(bf16[2,24,512]{2,1,0:T(8,128)(2,1)S(1)} %pad_maximum_fusion.3), channel_id=1, source_target_pairs={{0,2},{1,3},{2,0},{3,1},{4,6},{5,7},{6,4},{7,5},{8,10},{9,11},{10,... | collective-permute-start | bytes 147464 | tf_op jit(solution)/shard_map/ppermute | solution.py:516
  30.6 8.3 %collective-permute-start.2 = (bf16[4,24,512]{2,1,0:T(8,128)(2,1)S(1)}, bf16[4,24,512]{2,1,0:T(8,128)(2,1)S(1)}, u32[]{:S(2)}, u32[]{:S(2)}) collective-permute-start(bf16[4,24,512]{2,1,0:T(8,128)(2,1)S(1)} %pad_maximum_fusion.2), channel_id=1, source_target_pairs={{0,4},{1,5},{2,6},{3,7},{4,0},{5,1},{6,2},{7,3},{8,12},{9,13},{10,... | collective-permute-start | bytes 294920 | tf_op jit(solution)/shard_map/ppermute | solution.py:516
  39.6 2.3 %copy-start = (bf16[16,64,512]{2,1,0:T(8,128)(2,1)}, bf16[16,64,512]{2,1,0:T(8,128)(2,1)S(1)}, u32[]{:S(2)}) copy-start(bf16[16,64,512]{2,1,0:T(8,128)(2,1)S(1)} %all-to-all-done.weights) | copy-start | bytes 3145732
  59.0 13.7 %all-to-all-start.1 = ((f32[8,32,512]{2,1,0:T(8,128)}), f32[8,32,512]{2,1,0:T(8,128)S(1)}, u32[]{:S(2)}, u32[]{:S(2)}) async-start(f32[8,32,512]{2,1,0:T(8,128)} %get-tuple-element.22), calls=%async_computation.1 | async-start | bytes 1048576 | tf_op jit(solution)/shard_map/all_to_all | solution.py:53
  72.8 0.8 copy-start.1
  73.6 24.1 %copy-start.4 = (bf16[32,512]{1,0:T(8,128)(2,1)S(1)}, bf16[32,512]{1,0:T(8,128)(2,1)}, u32[]{:S(2)}) copy-start(bf16[32,512]{1,0:T(8,128)(2,1)} %mix_last.1) | copy-start | bytes 98308
  73.6 24.3 %copy-start.2 = (bf16[2,64,1536]{2,1,0:T(8,128)(2,1)S(1)}, bf16[2,64,1536]{2,1,0:T(8,128)(2,1)}, u32[]{:S(2)}) copy-start(bf16[2,64,1536]{2,1,0:T(8,128)(2,1)} %conv.1) | copy-start | bytes 1179652
  91.2 30.3 %copy-start.8 = (f32[1,3,512]{2,1,0:T(4,128)S(1)}, f32[1,3,512]{2,1,0:T(4,128)}, u32[]{:S(2)}) copy-start(f32[1,3,512]{2,1,0:T(4,128)} %get-tuple-element.56) | copy-start | bytes 18436
  91.2 41.5 %copy-start.3 = (f32[512,3]{0,1:T(4,128)S(1)}, f32[512,3]{0,1:T(4,128)}, u32[]{:S(2)}) copy-start(f32[512,3]{0,1:T(4,128)} %param.13) | copy-start | bytes 18436
  91.2 23.7 %all-to-all-start.2 = ((bf16[16,64,512]{2,1,0:T(8,128)(2,1)}), bf16[16,64,512]{2,1,0:T(8,128)(2,1)S(1)}, u32[]{:S(2)}, u32[]{:S(2)}) async-start(bf16[16,64,512]{2,1,0:T(8,128)(2,1)} %get-tuple-element.34), calls=%async_computation.2 | async-start | bytes 2097152 | tf_op jit(solution)/shard_map/all_to_all | solution.py:53
  117.1 24.8 %copy-start.6 = (f32[6,512]{1,0:T(8,128)S(1)}, f32[6,512]{1,0:T(8,128)}, u32[]{:S(2)}) copy-start(f32[6,512]{1,0:T(8,128)} %ends.1) | copy-start | bytes 36868
  118.0 14.4 %all-to-all-start.3 = ((bf16[8,72,512]{2,1,0:T(8,128)(2,1)}), bf16[8,72,512]{2,1,0:T(8,128)(2,1)S(1)}, u32[]{:S(2)}, u32[]{:S(2)}) async-start(bf16[8,72,512]{2,1,0:T(8,128)(2,1)} %broadcast_in_dim.44), calls=%async_computation.3 | async-start | bytes 1179648 | tf_op jit(solution)/shard_map/all_to_all | solution.py:53
  134.5 13.3 %all-to-all-start.4 = ((f32[16,24,128]{2,1,0:T(8,128)}), f32[16,24,128]{2,1,0:T(8,128)S(1)}, u32[]{:S(2)}, u32[]{:S(2)}) async-start(f32[16,24,128]{2,1,0:T(8,128)} %broadcast_in_dim.45), calls=%async_computation.4 | async-start | bytes 393216 | tf_op jit(solution)/shard_map/all_to_all | solution.py:53
  139.3 7.4 %collective-permute-start.4 = (f32[32,512]{1,0:T(8,128)S(1)}, f32[32,512]{1,0:T(8,128)S(1)}, u32[]{:S(2)}, u32[]{:S(2)}) collective-permute-start(f32[32,512]{1,0:T(8,128)S(1)} %convert_reduce_fusion.1), channel_id=1, source_target_pairs={{64,0},{72,8},{80,16},{88,24},{96,32},{104,40},{112,48},{120,56},{... | collective-permute-start | bytes 196616 | tf_op jit(solution)/shard_map/ppermute | solution.py:734

commit v5 on v4

--- a/solution.py
+++ b/solution.py
@@ -346,7 +346,7 @@
             dz_pad[rows:, pl.ds(at, bw)] = (up * dv1[:, pl.ds(base, bw)]).astype(bf16)
             return carry
 
-        lax.fori_loop(0, nb, first, 0, unroll=2)
+        lax.fori_loop(0, nb, first, 0, unroll=4)
 
         apart = steps_apart((128, 256))
 
@@ -368,7 +368,7 @@
             acc_b[...] += nt(jnp.ones((16, bw), bf16), centre)
             return carry
 
-        lax.fori_loop(0, nb, second, 0, unroll=2)
+        lax.fori_loop(0, nb, second, 0, unroll=4)
 
     mw = g0.shape[1]
     base = pl.multiple_of(i * mw, mw)
@@ -604,7 +604,7 @@
     per = n_mix + n_conv + 8
     backward = pl.pallas_call(
         functools.partial(backward_kernel, dilations[1], half),
-        grid=(epochs // main,),
+        grid=(n_ctx,),
         in_specs=[
             smem,
             whole((n_ctx, 32, shard_len)),
@@ -620,8 +620,8 @@
             whole((channels, 3 * pair)),
             whole((32, channels)),
         ]
-        + [columns(channels, main)] * 3
-        + [columns(32, main)],
+        + [columns(channels, shard_len)] * 3
+        + [columns(32, shard_len)],
         out_specs=[whole((1, half, shard_len)), whole((n_dp, per, channels))],
         out_shape=[shapes((1, half, shard_len), f32), shapes((n_dp, per, channels), bf16)],
         scratch_shapes=[
@@ -637,7 +637,7 @@
             pltpu.VMEM((32, 3 * pair), f32),
             pltpu.VMEM((16, pair), f32),
             pltpu.VMEM((16, pair), f32),
-            pltpu.VMEM((channels, main), f32),
+            pltpu.VMEM((channels, shard_len), f32),
             pltpu.VMEM((16, 2 * channels), f32),
             pltpu.VMEM((8, 256), f32),
             pltpu.VMEM((3 * pair, channels), f32),

time: 151 us -> 152 us (level)
  no operation moved by 1% of the time
where the time goes in v5:
time: 152 us; the launch traced here: 151 us
  waiting for transfers between devices  42.1 us (28%)
  Pallas kernels  37.9 us (25%)
  starting transfers between devices  37 us (24%)
  local copies, waits for them, and re-layouts  16.3 us (11%)
  other arithmetic  8.61 us (6%)
  matrix products  6.89 us (5%)
  between operations  1.81 us (1%)
    all_to_all x5, waiting for transfers between devices, exchange(): return lax.all_to_all(x, axis, 0, 0, tiled=True)  31.7 us
    all_to_all x5, starting transfers between devices, exchange(): return lax.all_to_all(x, axis, 0, 0, tiled=True)  25 us
    pallas_call x1, Pallas kernels, local(): backward(info, got, fields, light_flux[0], e_up, g_own, du1, dv1, w_taps,...  18.2 us
    pallas_call x1, Pallas kernels, local(): forward(info, fields, a_cat, w_hi, w_lo, weights, bias1, e_pair)  17.1 us
    ppermute x3, waiting for transfers between devices, local(): other = lax.ppermute(fields, 'ctx', [(c, c ^ hop) for c in range(n_ctx)])  6.92 us
    dot_general x11, matrix products, dot(): lax.dot_general(a, b, (((ca,), (cb,)), ((), ())), precision=precision, pr...  6.89 us
    ppermute x1, starting transfers between devices, local(): lax.ppermute(mix_first[half_rows:], 'dp', [(i, i + half_dp) for i in rang...  5.47 us
    ppermute x3, starting transfers between devices, local(): other = lax.ppermute(fields, 'ctx', [(c, c ^ hop) for c in range(n_ctx)])  5.21 us
  transfers between devices with their start and end apart: 10, of which 5 were waited for; matrix products, arithmetic and copies ran while one was open for 13% of the time, Pallas kernels for 2%

profile of v5, /device:TPU:1, one launch (start us, length us, event | category | flops | bytes accessed | tf_op | source)
XLA Modules:
  0.0 150.6 jit_solution(18141676339376893395)
XLA Ops:
  0.6 0.8 slice.209
  1.4 5.5 %collective-permute-start.3 = (bf16[32,512]{1,0:T(8,128)(2,1)S(1)}, bf16[32,512]{1,0:T(8,128)(2,1)S(1)}, u32[]{:S(2)}, u32[]{:S(2)}) collective-permute-start(bf16[32,512]{1,0:T(8,128)(2,1)S(1)} %slice.209), channel_id=1, source_target_pairs={{0,64},{8,72},{16,80},{24,88},{32,96},{40,104},{48,112},{56,120},{... | collective-permute-start | bytes 98312 | tf_op jit(solution)/shard_map/ppermute | solution.py:477
  6.9 0.7 fusion.9
  7.6 0.7 fusion.17
  8.3 0.7 convert_element_type.115
  9.0 0.2 concatenate.65
  9.2 1.4 collective-permute-start
  10.6 0.6 pad_add_fusion.1.info
  11.2 0.6 copy-done.7
  11.8 2.5 %weight_packets.1 = bf16[16,64,512]{2,1,0:T(8,128)(2,1)} custom-call(s32[2]{0:T(128)} %pad_add_fusion.1.info, bf16[2,64,1536]{2,1,0:T(8,128)(2,1)} %conv.1, bf16[64,512]{1,0:T(8,128)(2,1)} %mix_first.1, bf16[32,512]{1,0:T(8,128)(2,1)} %copy-done.7, bf16[32,512]{1,0:T(8,128)(2,1)} %mix_last.1, f32[3,512]{1,0:T(4,128)} %bitcast.66, f32[6,512]{1,0:T(8,128)} %ends.1), custom_call_target="tpu_custom_call" | custom-call | tf_op jit(solution)/shard_map/weight_packets/pallas_call | solution.py:490
  14.3 6.8 %all-to-all-start = ((bf16[16,64,512]{2,1,0:T(8,128)(2,1)}), bf16[16,64,512]{2,1,0:T(8,128)(2,1)S(1)}, u32[]{:S(2)}, u32[]{:S(2)}) async-start(bf16[16,64,512]{2,1,0:T(8,128)(2,1)} %weight_packets.1), calls=%async_computation | async-start | bytes 2097152 | tf_op jit(solution)/shard_map/all_to_all | solution.py:53
  21.1 0.7 fusion.18
  22.1 3.0 %collective-permute-start.1 = (bf16[2,24,512]{2,1,0:T(8,128)(2,1)S(1)}, bf16[2,24,512]{2,1,0:T(8,128)(2,1)S(1)}, u32[]{:S(2)}, u32[]{:S(2)}) collective-permute-start(bf16[2,24,512]{2,1,0:T(8,128)(2,1)S(1)} %pad_maximum_fusion.3), channel_id=1, source_target_pairs={{0,2},{1,3},{2,0},{3,1},{4,6},{5,7},{6,4},{7,5},{8,10},{9,11},{10,... | collective-permute-start | bytes 147464 | tf_op jit(solution)/shard_map/ppermute | solution.py:516
  25.2 0.7 transpose_reshape.4.bias1
  26.6 0.8 copy.60.w_hi
  27.4 0.8 copy.61.w_lo
  28.1 2.4 %concatenate.69.w_start = bf16[32,512]{1,0:T(8,128)(2,1)} concatenate(bf16[3,512]{1,0:T(4,128)(2,1)S(1)} %bitcast.69, bf16[5,512]{1,0:T(8,128)(2,1)S(1)} %broadcast_in_dim.38, bf16[3,512]{1,0:T(4,128)(2,1)S(1)} %bitcast.70, bf16[5,512]{1,0:T(8,128)(2,1)S(1)} %broadcast_in_dim.38, bf16[3,512]{1,0:T(4,128)(2,1)S(1)} %bitcast.71, bf16[5,512]{1,0:T(8,128)(2,1)S(1)} %broadcast_in_dim.38, ...), dimensions={0} | concatenate | bytes 65536 | tf_op jit(solution)/shard_map/concatenate | solution.py:535
  30.6 0.8 collective-permute-start.2
  31.4 0.6 pad_add_fusion.info
  32.0 6.9 %collective-permute-done.2 = bf16[4,24,512]{2,1,0:T(8,128)(2,1)S(1)} collective-permute-done((bf16[4,24,512]{2,1,0:T(8,128)(2,1)S(1)}, bf16[4,24,512]{2,1,0:T(8,128)(2,1)S(1)}, u32[]{:S(2)}, u32[]{:S(2)}) %collective-permute-start.2) | collective-permute-done | bytes 98336 | tf_op jit(solution)/shard_map/ppermute | solution.py:516
  38.9 0.7 pad_maximum_fusion.1.fields
  39.8 0.1 slice.215
  39.9 0.1 slice.217
  40.1 0.4 concatenate.71
  40.4 0.9 copy.59
  41.3 0.6 pad_maximum_fusion.7.e_pair
  41.9 17.1 %layers_forward.1 = (bf16[512,4096]{1,0:T(8,128)(2,1)}, bf16[512,4096]{1,0:T(8,128)(2,1)}, bf16[512,4096]{1,0:T(8,128)(2,1)}, bf16[32,4096]{1,0:T(8,128)(2,1)}, ...) custom-call(s32[2]{0:T(128)} %pad_add_fusion.info, ...), custom_call_target="tpu_custom_call" | custom-call | tf_op jit(solution)/shard_map/layers_forward/pallas_call | solution.py:597
  59.0 3.5 %all-to-all-start.1 = ((f32[8,32,512]{2,1,0:T(8,128)}), f32[8,32,512]{2,1,0:T(8,128)S(1)}, u32[]{:S(2)}, u32[]{:S(2)}) async-start(f32[8,32,512]{2,1,0:T(8,128)} %get-tuple-element.22), calls=%async_computation.1 | async-start | bytes 1048576 | tf_op jit(solution)/shard_map/all_to_all | solution.py:53
  62.6 0.6 copy.82
  63.3 1.9 %copy.64 = bf16[384,512]{0,1:T(8,128)(2,1)} copy(bf16[384,512]{1,0:T(8,128)(2,1)} %get-tuple-element.26.w_taps) | data formatting | bytes 786432 | tf_op jit(solution)/shard_map/layers_forward/pallas_call | solution.py:597
  65.2 0.1 copy.63
  65.3 0.6 pad_bitcast_fusion.e_up
  65.9 2.4 %convolution_convert_fusion.w_mix_t = bf16[512,384]{1,0:T(8,128)(2,1)} fusion(bf16[512,512]{1,0:T(8,128)(2,1)} %get-tuple-element.27.mix, bf16[384,512]{1,0:T(8,128)(2,1)} %get-tuple-element.26.w_taps), kind=kOutput, calls=%fused_computation.1 | convolution fusion | flops 201523200 | bytes 1310720 | tf_op jit(solution)/shard_map/dot_general | solution.py:17
  68.3 4.4 %all-to-all-done.1.got = f32[8,32,512]{2,1,0:T(8,128)S(1)} async-done(((f32[8,32,512]{2,1,0:T(8,128)}), f32[8,32,512]{2,1,0:T(8,128)S(1)}, u32[]{:S(2)}, u32[]{:S(2)}) %all-to-all-start.1) | async-done | bytes 524320 | tf_op jit(solution)/shard_map/all_to_all | solution.py:53
  72.8 0.8 copy-done.1
  73.6 18.2 %layers_backward.1 = (f32[1,3,512]{2,1,0:T(4,128)}, bf16[16,64,512]{2,1,0:T(8,128)(2,1)}) custom-call(s32[2]{0:T(128)} %pad_add_fusion.info, f32[8,32,512]{2,1,0:T(8,128)} %copy-done.1, bf16[8,24,512]{2,1,0:T(8,128)(2,1)} %pad_maximum_fusion.1.fields, f32[6,512]{1,0:T(8,128)} %bitcast.68, bf16[128,32]{1,0:T(8,128)(2,1)} %pad_bitcast_fusion.e_up, ...), custom_call_target="tpu_custom_call" | custom-call | tf_op jit(solution)/shard_map/layers_backward/pallas_call | solution.py:649
  91.8 6.5 %all-to-all-start.2 = ((bf16[16,64,512]{2,1,0:T(8,128)(2,1)}), bf16[16,64,512]{2,1,0:T(8,128)(2,1)S(1)}, u32[]{:S(2)}, u32[]{:S(2)}) async-start(bf16[16,64,512]{2,1,0:T(8,128)(2,1)} %get-tuple-element.34), calls=%async_computation.2 | async-start | bytes 2097152 | tf_op jit(solution)/shard_map/all_to_all | solution.py:53
  98.3 0.1 copy.65
  98.5 17.0 %all-to-all-done.2 = bf16[16,64,512]{2,1,0:T(8,128)(2,1)S(1)} async-done(((bf16[16,64,512]{2,1,0:T(8,128)(2,1)}), bf16[16,64,512]{2,1,0:T(8,128)(2,1)S(1)}, u32[]{:S(2)}, u32[]{:S(2)}) %all-to-all-start.2) | async-done | bytes 1048608 | tf_op jit(solution)/shard_map/all_to_all | solution.py:53
  115.5 0.1 convert_reduce_fusion
  115.8 0.1 fusion.5
  115.9 0.1 fusion.3
  116.1 0.1 fusion.1
  116.3 0.2 fusion.12
  116.5 0.9 convolution_select_fusion
  117.8 0.9 broadcast_in_dim.44
  118.6 3.5 %all-to-all-start.3 = ((bf16[8,72,512]{2,1,0:T(8,128)(2,1)}), bf16[8,72,512]{2,1,0:T(8,128)(2,1)S(1)}, u32[]{:S(2)}, u32[]{:S(2)}) async-start(bf16[8,72,512]{2,1,0:T(8,128)(2,1)} %broadcast_in_dim.44), calls=%async_computation.3 | async-start | bytes 1179648 | tf_op jit(solution)/shard_map/all_to_all | solution.py:53
  122.2 0.6 copy.72
  122.8 10.2 %all-to-all-done.3 = bf16[8,72,512]{2,1,0:T(8,128)(2,1)S(1)} async-done(((bf16[8,72,512]{2,1,0:T(8,128)(2,1)}), bf16[8,72,512]{2,1,0:T(8,128)(2,1)S(1)}, u32[]{:S(2)}, u32[]{:S(2)}) %all-to-all-start.3) | async-done | bytes 589856 | tf_op jit(solution)/shard_map/all_to_all | solution.py:53
  133.3 0.3 fusion.37
  133.7 0.3 fusion.39
  134.0 0.3 fusion.41
  134.4 0.7 broadcast_in_dim.45
  135.1 4.7 %all-to-all-start.4 = ((f32[16,24,128]{2,1,0:T(8,128)}), f32[16,24,128]{2,1,0:T(8,128)S(1)}, u32[]{:S(2)}, u32[]{:S(2)}) async-start(f32[16,24,128]{2,1,0:T(8,128)} %broadcast_in_dim.45), calls=%async_computation.4 | async-start | bytes 393216 | tf_op jit(solution)/shard_map/all_to_all | solution.py:53
  139.9 1.3 collective-permute-start.4
  141.2 0.1 reshape.97
  141.4 0.1 reshape.98
  141.6 0.9 pad_maximum_fusion
  142.5 1.0 fusion.25
  143.8 3.5 %collective-permute-done.4 = f32[32,512]{1,0:T(8,128)S(1)} collective-permute-done((f32[32,512]{1,0:T(8,128)S(1)}, f32[32,512]{1,0:T(8,128)S(1)}, u32[]{:S(2)}, u32[]{:S(2)}) %collective-permute-start.4) | collective-permute-done | bytes 65568 | tf_op jit(solution)/shard_map/ppermute | solution.py:734
  147.3 1.0 maximum_select_fusion
  148.8 0.6 reshape.95
  149.4 0.6 add.110
  150.0 0.6 pad_maximum_fusion.5
  (99 shorter events, 2.5 us)
Async XLA Ops:
  0.6 24.4 %copy-start.9 = (f32[2,1024]{1,0:T(2,128)S(1)}, f32[2,1024]{1,0:T(2,128)}, u32[]{:S(2)}) copy-start(f32[2,1024]{1,0:T(2,128)} %param.15) | copy-start | bytes 24580
  1.4 9.7 %collective-permute-start.3 = (bf16[32,512]{1,0:T(8,128)(2,1)S(1)}, bf16[32,512]{1,0:T(8,128)(2,1)S(1)}, u32[]{:S(2)}, u32[]{:S(2)}) collective-permute-start(bf16[32,512]{1,0:T(8,128)(2,1)S(1)} %slice.209), channel_id=1, source_target_pairs={{0,64},{8,72},{16,80},{24,88},{32,96},{40,104},{48,112},{56,120},{... | collective-permute-start | bytes 98312 | tf_op jit(solution)/shard_map/ppermute | solution.py:477
  9.2 12.8 %collective-permute-start = (bf16[1,24,512]{2,1,0:T(8,128)(2,1)S(1)}, bf16[1,24,512]{2,1,0:T(8,128)(2,1)S(1)}, u32[]{:S(2)}, u32[]{:S(2)}) collective-permute-start(bf16[1,24,512]{2,1,0:T(8,128)(2,1)S(1)} %pad_bitcast_fusion.1), channel_id=1, source_target_pairs={{0,1},{1,0},{2,3},{3,2},{4,5},{5,4},{6,7},{7,6},{8,9},{9,8},{10,11... | collective-permute-start | bytes 73736 | tf_op jit(solution)/shard_map/ppermute | solution.py:516
  11.2 0.6 copy-start.7
  14.3 48.3 %copy-start.5 = (f32[1,6,512]{2,0,1:T(1,128)S(1)}, f32[1,6,512]{2,0,1:T(1,128)}, u32[]{:S(2)}) copy-start(f32[1,6,512]{2,0,1:T(1,128)} %param.10) | copy-start | bytes 36868
  14.3 25.3 %all-to-all-start = ((bf16[16,64,512]{2,1,0:T(8,128)(2,1)}), bf16[16,64,512]{2,1,0:T(8,128)(2,1)S(1)}, u32[]{:S(2)}, u32[]{:S(2)}) async-start(bf16[16,64,512]{2,1,0:T(8,128)(2,1)} %weight_packets.1), calls=%async_computation | async-start | bytes 2097152 | tf_op jit(solution)/shard_map/all_to_all | solution.py:53
  22.1 8.5 %collective-permute-start.1 = (bf16[2,24,512]{2,1,0:T(8,128)(2,1)S(1)}, bf16[2,24,512]{2,1,0:T(8,128)(2,1)S(1)}, u32[]{:S(2)}, u32[]{:S(2)}) collective-permute-start(bf16[2,24,512]{2,1,0:T(8,128)(2,1)S(1)} %pad_maximum_fusion.3), channel_id=1, source_target_pairs={{0,2},{1,3},{2,0},{3,1},{4,6},{5,7},{6,4},{7,5},{8,10},{9,11},{10,... | collective-permute-start | bytes 147464 | tf_op jit(solution)/shard_map/ppermute | solution.py:516
  30.6 8.3 %collective-permute-start.2 = (bf16[4,24,512]{2,1,0:T(8,128)(2,1)S(1)}, bf16[4,24,512]{2,1,0:T(8,128)(2,1)S(1)}, u32[]{:S(2)}, u32[]{:S(2)}) collective-permute-start(bf16[4,24,512]{2,1,0:T(8,128)(2,1)S(1)} %pad_maximum_fusion.2), channel_id=1, source_target_pairs={{0,4},{1,5},{2,6},{3,7},{4,0},{5,1},{6,2},{7,3},{8,12},{9,13},{10,... | collective-permute-start | bytes 294920 | tf_op jit(solution)/shard_map/ppermute | solution.py:516
  39.6 2.3 %copy-start = (bf16[16,64,512]{2,1,0:T(8,128)(2,1)}, bf16[16,64,512]{2,1,0:T(8,128)(2,1)S(1)}, u32[]{:S(2)}) copy-start(bf16[16,64,512]{2,1,0:T(8,128)(2,1)S(1)} %all-to-all-done.weights) | copy-start | bytes 3145732
  59.0 13.7 %all-to-all-start.1 = ((f32[8,32,512]{2,1,0:T(8,128)}), f32[8,32,512]{2,1,0:T(8,128)S(1)}, u32[]{:S(2)}, u32[]{:S(2)}) async-start(f32[8,32,512]{2,1,0:T(8,128)} %get-tuple-element.22), calls=%async_computation.1 | async-start | bytes 1048576 | tf_op jit(solution)/shard_map/all_to_all | solution.py:53
  72.8 0.8 copy-start.1
  73.6 24.8 %copy-start.4 = (bf16[32,512]{1,0:T(8,128)(2,1)S(1)}, bf16[32,512]{1,0:T(8,128)(2,1)}, u32[]{:S(2)}) copy-start(bf16[32,512]{1,0:T(8,128)(2,1)} %mix_last.1) | copy-start | bytes 98308
  73.6 24.9 %copy-start.2 = (bf16[2,64,1536]{2,1,0:T(8,128)(2,1)S(1)}, bf16[2,64,1536]{2,1,0:T(8,128)(2,1)}, u32[]{:S(2)}) copy-start(bf16[2,64,1536]{2,1,0:T(8,128)(2,1)} %conv.1) | copy-start | bytes 1179652
  91.8 30.4 %copy-start.8 = (f32[1,3,512]{2,1,0:T(4,128)S(1)}, f32[1,3,512]{2,1,0:T(4,128)}, u32[]{:S(2)}) copy-start(f32[1,3,512]{2,1,0:T(4,128)} %get-tuple-element.56) | copy-start | bytes 18436
  91.8 41.5 %copy-start.3 = (f32[512,3]{0,1:T(4,128)S(1)}, f32[512,3]{0,1:T(4,128)}, u32[]{:S(2)}) copy-start(f32[512,3]{0,1:T(4,128)} %param.13) | copy-start | bytes 18436
  91.8 23.7 %all-to-all-start.2 = ((bf16[16,64,512]{2,1,0:T(8,128)(2,1)}), bf16[16,64,512]{2,1,0:T(8,128)(2,1)S(1)}, u32[]{:S(2)}, u32[]{:S(2)}) async-start(bf16[16,64,512]{2,1,0:T(8,128)(2,1)} %get-tuple-element.34), calls=%async_computation.2 | async-start | bytes 2097152 | tf_op jit(solution)/shard_map/all_to_all | solution.py:53
  117.7 24.8 %copy-start.6 = (f32[6,512]{1,0:T(8,128)S(1)}, f32[6,512]{1,0:T(8,128)}, u32[]{:S(2)}) copy-start(f32[6,512]{1,0:T(8,128)} %ends.1) | copy-start | bytes 36868
  118.6 14.4 %all-to-all-start.3 = ((bf16[8,72,512]{2,1,0:T(8,128)(2,1)}), bf16[8,72,512]{2,1,0:T(8,128)(2,1)S(1)}, u32[]{:S(2)}, u32[]{:S(2)}) async-start(bf16[8,72,512]{2,1,0:T(8,128)(2,1)} %broadcast_in_dim.44), calls=%async_computation.3 | async-start | bytes 1179648 | tf_op jit(solution)/shard_map/all_to_all | solution.py:53
  135.1 13.3 %all-to-all-start.4 = ((f32[16,24,128]{2,1,0:T(8,128)}), f32[16,24,128]{2,1,0:T(8,128)S(1)}, u32[]{:S(2)}, u32[]{:S(2)}) async-start(f32[16,24,128]{2,1,0:T(8,128)} %broadcast_in_dim.45), calls=%async_computation.4 | async-start | bytes 393216 | tf_op jit(solution)/shard_map/all_to_all | solution.py:53
  139.9 7.4 %collective-permute-start.4 = (f32[32,512]{1,0:T(8,128)S(1)}, f32[32,512]{1,0:T(8,128)S(1)}, u32[]{:S(2)}, u32[]{:S(2)}) collective-permute-start(f32[32,512]{1,0:T(8,128)S(1)} %convert_reduce_fusion.1), channel_id=1, source_target_pairs={{64,0},{72,8},{80,16},{88,24},{96,32},{104,40},{112,48},{120,56},{... | collective-permute-start | bytes 196616 | tf_op jit(solution)/shard_map/ppermute | solution.py:734

commit v6 on v4

--- a/solution.py
+++ b/solution.py
@@ -143,7 +143,9 @@
     e_hi = dot(e0_hi, pick0) + dot(e1_hi, pick1)
     e_lo = dot(e0_lo, pick0) + dot(e1_lo, pick1)
 
-    send = jnp.where(upper, mix_far[...].astype(f32), mix_first[0 : rows // 2, :].astype(f32))
+    send = jnp.where(
+        upper, mix_far[rows // 2 :, :].astype(f32), mix_first[0 : rows // 2, :].astype(f32)
+    )
     send = send.astype(bf16)
     base = 3 * part
     for j in range(n_dp):
@@ -475,7 +477,7 @@
 
     half_rows = rows // 2
     mix_far = lax.ppermute(
-        mix_first[half_rows:], "dp", [(i, i + half_dp) for i in range(half_dp)]
+        mix_first, "dp", [(i, i + half_dp) for i in range(half_dp)]
     )
     sw_hi, sw_lo = split(start_weight)
     ew_last = lax.dynamic_slice(end_weight, (0, last_rows * dp), (n_e, last_rows))
@@ -731,7 +733,9 @@
     grad_mix_last = dot(ew_last, g1_all, 0, 0, highest)
     skip_rows = dot(ew_skip, g0_all, 0, 0, highest)
 
-    other = lax.ppermute(mix_rows, "dp", [(i + half_dp, i) for i in range(half_dp)])
+    other = lax.ppermute(
+        mix_rows.astype(bf16), "dp", [(i + half_dp, i) for i in range(half_dp)]
+    ).astype(f32)
     final = jnp.concatenate(
         [
             start_t.reshape(-1, 128),

time: 151 us -> 151 us (level)
  transfers between devices with their start and end apart: 10 -> 10, of which waited for: 5 -> 6; matrix products, arithmetic and copies ran while one was open for 13% -> 14% of each run, Pallas kernels for 2% -> 2%
where the time goes in v6:
time: 151 us; the launch traced here: 150 us
  waiting for transfers between devices  40.7 us (27%)
  starting transfers between devices  38 us (25%)
  Pallas kernels  37.3 us (25%)
  local copies, waits for them, and re-layouts  15.5 us (10%)
  other arithmetic  9.45 us (6%)
  matrix products  6.9 us (5%)
  between operations  1.81 us (1%)
    all_to_all x5, waiting for transfers between devices, exchange(): return lax.all_to_all(x, axis, 0, 0, tiled=True)  32 us
    all_to_all x5, starting transfers between devices, exchange(): return lax.all_to_all(x, axis, 0, 0, tiled=True)  26 us
    pallas_call x1, Pallas kernels, local(): backward(info, got, fields, light_flux[0], e_up, g_own, du1, dv1, w_taps,...  17.7 us
    pallas_call x1, Pallas kernels, local(): forward(info, fields, a_cat, w_hi, w_lo, weights, bias1, e_pair)  17.1 us
    dot_general x11, matrix products, dot(): lax.dot_general(a, b, (((ca,), (cb,)), ((), ())), precision=precision, pr...  6.9 us
    ppermute x3, waiting for transfers between devices, local(): other = lax.ppermute(fields, 'ctx', [(c, c ^ hop) for c in range(n_ctx)])  5.87 us
    ppermute x1, starting transfers between devices, local(): lax.ppermute(mix_first, 'dp', [(i, i + half_dp) for i in range(half_dp)])  5.48 us
    ppermute x3, starting transfers between devices, local(): other = lax.ppermute(fields, 'ctx', [(c, c ^ hop) for c in range(n_ctx)])  5.21 us
  transfers between devices with their start and end apart: 10, of which 6 were waited for; matrix products, arithmetic and copies ran while one was open for 14% of the time, Pallas kernels for 2%

profile of v6, /device:TPU:1, one launch (start us, length us, event | category | flops | bytes accessed | tf_op | source)
XLA Modules:
  0.0 149.7 jit_solution(2490882599956395273)
XLA Ops:
  0.6 5.5 %collective-permute-start.3 = (bf16[64,512]{1,0:T(8,128)(2,1)}, bf16[64,512]{1,0:T(8,128)(2,1)S(1)}, u32[]{:S(2)}, u32[]{:S(2)}) collective-permute-start(bf16[64,512]{1,0:T(8,128)(2,1)} %mix_first.1), channel_id=1, source_target_pairs={{0,64},{8,72},{16,80},{24,88},{32,96},{40,104},{48,112},{56,120},{... | collective-permute-start | bytes 196616 | tf_op jit(solution)/shard_map/ppermute | solution.py:479
  6.1 0.7 fusion.9
  6.8 0.7 fusion.17
  7.5 0.7 convert_element_type.121
  8.2 0.2 concatenate.65
  8.4 1.4 collective-permute-start
  9.8 0.6 pad_add_fusion.1.info
  10.4 0.6 copy-done.5
  11.0 2.5 %weight_packets.1 = bf16[16,64,512]{2,1,0:T(8,128)(2,1)} custom-call(s32[2]{0:T(128)} %pad_add_fusion.1.info, bf16[2,64,1536]{2,1,0:T(8,128)(2,1)} %conv.1, bf16[64,512]{1,0:T(8,128)(2,1)} %mix_first.1, bf16[64,512]{1,0:T(8,128)(2,1)} %copy-done.5, bf16[32,512]{1,0:T(8,128)(2,1)} %mix_last.1, f32[3,512]{1,0:T(4,128)} %bitcast.66, f32[6,512]{1,0:T(8,128)} %ends.1), custom_call_target="tpu_custom_call" | custom-call | tf_op jit(solution)/shard_map/weight_packets/pallas_call | solution.py:492
  13.6 7.4 %all-to-all-start = ((bf16[16,64,512]{2,1,0:T(8,128)(2,1)}), bf16[16,64,512]{2,1,0:T(8,128)(2,1)S(1)}, u32[]{:S(2)}, u32[]{:S(2)}) async-start(bf16[16,64,512]{2,1,0:T(8,128)(2,1)} %weight_packets.1), calls=%async_computation | async-start | bytes 2097152 | tf_op jit(solution)/shard_map/all_to_all | solution.py:53
  21.0 0.7 fusion.18
  21.9 3.0 %collective-permute-start.1 = (bf16[2,24,512]{2,1,0:T(8,128)(2,1)S(1)}, bf16[2,24,512]{2,1,0:T(8,128)(2,1)S(1)}, u32[]{:S(2)}, u32[]{:S(2)}) collective-permute-start(bf16[2,24,512]{2,1,0:T(8,128)(2,1)S(1)} %pad_maximum_fusion.3), channel_id=1, source_target_pairs={{0,2},{1,3},{2,0},{3,1},{4,6},{5,7},{6,4},{7,5},{8,10},{9,11},{10,... | collective-permute-start | bytes 147464 | tf_op jit(solution)/shard_map/ppermute | solution.py:518
  24.9 0.8 slice_reduce_fusion.5
  25.8 0.7 transpose_reshape.4.bias1
  27.2 0.8 copy.60.w_hi
  27.9 0.8 copy.61.w_lo
  28.7 2.4 %concatenate.69.w_start = bf16[32,512]{1,0:T(8,128)(2,1)} concatenate(bf16[3,512]{1,0:T(4,128)(2,1)S(1)} %bitcast.69, bf16[5,512]{1,0:T(8,128)(2,1)S(1)} %broadcast_in_dim.38, bf16[3,512]{1,0:T(4,128)(2,1)S(1)} %bitcast.70, bf16[5,512]{1,0:T(8,128)(2,1)S(1)} %broadcast_in_dim.38, bf16[3,512]{1,0:T(4,128)(2,1)S(1)} %bitcast.71, bf16[5,512]{1,0:T(8,128)(2,1)S(1)} %broadcast_in_dim.38, ...), dimensions={0} | concatenate | bytes 65536 | tf_op jit(solution)/shard_map/concatenate | solution.py:537
  31.2 0.8 collective-permute-start.2
  32.0 0.6 pad_add_fusion.info
  32.6 5.9 %collective-permute-done.2 = bf16[4,24,512]{2,1,0:T(8,128)(2,1)S(1)} collective-permute-done((bf16[4,24,512]{2,1,0:T(8,128)(2,1)S(1)}, bf16[4,24,512]{2,1,0:T(8,128)(2,1)S(1)}, u32[]{:S(2)}, u32[]{:S(2)}) %collective-permute-start.2) | collective-permute-done | bytes 98336 | tf_op jit(solution)/shard_map/ppermute | solution.py:518
  38.5 0.7 pad_maximum_fusion.1.fields
  39.4 0.1 slice.211
  39.7 0.4 concatenate.71
  40.0 0.9 copy.59
  40.9 0.6 pad_maximum_fusion.7.e_pair
  41.5 17.1 %layers_forward.1 = (bf16[512,4096]{1,0:T(8,128)(2,1)}, bf16[512,4096]{1,0:T(8,128)(2,1)}, bf16[512,4096]{1,0:T(8,128)(2,1)}, bf16[32,4096]{1,0:T(8,128)(2,1)}, ...) custom-call(s32[2]{0:T(128)} %pad_add_fusion.info, ...), custom_call_target="tpu_custom_call" | custom-call | tf_op jit(solution)/shard_map/layers_forward/pallas_call | solution.py:599
  58.7 3.9 %all-to-all-start.1 = ((f32[8,32,512]{2,1,0:T(8,128)}), f32[8,32,512]{2,1,0:T(8,128)S(1)}, u32[]{:S(2)}, u32[]{:S(2)}) async-start(f32[8,32,512]{2,1,0:T(8,128)} %get-tuple-element.22), calls=%async_computation.1 | async-start | bytes 1048576 | tf_op jit(solution)/shard_map/all_to_all | solution.py:53
  62.6 0.6 copy.82
  63.3 1.9 %copy.64 = bf16[384,512]{0,1:T(8,128)(2,1)} copy(bf16[384,512]{1,0:T(8,128)(2,1)} %get-tuple-element.26.w_taps) | data formatting | bytes 786432 | tf_op jit(solution)/shard_map/layers_forward/pallas_call | solution.py:599
  65.2 0.1 copy.63
  65.3 0.6 pad_bitcast_fusion.e_up
  65.9 2.4 %convolution_convert_fusion.w_mix_t = bf16[512,384]{1,0:T(8,128)(2,1)} fusion(bf16[512,512]{1,0:T(8,128)(2,1)} %get-tuple-element.27.mix, bf16[384,512]{1,0:T(8,128)(2,1)} %get-tuple-element.26.w_taps), kind=kOutput, calls=%fused_computation.1 | convolution fusion | flops 201523200 | bytes 1310720 | tf_op jit(solution)/shard_map/dot_general | solution.py:17
  68.3 4.4 %all-to-all-done.1.got = f32[8,32,512]{2,1,0:T(8,128)S(1)} async-done(((f32[8,32,512]{2,1,0:T(8,128)}), f32[8,32,512]{2,1,0:T(8,128)S(1)}, u32[]{:S(2)}, u32[]{:S(2)}) %all-to-all-start.1) | async-done | bytes 524320 | tf_op jit(solution)/shard_map/all_to_all | solution.py:53
  72.8 0.8 copy-done.1
  73.6 17.7 %layers_backward.1 = (f32[1,3,512]{2,1,0:T(4,128)}, bf16[16,64,512]{2,1,0:T(8,128)(2,1)}) custom-call(s32[2]{0:T(128)} %pad_add_fusion.info, f32[8,32,512]{2,1,0:T(8,128)} %copy-done.1, bf16[8,24,512]{2,1,0:T(8,128)(2,1)} %pad_maximum_fusion.1.fields, f32[6,512]{1,0:T(8,128)} %bitcast.68, bf16[128,32]{1,0:T(8,128)(2,1)} %pad_bitcast_fusion.e_up, ...), custom_call_target="tpu_custom_call" | custom-call | tf_op jit(solution)/shard_map/layers_backward/pallas_call | solution.py:651
  91.2 6.5 %all-to-all-start.2 = ((bf16[16,64,512]{2,1,0:T(8,128)(2,1)}), bf16[16,64,512]{2,1,0:T(8,128)(2,1)S(1)}, u32[]{:S(2)}, u32[]{:S(2)}) async-start(bf16[16,64,512]{2,1,0:T(8,128)(2,1)} %get-tuple-element.34), calls=%async_computation.2 | async-start | bytes 2097152 | tf_op jit(solution)/shard_map/all_to_all | solution.py:53
  97.7 0.1 copy.65
  97.9 17.0 %all-to-all-done.2 = bf16[16,64,512]{2,1,0:T(8,128)(2,1)S(1)} async-done(((bf16[16,64,512]{2,1,0:T(8,128)(2,1)}), bf16[16,64,512]{2,1,0:T(8,128)(2,1)S(1)}, u32[]{:S(2)}, u32[]{:S(2)}) %all-to-all-start.2) | async-done | bytes 1048608 | tf_op jit(solution)/shard_map/all_to_all | solution.py:53
  115.0 0.1 convert_reduce_fusion
  115.2 0.1 fusion.5
  115.3 0.1 fusion.3
  115.5 0.1 fusion.1
  115.7 0.2 fusion.12
  115.9 0.9 convolution_select_fusion
  117.2 0.9 broadcast_in_dim.44
  118.0 3.5 %all-to-all-start.3 = ((bf16[8,72,512]{2,1,0:T(8,128)(2,1)}), bf16[8,72,512]{2,1,0:T(8,128)(2,1)S(1)}, u32[]{:S(2)}, u32[]{:S(2)}) async-start(bf16[8,72,512]{2,1,0:T(8,128)(2,1)} %broadcast_in_dim.44), calls=%async_computation.3 | async-start | bytes 1179648 | tf_op jit(solution)/shard_map/all_to_all | solution.py:53
  121.6 0.6 copy.72
  122.2 10.2 %all-to-all-done.3 = bf16[8,72,512]{2,1,0:T(8,128)(2,1)S(1)} async-done(((bf16[8,72,512]{2,1,0:T(8,128)(2,1)}), bf16[8,72,512]{2,1,0:T(8,128)(2,1)S(1)}, u32[]{:S(2)}, u32[]{:S(2)}) %all-to-all-start.3) | async-done | bytes 589856 | tf_op jit(solution)/shard_map/all_to_all | solution.py:53
  132.7 0.3 fusion.37
  133.1 0.3 fusion.39
  133.4 0.3 fusion.41
  133.9 0.7 broadcast_in_dim.45
  134.5 4.7 %all-to-all-start.4 = ((f32[16,24,128]{2,1,0:T(8,128)}), f32[16,24,128]{2,1,0:T(8,128)S(1)}, u32[]{:S(2)}, u32[]{:S(2)}) async-start(f32[16,24,128]{2,1,0:T(8,128)} %broadcast_in_dim.45), calls=%async_computation.4 | async-start | bytes 393216 | tf_op jit(solution)/shard_map/all_to_all | solution.py:53
  139.2 1.3 collective-permute-start.4
  140.6 0.1 reshape.97
  140.7 0.1 reshape.98
  140.9 0.9 pad_maximum_fusion
  141.9 1.0 fusion.25
  143.2 2.8 %collective-permute-done.4 = bf16[32,512]{1,0:T(8,128)(2,1)S(1)} collective-permute-done((bf16[32,512]{1,0:T(8,128)(2,1)S(1)}, bf16[32,512]{1,0:T(8,128)(2,1)S(1)}, u32[]{:S(2)}, u32[]{:S(2)}) %collective-permute-start.4) | collective-permute-done | bytes 32800 | tf_op jit(solution)/shard_map/ppermute | solution.py:736
  146.1 1.0 maximum_select_fusion
  147.1 0.4 all-to-all-done.4
  147.9 0.6 reshape.95
  148.5 0.6 add.110
  149.1 0.6 pad_maximum_fusion.5
  (98 shorter events, 2.6 us)
Async XLA Ops:
  0.6 9.8 %collective-permute-start.3 = (bf16[64,512]{1,0:T(8,128)(2,1)}, bf16[64,512]{1,0:T(8,128)(2,1)S(1)}, u32[]{:S(2)}, u32[]{:S(2)}) collective-permute-start(bf16[64,512]{1,0:T(8,128)(2,1)} %mix_first.1), channel_id=1, source_target_pairs={{0,64},{8,72},{16,80},{24,88},{32,96},{40,104},{48,112},{56,120},{... | collective-permute-start | bytes 196616 | tf_op jit(solution)/shard_map/ppermute | solution.py:479
  8.4 13.4 %collective-permute-start = (bf16[1,24,512]{2,1,0:T(8,128)(2,1)S(1)}, bf16[1,24,512]{2,1,0:T(8,128)(2,1)S(1)}, u32[]{:S(2)}, u32[]{:S(2)}) collective-permute-start(bf16[1,24,512]{2,1,0:T(8,128)(2,1)S(1)} %pad_bitcast_fusion.1), channel_id=1, source_target_pairs={{0,1},{1,0},{2,3},{3,2},{4,5},{5,4},{6,7},{7,6},{8,9},{9,8},{10,11... | collective-permute-start | bytes 73736 | tf_op jit(solution)/shard_map/ppermute | solution.py:518
  10.4 0.6 copy-start.5
  13.6 49.0 %copy-start.6 = (f32[1,6,512]{2,0,1:T(1,128)S(1)}, f32[1,6,512]{2,0,1:T(1,128)}, u32[]{:S(2)}) copy-start(f32[1,6,512]{2,0,1:T(1,128)} %param.10) | copy-start | bytes 36868
  13.6 25.6 %all-to-all-start = ((bf16[16,64,512]{2,1,0:T(8,128)(2,1)}), bf16[16,64,512]{2,1,0:T(8,128)(2,1)S(1)}, u32[]{:S(2)}, u32[]{:S(2)}) async-start(bf16[16,64,512]{2,1,0:T(8,128)(2,1)} %weight_packets.1), calls=%async_computation | async-start | bytes 2097152 | tf_op jit(solution)/shard_map/all_to_all | solution.py:53
  21.9 9.3 %collective-permute-start.1 = (bf16[2,24,512]{2,1,0:T(8,128)(2,1)S(1)}, bf16[2,24,512]{2,1,0:T(8,128)(2,1)S(1)}, u32[]{:S(2)}, u32[]{:S(2)}) collective-permute-start(bf16[2,24,512]{2,1,0:T(8,128)(2,1)S(1)} %pad_maximum_fusion.3), channel_id=1, source_target_pairs={{0,2},{1,3},{2,0},{3,1},{4,6},{5,7},{6,4},{7,5},{8,10},{9,11},{10,... | collective-permute-start | bytes 147464 | tf_op jit(solution)/shard_map/ppermute | solution.py:518
  31.2 7.3 %collective-permute-start.2 = (bf16[4,24,512]{2,1,0:T(8,128)(2,1)S(1)}, bf16[4,24,512]{2,1,0:T(8,128)(2,1)S(1)}, u32[]{:S(2)}, u32[]{:S(2)}) collective-permute-start(bf16[4,24,512]{2,1,0:T(8,128)(2,1)S(1)} %pad_maximum_fusion.2), channel_id=1, source_target_pairs={{0,4},{1,5},{2,6},{3,7},{4,0},{5,1},{6,2},{7,3},{8,12},{9,13},{10,... | collective-permute-start | bytes 294920 | tf_op jit(solution)/shard_map/ppermute | solution.py:518
  39.2 2.3 %copy-start = (bf16[16,64,512]{2,1,0:T(8,128)(2,1)}, bf16[16,64,512]{2,1,0:T(8,128)(2,1)S(1)}, u32[]{:S(2)}) copy-start(bf16[16,64,512]{2,1,0:T(8,128)(2,1)S(1)} %all-to-all-done.weights) | copy-start | bytes 3145732
  58.7 14.1 %all-to-all-start.1 = ((f32[8,32,512]{2,1,0:T(8,128)}), f32[8,32,512]{2,1,0:T(8,128)S(1)}, u32[]{:S(2)}, u32[]{:S(2)}) async-start(f32[8,32,512]{2,1,0:T(8,128)} %get-tuple-element.22), calls=%async_computation.1 | async-start | bytes 1048576 | tf_op jit(solution)/shard_map/all_to_all | solution.py:53
  72.8 0.8 copy-start.1
  73.6 24.2 %copy-start.4 = (bf16[32,512]{1,0:T(8,128)(2,1)S(1)}, bf16[32,512]{1,0:T(8,128)(2,1)}, u32[]{:S(2)}) copy-start(bf16[32,512]{1,0:T(8,128)(2,1)} %mix_last.1) | copy-start | bytes 98308
  73.6 24.3 %copy-start.2 = (bf16[2,64,1536]{2,1,0:T(8,128)(2,1)S(1)}, bf16[2,64,1536]{2,1,0:T(8,128)(2,1)}, u32[]{:S(2)}) copy-start(bf16[2,64,1536]{2,1,0:T(8,128)(2,1)} %conv.1) | copy-start | bytes 1179652
  91.2 30.4 %copy-start.8 = (f32[1,3,512]{2,1,0:T(4,128)S(1)}, f32[1,3,512]{2,1,0:T(4,128)}, u32[]{:S(2)}) copy-start(f32[1,3,512]{2,1,0:T(4,128)} %get-tuple-element.56) | copy-start | bytes 18436
  91.2 41.5 %copy-start.3 = (f32[512,3]{0,1:T(4,128)S(1)}, f32[512,3]{0,1:T(4,128)}, u32[]{:S(2)}) copy-start(f32[512,3]{0,1:T(4,128)} %param.13) | copy-start | bytes 18436
  91.2 23.7 %all-to-all-start.2 = ((bf16[16,64,512]{2,1,0:T(8,128)(2,1)}), bf16[16,64,512]{2,1,0:T(8,128)(2,1)S(1)}, u32[]{:S(2)}, u32[]{:S(2)}) async-start(bf16[16,64,512]{2,1,0:T(8,128)(2,1)} %get-tuple-element.34), calls=%async_computation.2 | async-start | bytes 2097152 | tf_op jit(solution)/shard_map/all_to_all | solution.py:53
  117.2 24.7 %copy-start.7 = (f32[6,512]{1,0:T(8,128)S(1)}, f32[6,512]{1,0:T(8,128)}, u32[]{:S(2)}) copy-start(f32[6,512]{1,0:T(8,128)} %ends.1) | copy-start | bytes 36868
  118.0 14.4 %all-to-all-start.3 = ((bf16[8,72,512]{2,1,0:T(8,128)(2,1)}), bf16[8,72,512]{2,1,0:T(8,128)(2,1)S(1)}, u32[]{:S(2)}, u32[]{:S(2)}) async-start(bf16[8,72,512]{2,1,0:T(8,128)(2,1)} %broadcast_in_dim.44), calls=%async_computation.3 | async-start | bytes 1179648 | tf_op jit(solution)/shard_map/all_to_all | solution.py:53
  134.5 12.9 %all-to-all-start.4 = ((f32[16,24,128]{2,1,0:T(8,128)}), f32[16,24,128]{2,1,0:T(8,128)S(1)}, u32[]{:S(2)}, u32[]{:S(2)}) async-start(f32[16,24,128]{2,1,0:T(8,128)} %broadcast_in_dim.45), calls=%async_computation.4 | async-start | bytes 393216 | tf_op jit(solution)/shard_map/all_to_all | solution.py:53
  139.2 6.8 %collective-permute-start.4 = (bf16[32,512]{1,0:T(8,128)(2,1)S(1)}, bf16[32,512]{1,0:T(8,128)(2,1)S(1)}, u32[]{:S(2)}, u32[]{:S(2)}) collective-permute-start(bf16[32,512]{1,0:T(8,128)(2,1)S(1)} %convert_element_type.144), channel_id=1, source_target_pairs={{64,0},{72,8},{80,16},{88,24},{96,32},{104,40},{112,48},{120,56},{... | collective-permute-start | bytes 98312 | tf_op jit(solution)/shard_map/ppermute | solution.py:736

commit v7 on v6

--- a/solution.py
+++ b/solution.py
@@ -747,6 +747,7 @@
     per0 = final.shape[0]
     per = -(-per0 // 8) * 8
     final = pad_to(final, per, 128)
+    final, _ = lax.optimization_barrier((final, mix_rows.astype(bf16)))
     got = exchange(
         jnp.broadcast_to(final[None], (n_dp, per, 128)).reshape(n_dp * per, 128), "dp"
     ).reshape(n_dp, per, 128)

time: 151 us -> 154 us (1.020)
  starting transfers between devices: 38 us -> 40.1 us
    all_to_all x5, waiting for transfers between devices: 32 us -> 36.2 us  [exchange(): return lax.all_to_all(x, axis, 0, 0, tiled=True)]
    ppermute x1, waiting for transfers between devices: 2.82 us -> 0.01 us  [local(): lax.ppermute(mix_rows.astype(bf16), 'dp', [(i + half_dp, i) for i in rang...]
    all_to_all x5, starting transfers between devices: 26 us -> 28.1 us  [exchange(): return lax.all_to_all(x, axis, 0, 0, tiled=True)]
  transfers between devices with their start and end apart: 10 -> 10, of which waited for: 6 -> 5; matrix products, arithmetic and copies ran while one was open for 14% -> 14% of each run, Pallas kernels for 2% -> 2%
where the time goes in v7:
time: 154 us; the launch traced here: 153 us
  waiting for transfers between devices  42.1 us (27%)
  starting transfers between devices  40.1 us (26%)
  Pallas kernels  37.3 us (24%)
  local copies, waits for them, and re-layouts  15.5 us (10%)
  other arithmetic  9.45 us (6%)
  matrix products  6.9 us (4%)
  between operations  1.82 us (1%)
    all_to_all x5, waiting for transfers between devices, exchange(): return lax.all_to_all(x, axis, 0, 0, tiled=True)  36.2 us
    all_to_all x5, starting transfers between devices, exchange(): return lax.all_to_all(x, axis, 0, 0, tiled=True)  28.1 us
    pallas_call x1, Pallas kernels, local(): backward(info, got, fields, light_flux[0], e_up, g_own, du1, dv1, w_taps,...  17.7 us
    pallas_call x1, Pallas kernels, local(): forward(info, fields, a_cat, w_hi, w_lo, weights, bias1, e_pair)  17.1 us
    dot_general x11, matrix products, dot(): lax.dot_general(a, b, (((ca,), (cb,)), ((), ())), precision=precision, pr...  6.9 us
    ppermute x3, waiting for transfers between devices, local(): other = lax.ppermute(fields, 'ctx', [(c, c ^ hop) for c in range(n_ctx)])  5.87 us
    ppermute x1, starting transfers between devices, local(): lax.ppermute(mix_first, 'dp', [(i, i + half_dp) for i in range(half_dp)])  5.48 us
    ppermute x3, starting transfers between devices, local(): other = lax.ppermute(fields, 'ctx', [(c, c ^ hop) for c in range(n_ctx)])  5.21 us
  transfers between devices with their start and end apart: 10, of which 5 were waited for; matrix products, arithmetic and copies ran while one was open for 14% of the time, Pallas kernels for 2%

profile of v7, /device:TPU:1, one launch (start us, length us, event | category | flops | bytes accessed | tf_op | source)
XLA Modules:
  0.0 153.2 jit_solution(9257041032149690553)
XLA Ops:
  0.6 5.5 %collective-permute-start.3 = (bf16[64,512]{1,0:T(8,128)(2,1)}, bf16[64,512]{1,0:T(8,128)(2,1)S(1)}, u32[]{:S(2)}, u32[]{:S(2)}) collective-permute-start(bf16[64,512]{1,0:T(8,128)(2,1)} %mix_first.1), channel_id=1, source_target_pairs={{0,64},{8,72},{16,80},{24,88},{32,96},{40,104},{48,112},{56,120},{... | collective-permute-start | bytes 196616 | tf_op jit(solution)/shard_map/ppermute | solution.py:479
  6.1 0.7 fusion.9
  6.8 0.7 fusion.17
  7.5 0.7 convert_element_type.122
  8.2 0.2 concatenate.65
  8.4 1.4 collective-permute-start
  9.8 0.6 pad_add_fusion.1.info
  10.4 0.6 copy-done.5
  11.0 2.5 %weight_packets.1 = bf16[16,64,512]{2,1,0:T(8,128)(2,1)} custom-call(s32[2]{0:T(128)} %pad_add_fusion.1.info, bf16[2,64,1536]{2,1,0:T(8,128)(2,1)} %conv.1, bf16[64,512]{1,0:T(8,128)(2,1)} %mix_first.1, bf16[64,512]{1,0:T(8,128)(2,1)} %copy-done.5, bf16[32,512]{1,0:T(8,128)(2,1)} %mix_last.1, f32[3,512]{1,0:T(4,128)} %bitcast.66, f32[6,512]{1,0:T(8,128)} %ends.1), custom_call_target="tpu_custom_call" | custom-call | tf_op jit(solution)/shard_map/weight_packets/pallas_call | solution.py:492
  13.6 7.4 %all-to-all-start = ((bf16[16,64,512]{2,1,0:T(8,128)(2,1)}), bf16[16,64,512]{2,1,0:T(8,128)(2,1)S(1)}, u32[]{:S(2)}, u32[]{:S(2)}) async-start(bf16[16,64,512]{2,1,0:T(8,128)(2,1)} %weight_packets.1), calls=%async_computation | async-start | bytes 2097152 | tf_op jit(solution)/shard_map/all_to_all | solution.py:53
  21.0 0.7 fusion.18
  21.9 3.0 %collective-permute-start.1 = (bf16[2,24,512]{2,1,0:T(8,128)(2,1)S(1)}, bf16[2,24,512]{2,1,0:T(8,128)(2,1)S(1)}, u32[]{:S(2)}, u32[]{:S(2)}) collective-permute-start(bf16[2,24,512]{2,1,0:T(8,128)(2,1)S(1)} %pad_maximum_fusion.3), channel_id=1, source_target_pairs={{0,2},{1,3},{2,0},{3,1},{4,6},{5,7},{6,4},{7,5},{8,10},{9,11},{10,... | collective-permute-start | bytes 147464 | tf_op jit(solution)/shard_map/ppermute | solution.py:518
  24.9 0.8 slice_reduce_fusion.5
  25.8 0.7 transpose_reshape.4.bias1
  27.2 0.8 copy.60.w_hi
  27.9 0.8 copy.61.w_lo
  28.7 2.4 %concatenate.69.w_start = bf16[32,512]{1,0:T(8,128)(2,1)} concatenate(bf16[3,512]{1,0:T(4,128)(2,1)S(1)} %bitcast.69, bf16[5,512]{1,0:T(8,128)(2,1)S(1)} %broadcast_in_dim.38, bf16[3,512]{1,0:T(4,128)(2,1)S(1)} %bitcast.70, bf16[5,512]{1,0:T(8,128)(2,1)S(1)} %broadcast_in_dim.38, bf16[3,512]{1,0:T(4,128)(2,1)S(1)} %bitcast.71, bf16[5,512]{1,0:T(8,128)(2,1)S(1)} %broadcast_in_dim.38, ...), dimensions={0} | concatenate | bytes 65536 | tf_op jit(solution)/shard_map/concatenate | solution.py:537
  31.2 0.8 collective-permute-start.2
  32.0 0.6 pad_add_fusion.info
  32.6 5.9 %collective-permute-done.2 = bf16[4,24,512]{2,1,0:T(8,128)(2,1)S(1)} collective-permute-done((bf16[4,24,512]{2,1,0:T(8,128)(2,1)S(1)}, bf16[4,24,512]{2,1,0:T(8,128)(2,1)S(1)}, u32[]{:S(2)}, u32[]{:S(2)}) %collective-permute-start.2) | collective-permute-done | bytes 98336 | tf_op jit(solution)/shard_map/ppermute | solution.py:518
  38.5 0.7 pad_maximum_fusion.1.fields
  39.4 0.1 slice.211
  39.6 0.1 slice.213
  39.7 0.4 concatenate.71
  40.0 0.9 copy.59
  40.9 0.6 pad_maximum_fusion.7.e_pair
  41.5 17.1 %layers_forward.1 = (bf16[512,4096]{1,0:T(8,128)(2,1)}, bf16[512,4096]{1,0:T(8,128)(2,1)}, bf16[512,4096]{1,0:T(8,128)(2,1)}, bf16[32,4096]{1,0:T(8,128)(2,1)}, ...) custom-call(s32[2]{0:T(128)} %pad_add_fusion.info, ...), custom_call_target="tpu_custom_call" | custom-call | tf_op jit(solution)/shard_map/layers_forward/pallas_call | solution.py:599
  58.7 3.9 %all-to-all-start.1 = ((f32[8,32,512]{2,1,0:T(8,128)}), f32[8,32,512]{2,1,0:T(8,128)S(1)}, u32[]{:S(2)}, u32[]{:S(2)}) async-start(f32[8,32,512]{2,1,0:T(8,128)} %get-tuple-element.23), calls=%async_computation.1 | async-start | bytes 1048576 | tf_op jit(solution)/shard_map/all_to_all | solution.py:53
  62.6 0.6 copy.82
  63.3 1.9 %copy.64 = bf16[384,512]{0,1:T(8,128)(2,1)} copy(bf16[384,512]{1,0:T(8,128)(2,1)} %get-tuple-element.27.w_taps) | data formatting | bytes 786432 | tf_op jit(solution)/shard_map/layers_forward/pallas_call | solution.py:599
  65.2 0.1 copy.63
  65.3 0.6 pad_bitcast_fusion.e_up
  65.9 2.4 %convolution_convert_fusion.w_mix_t = bf16[512,384]{1,0:T(8,128)(2,1)} fusion(bf16[512,512]{1,0:T(8,128)(2,1)} %get-tuple-element.28.mix, bf16[384,512]{1,0:T(8,128)(2,1)} %get-tuple-element.27.w_taps), kind=kOutput, calls=%fused_computation.1 | convolution fusion | flops 201523200 | bytes 1310720 | tf_op jit(solution)/shard_map/dot_general | solution.py:17
  68.3 4.4 %all-to-all-done.1.got = f32[8,32,512]{2,1,0:T(8,128)S(1)} async-done(((f32[8,32,512]{2,1,0:T(8,128)}), f32[8,32,512]{2,1,0:T(8,128)S(1)}, u32[]{:S(2)}, u32[]{:S(2)}) %all-to-all-start.1) | async-done | bytes 524320 | tf_op jit(solution)/shard_map/all_to_all | solution.py:53
  72.8 0.8 copy-done.1
  73.6 17.7 %layers_backward.1 = (f32[1,3,512]{2,1,0:T(4,128)}, bf16[16,64,512]{2,1,0:T(8,128)(2,1)}) custom-call(s32[2]{0:T(128)} %pad_add_fusion.info, f32[8,32,512]{2,1,0:T(8,128)} %copy-done.1, bf16[8,24,512]{2,1,0:T(8,128)(2,1)} %pad_maximum_fusion.1.fields, f32[6,512]{1,0:T(8,128)} %bitcast.68, bf16[128,32]{1,0:T(8,128)(2,1)} %pad_bitcast_fusion.e_up, ...), custom_call_target="tpu_custom_call" | custom-call | tf_op jit(solution)/shard_map/layers_backward/pallas_call | solution.py:651
  91.2 6.5 %all-to-all-start.2 = ((bf16[16,64,512]{2,1,0:T(8,128)(2,1)}), bf16[16,64,512]{2,1,0:T(8,128)(2,1)S(1)}, u32[]{:S(2)}, u32[]{:S(2)}) async-start(bf16[16,64,512]{2,1,0:T(8,128)(2,1)} %get-tuple-element.35), calls=%async_computation.2 | async-start | bytes 2097152 | tf_op jit(solution)/shard_map/all_to_all | solution.py:53
  97.7 0.1 copy.65
  97.9 17.0 %all-to-all-done.2 = bf16[16,64,512]{2,1,0:T(8,128)(2,1)S(1)} async-done(((bf16[16,64,512]{2,1,0:T(8,128)(2,1)}), bf16[16,64,512]{2,1,0:T(8,128)(2,1)S(1)}, u32[]{:S(2)}, u32[]{:S(2)}) %all-to-all-start.2) | async-done | bytes 1048608 | tf_op jit(solution)/shard_map/all_to_all | solution.py:53
  115.0 0.1 convert_reduce_fusion
  115.2 0.1 fusion.5
  115.3 0.1 fusion.3
  115.5 0.1 fusion.1
  115.7 0.2 fusion.12
  115.9 0.9 convolution_select_fusion
  117.2 0.9 broadcast_in_dim.44
  118.0 3.5 %all-to-all-start.3 = ((bf16[8,72,512]{2,1,0:T(8,128)(2,1)}), bf16[8,72,512]{2,1,0:T(8,128)(2,1)S(1)}, u32[]{:S(2)}, u32[]{:S(2)}) async-start(bf16[8,72,512]{2,1,0:T(8,128)(2,1)} %broadcast_in_dim.44), calls=%async_computation.3 | async-start | bytes 1179648 | tf_op jit(solution)/shard_map/all_to_all | solution.py:53
  121.6 0.6 copy.72
  122.2 10.2 %all-to-all-done.3 = bf16[8,72,512]{2,1,0:T(8,128)(2,1)S(1)} async-done(((bf16[8,72,512]{2,1,0:T(8,128)(2,1)}), bf16[8,72,512]{2,1,0:T(8,128)(2,1)S(1)}, u32[]{:S(2)}, u32[]{:S(2)}) %all-to-all-start.3) | async-done | bytes 589856 | tf_op jit(solution)/shard_map/all_to_all | solution.py:53
  132.7 0.3 fusion.37
  133.1 0.3 fusion.39
  133.4 0.3 fusion.41
  133.9 1.3 collective-permute-start.4
  135.2 0.7 broadcast_in_dim.45
  135.9 6.8 %all-to-all-start.4 = ((f32[16,24,128]{2,1,0:T(8,128)}), f32[16,24,128]{2,1,0:T(8,128)S(1)}, u32[]{:S(2)}, u32[]{:S(2)}) async-start(f32[16,24,128]{2,1,0:T(8,128)} %broadcast_in_dim.45), calls=%async_computation.4 | async-start | bytes 393216 | tf_op jit(solution)/shard_map/all_to_all | solution.py:53
  142.7 0.1 reshape.97
  142.8 0.1 reshape.98
  143.1 0.9 pad_maximum_fusion
  144.0 1.0 fusion.25
  145.4 1.1 maximum_select_fusion
  146.4 4.5 %all-to-all-done.4 = f32[16,24,128]{2,1,0:T(8,128)S(1)} async-done(((f32[16,24,128]{2,1,0:T(8,128)}), f32[16,24,128]{2,1,0:T(8,128)S(1)}, u32[]{:S(2)}, u32[]{:S(2)}) %all-to-all-start.4) | async-done | bytes 196640 | tf_op jit(solution)/shard_map/all_to_all | solution.py:53
  151.4 0.6 reshape.95
  152.0 0.6 add.110
  152.6 0.6 pad_maximum_fusion.5
  (98 shorter events, 2.5 us)
Async XLA Ops:
  0.6 9.8 %collective-permute-start.3 = (bf16[64,512]{1,0:T(8,128)(2,1)}, bf16[64,512]{1,0:T(8,128)(2,1)S(1)}, u32[]{:S(2)}, u32[]{:S(2)}) collective-permute-start(bf16[64,512]{1,0:T(8,128)(2,1)} %mix_first.1), channel_id=1, source_target_pairs={{0,64},{8,72},{16,80},{24,88},{32,96},{40,104},{48,112},{56,120},{... | collective-permute-start | bytes 196616 | tf_op jit(solution)/shard_map/ppermute | solution.py:479
  8.4 13.4 %collective-permute-start = (bf16[1,24,512]{2,1,0:T(8,128)(2,1)S(1)}, bf16[1,24,512]{2,1,0:T(8,128)(2,1)S(1)}, u32[]{:S(2)}, u32[]{:S(2)}) collective-permute-start(bf16[1,24,512]{2,1,0:T(8,128)(2,1)S(1)} %pad_bitcast_fusion.1), channel_id=1, source_target_pairs={{0,1},{1,0},{2,3},{3,2},{4,5},{5,4},{6,7},{7,6},{8,9},{9,8},{10,11... | collective-permute-start | bytes 73736 | tf_op jit(solution)/shard_map/ppermute | solution.py:518
  10.4 0.6 copy-start.5
  13.6 49.0 %copy-start.6 = (f32[1,6,512]{2,0,1:T(1,128)S(1)}, f32[1,6,512]{2,0,1:T(1,128)}, u32[]{:S(2)}) copy-start(f32[1,6,512]{2,0,1:T(1,128)} %param.10) | copy-start | bytes 36868
  13.6 25.6 %all-to-all-start = ((bf16[16,64,512]{2,1,0:T(8,128)(2,1)}), bf16[16,64,512]{2,1,0:T(8,128)(2,1)S(1)}, u32[]{:S(2)}, u32[]{:S(2)}) async-start(bf16[16,64,512]{2,1,0:T(8,128)(2,1)} %weight_packets.1), calls=%async_computation | async-start | bytes 2097152 | tf_op jit(solution)/shard_map/all_to_all | solution.py:53
  21.9 9.3 %collective-permute-start.1 = (bf16[2,24,512]{2,1,0:T(8,128)(2,1)S(1)}, bf16[2,24,512]{2,1,0:T(8,128)(2,1)S(1)}, u32[]{:S(2)}, u32[]{:S(2)}) collective-permute-start(bf16[2,24,512]{2,1,0:T(8,128)(2,1)S(1)} %pad_maximum_fusion.3), channel_id=1, source_target_pairs={{0,2},{1,3},{2,0},{3,1},{4,6},{5,7},{6,4},{7,5},{8,10},{9,11},{10,... | collective-permute-start | bytes 147464 | tf_op jit(solution)/shard_map/ppermute | solution.py:518
  31.2 7.3 %collective-permute-start.2 = (bf16[4,24,512]{2,1,0:T(8,128)(2,1)S(1)}, bf16[4,24,512]{2,1,0:T(8,128)(2,1)S(1)}, u32[]{:S(2)}, u32[]{:S(2)}) collective-permute-start(bf16[4,24,512]{2,1,0:T(8,128)(2,1)S(1)} %pad_maximum_fusion.2), channel_id=1, source_target_pairs={{0,4},{1,5},{2,6},{3,7},{4,0},{5,1},{6,2},{7,3},{8,12},{9,13},{10,... | collective-permute-start | bytes 294920 | tf_op jit(solution)/shard_map/ppermute | solution.py:518
  39.2 2.3 %copy-start = (bf16[16,64,512]{2,1,0:T(8,128)(2,1)}, bf16[16,64,512]{2,1,0:T(8,128)(2,1)S(1)}, u32[]{:S(2)}) copy-start(bf16[16,64,512]{2,1,0:T(8,128)(2,1)S(1)} %all-to-all-done.weights) | copy-start | bytes 3145732
  58.7 14.1 %all-to-all-start.1 = ((f32[8,32,512]{2,1,0:T(8,128)}), f32[8,32,512]{2,1,0:T(8,128)S(1)}, u32[]{:S(2)}, u32[]{:S(2)}) async-start(f32[8,32,512]{2,1,0:T(8,128)} %get-tuple-element.23), calls=%async_computation.1 | async-start | bytes 1048576 | tf_op jit(solution)/shard_map/all_to_all | solution.py:53
  72.8 0.8 copy-start.1
  73.6 24.2 %copy-start.4 = (bf16[32,512]{1,0:T(8,128)(2,1)S(1)}, bf16[32,512]{1,0:T(8,128)(2,1)}, u32[]{:S(2)}) copy-start(bf16[32,512]{1,0:T(8,128)(2,1)} %mix_last.1) | copy-start | bytes 98308
  73.6 24.3 %copy-start.2 = (bf16[2,64,1536]{2,1,0:T(8,128)(2,1)S(1)}, bf16[2,64,1536]{2,1,0:T(8,128)(2,1)}, u32[]{:S(2)}) copy-start(bf16[2,64,1536]{2,1,0:T(8,128)(2,1)} %conv.1) | copy-start | bytes 1179652
  91.2 30.4 %copy-start.8 = (f32[1,3,512]{2,1,0:T(4,128)S(1)}, f32[1,3,512]{2,1,0:T(4,128)}, u32[]{:S(2)}) copy-start(f32[1,3,512]{2,1,0:T(4,128)} %get-tuple-element.58) | copy-start | bytes 18436
  91.2 41.5 %copy-start.3 = (f32[512,3]{0,1:T(4,128)S(1)}, f32[512,3]{0,1:T(4,128)}, u32[]{:S(2)}) copy-start(f32[512,3]{0,1:T(4,128)} %param.13) | copy-start | bytes 18436
  91.2 23.7 %all-to-all-start.2 = ((bf16[16,64,512]{2,1,0:T(8,128)(2,1)}), bf16[16,64,512]{2,1,0:T(8,128)(2,1)S(1)}, u32[]{:S(2)}, u32[]{:S(2)}) async-start(bf16[16,64,512]{2,1,0:T(8,128)(2,1)} %get-tuple-element.35), calls=%async_computation.2 | async-start | bytes 2097152 | tf_op jit(solution)/shard_map/all_to_all | solution.py:53
  117.2 26.8 %copy-start.7 = (f32[6,512]{1,0:T(8,128)S(1)}, f32[6,512]{1,0:T(8,128)}, u32[]{:S(2)}) copy-start(f32[6,512]{1,0:T(8,128)} %ends.1) | copy-start | bytes 36868
  118.0 14.4 %all-to-all-start.3 = ((bf16[8,72,512]{2,1,0:T(8,128)(2,1)}), bf16[8,72,512]{2,1,0:T(8,128)(2,1)S(1)}, u32[]{:S(2)}, u32[]{:S(2)}) async-start(bf16[8,72,512]{2,1,0:T(8,128)(2,1)} %broadcast_in_dim.44), calls=%async_computation.3 | async-start | bytes 1179648 | tf_op jit(solution)/shard_map/all_to_all | solution.py:53
  133.9 11.5 %collective-permute-start.4 = (bf16[32,512]{1,0:T(8,128)(2,1)S(1)}, bf16[32,512]{1,0:T(8,128)(2,1)S(1)}, u32[]{:S(2)}, u32[]{:S(2)}) collective-permute-start(bf16[32,512]{1,0:T(8,128)(2,1)S(1)} %convert_element_type.141), channel_id=1, source_target_pairs={{64,0},{72,8},{80,16},{88,24},{96,32},{104,40},{112,48},{120,56},{... | collective-permute-start | bytes 98312 | tf_op jit(solution)/shard_map/ppermute | solution.py:736
  135.9 15.1 %all-to-all-start.4 = ((f32[16,24,128]{2,1,0:T(8,128)}), f32[16,24,128]{2,1,0:T(8,128)S(1)}, u32[]{:S(2)}, u32[]{:S(2)}) async-start(f32[16,24,128]{2,1,0:T(8,128)} %broadcast_in_dim.45), calls=%async_computation.4 | async-start | bytes 393216 | tf_op jit(solution)/shard_map/all_to_all | solution.py:53
